TPU v7x, 256 devices: a whole 4x4x8 slice. The times are simulated.
256 devices in a mesh: shot: 128 (over z, x, y_hi, core), ap: 2 (over y_lo).
Axes of the slice: x: 4, y: 4 (y_hi: 2, y_lo: 2; y = y_hi * 2 + y_lo), z: 8, core: 2. Of those that a mesh axis runs over, the one named last changes fastest.
Arguments:
- wave_prev: float32 [128, 32, 64, 256], P('shot', None, None, 'ap'), may hold values from -6 to 6
- wave_now: float32 [128, 32, 64, 256], P('shot', None, None, 'ap'), may hold values from -6 to 6
- adjoint_late: float32 [128, 32, 64, 256], P('shot', None, None, 'ap'), may hold values from -6 to 6
- adjoint_next: float32 [128, 32, 64, 256], P('shot', None, None, 'ap'), may hold values from -6 to 6
- bulk: float32 [128, 32, 64, 256], P('shot', None, None, 'ap'), may hold values from 0.5 to 2
- buoyancy: float32 [128, 32, 64, 256], P('shot', None, None, 'ap'), may hold values from 0.5 to 2
- traces: bfloat16 [32768, 2048], P(('shot', 'ap')), may hold values from -6 to 6
- group_filter: bfloat16 [128, 2, 2048], P('shot'), may hold values from -0.125 to 0.125
- trace_group: int32 [32768, 1], P(('shot', 'ap')), may hold values from 0 to 127; in each aligned block of 128 rows (0 to 127, 128 to 255, ...) at most 2 rows name the same one
- trace_receiver: int32 [32768], P(('shot', 'ap')), may hold values from 0 to 255
- receiver_cell: int32 [128, 512], P('shot', 'ap'), may hold values from 0 to 262143
- tile_owner: int32 [32768, 1], P('shot'), may hold values from 0 to 127; in each aligned block of 256 rows (0 to 255, 256 to 511, ...) at most 4 rows name the same one
- tile_slot: int32 [32768], P('shot'), may hold values from 0 to 7
Outputs:
- model_grad: float32 [1024, 8, 256], P('shot', None, 'ap')
- wave_last: float32 [128, 32, 64, 256], P('shot', None, None, 'ap')
- adjoint_last: float32 [128, 32, 64, 256], P('shot', None, None, 'ap')
Inputs may be any that keep to these rules, and one draw needn't show every extreme that they name: `trace_group`: in each device's aligned block of 128 rows no shot group is named by more than 2 rows, and some block reaches 2; every group is named somewhere. `tile_owner`: in each group's aligned block of 256 rows no owner is named by more than 4 rows, and some block reaches 4; every owner is named somewhere.
All inputs are finite; a program needn't handle non-finite values.
Results may differ from a plain program's by a relative error of at most 0.002.
Values may be sent and summed in bfloat16 or wider, within the bound.
No kernel may reach another device: no remote copies, remote signals or barrier semaphores. Data moves between devices by JAX's collectives and lax.ppermute only.
A program may use at most 128 MiB of HBM per device.

v0:
```python
import jax
import jax.numpy as jnp
from jax import lax
from jax.sharding import PartitionSpec as P

TILE_CELLS_SECOND = 8
NREC = 256
MT_DEV = 8


STEP = 0.08


def padded(cells, sides, width):
    for axis, dim in sides:
        count = lax.axis_size(axis)
        ends = count - 1
        head = lax.slice_in_dim(cells, 0, width, axis=dim)
        tail = lax.slice_in_dim(cells, cells.shape[dim] - width, cells.shape[dim], axis=dim)
        cells = jnp.concatenate(
            [
                lax.ppermute(tail, axis, [(i, (i + 1) % count) for i in range(ends)]),
                cells,
                lax.ppermute(head, axis, [((i + 1) % count, i) for i in range(ends)]),
            ],
            axis=dim,
        )
    return cells


def neighbours(padded_field):
    return (
        padded_field[2:, 1:-1, 1:-1],
        padded_field[:-2, 1:-1, 1:-1],
        padded_field[1:-1, 2:, 1:-1],
        padded_field[1:-1, :-2, 1:-1],
        padded_field[1:-1, 1:-1, 2:],
        padded_field[1:-1, 1:-1, :-2],
    )


def operate(wavefield, buoyancy, buoy_pad, rimmed):
    rimmed = padded(wavefield, (("ap", 2),), 1)
    wavefield_padded = jnp.pad(rimmed, ((1, 1), (1, 1), (0, 0)))
    total = jnp.zeros_like(wavefield)
    for wave_side, buoy_side in zip(neighbours(wavefield_padded), neighbours(buoy_pad)):
        total = total + 0.5 * (buoyancy + buoy_side) * (wave_side - wavefield)
    return total


def ranking(keys, width):
    onehot = (keys[:, None] == jnp.arange(width, dtype=jnp.int32)[None, :]).astype(jnp.int32)
    return jnp.sum(jnp.cumsum(onehot, axis=0) * onehot, axis=1) - 1


def local(
    wave_prev,
    wave_now,
    adjoint_late,
    adjoint_next,
    bulk,
    buoyancy,
    traces,
    group_filter,
    trace_group,
    trace_receiver,
    receiver_cell,
    tile_owner,
    tile_slot,
):
    shot_count = lax.axis_size("shot")
    trace_count = traces.shape[0]
    samples = traces.shape[1]
    capacity = max(2, 2 * trace_count // shot_count)
    row_groups = trace_group[:, 0]
    position = row_groups * capacity + ranking(row_groups, shot_count)
    send_ids = jnp.zeros((shot_count * capacity,), jnp.int32).at[position].set(trace_receiver)
    send_ids = send_ids.reshape(shot_count, capacity)
    own_filter = group_filter[0]
    send_rows = jnp.zeros((shot_count * capacity, samples), traces.dtype).at[position].set(traces)
    send_rows = send_rows.reshape(shot_count, capacity, samples)
    values_out = jnp.einsum(
        "sct,kt->sck",
        lax.all_to_all(send_rows, "shot", split_axis=0, concat_axis=0, tiled=True),
        own_filter,
        preferred_element_type=jnp.float32,
    )
    got_ids = lax.all_to_all(send_ids, "shot", split_axis=0, concat_axis=0, tiled=True)
    observed = (
        jnp.zeros((NREC, 2), jnp.float32).at[got_ids.reshape(-1)].add(values_out.reshape(-1, 2))
    )
    wave_old = wave_prev[0]
    wave_cur = wave_now[0]
    adjoint_old = adjoint_late[0]
    adjoint_current = adjoint_next[0]
    bulk_here = bulk[0]
    buoy_here = buoyancy[0]
    cells_x, cells_y, depth = wave_cur.shape
    adjoint_scaled = bulk_here * adjoint_current
    buoy_rimmed = padded(buoy_here.astype(jnp.bfloat16), (("ap", 2),), 1).astype(buoy_here.dtype)
    buoy_pad = jnp.pad(buoy_rimmed, ((1, 1), (1, 1), (0, 0)))
    receiver_cells = receiver_cell[0]
    lap_now = operate(wave_cur, buoy_here, buoy_pad, None)
    wave_mid = 2.0 * wave_cur - wave_old + STEP * bulk_here * lap_now
    lap_mid = operate(wave_mid, buoy_here, buoy_pad, None)
    wave_end = 2.0 * wave_mid - wave_cur + STEP * bulk_here * lap_mid
    resid_mid = wave_mid.reshape(-1)[receiver_cells] - observed[:, 0]
    resid_end = wave_end.reshape(-1)[receiver_cells] - observed[:, 1]

    def inject(residual):
        base = jnp.zeros((cells_x * cells_y * depth,), jnp.float32)
        return base.at[receiver_cells].add(residual).reshape(cells_x, cells_y, depth)

    adjoint_mid = (
        2.0 * adjoint_current
        - adjoint_old
        + STEP * operate(adjoint_scaled, buoy_here, buoy_pad, None)
        + inject(resid_end)
    )
    adjoint_end = (
        2.0 * adjoint_mid
        - adjoint_current
        + STEP * operate(bulk_here * adjoint_mid, buoy_here, buoy_pad, None)
        + inject(resid_mid)
    )
    image = STEP * (adjoint_mid * lap_mid + adjoint_end * lap_now)
    tile_total = cells_x * (cells_y // TILE_CELLS_SECOND)
    tile_rows = image.reshape(tile_total, TILE_CELLS_SECOND, depth)
    owners = tile_owner[:, 0]
    model_ids = owners * MT_DEV + tile_slot
    flat_tiles = tile_rows.reshape(tile_total, TILE_CELLS_SECOND * depth)
    wanted = jnp.arange(lax.axis_size("shot") * MT_DEV, dtype=jnp.int32)
    selector = (wanted[:, None] == model_ids[None, :]).astype(jnp.float32)
    summed = jnp.dot(
        selector, flat_tiles, precision=lax.Precision.HIGHEST, preferred_element_type=jnp.float32
    )
    model_grad = lax.psum_scatter(
        summed.reshape(lax.axis_size("shot") * MT_DEV, TILE_CELLS_SECOND, depth),
        "shot",
        scatter_dimension=0,
        tiled=True,
    )
    return (model_grad, wave_end[None], adjoint_end[None])


def solution(mesh):
    placed = (
        P("shot", None, None, "ap"),
        P("shot", None, None, "ap"),
        P("shot", None, None, "ap"),
        P("shot", None, None, "ap"),
        P("shot", None, None, "ap"),
        P("shot", None, None, "ap"),
        P(("shot", "ap"), None),
        P("shot", None, None),
        P(("shot", "ap"), None),
        P(("shot", "ap")),
        P("shot", "ap"),
        P("shot", None),
        P("shot"),
    )
    return jax.shard_map(
        local,
        mesh=mesh,
        in_specs=placed,
        out_specs=(P("shot", None, "ap"), P("shot", None, None, "ap"), P("shot", None, None, "ap")),
        check_vma=False,
    )
```

profile of v0, /device:TPU:1, one launch (start us, length us, event | category | flops | bytes accessed | tf_op | source)
XLA Modules:
  0.0 837.2 jit_solution(56531573709612252)
XLA Ops:
  7.2 3.0 fusion.103
  10.6 4.2 collective-permute-start.4
  14.8 1.7 copy.39
  19.9 4.8 collective-permute-start
  28.3 16.1 %all-to-all-start = ((s32[128,1,2]{2,1,0:T(1,128)}), s32[128,1,2]{2,1,0:T(1,128)S(1)}, u32[]{:S(2)}, u32[]{:S(2)}) async-start(s32[128,1,2]{2,1,0:T(1,128)} %bitcast.14), calls=%async_computation | async-start | bytes 131072 | tf_op jit(solution)/shard_map/all_to_all | solution.py:88
  46.4 4.5 collective-permute-start.2
  50.9 2.2 scatter_custom_fusion.1
  54.6 1.6 copy.33
  56.2 15.1 %all-to-all-start.1 = ((bf16[128,2,2048]{2,1,0:T(2,128)(2,1)}), bf16[128,2,2048]{2,1,0:T(2,128)(2,1)}, u32[]{:S(2)}, u32[]{:S(2)}) async-start(bf16[128,2,2048]{2,1,0:T(2,128)(2,1)} %reshape.103), calls=%async_computation.1 | async-start | bytes 2097152 | tf_op jit(solution)/shard_map/all_to_all | solution.py:84
  72.8 1.6 collective-permute-start.3
  74.5 3.1 maximum_convert_fusion
  79.5 2.4 select_maximum_fusion.4
  82.2 6.9 fusion.71
  89.1 1.7 fusion.102
  90.8 1.6 copy.44
  92.4 4.0 collective-permute-start.6
  96.4 1.6 copy.45
  102.0 4.0 select_maximum_fusion.6
  108.9 2.7 select_maximum_fusion.2
  112.0 5.5 multiply_add_fusion
  117.4 3.5 gather_fusion
  122.8 1.9 scatter_custom_fusion.2
  124.9 2.9 scatter_custom_fusion.3
  127.9 9.6 %bitcast_multiply_fusion = (f32[32,64,128]{2,1,0:T(8,128)S(1)}, f32[32,64,128]{2,1,0:T(8,128)}) fusion(f32[1,32,64,128]{3,2,1,0:T(8,128)} %param.17, f32[32,64,128]{2,1,0:T(8,128)} %bitcast.83, f32[32,64,128]{2,1,0:T(8,128)} %get-tuple-element.30, f32[32,64,128]{2,1,0:T(8,128)S(1)} %bitcast_multiply_fusion.2, f32[32,64,1]{2,1,0:T(8,128)} %copy.34, ...), kind=kLoop, calls=%fused_computation.123 | loop fusion | flops 6553600 | bytes 17842176 | tf_op jit(solution)/shard_map/mul | solution.py:123
  138.9 1.6 copy.52
  140.5 4.0 collective-permute-start.8
  146.1 1.7 gather_fusion.1
  147.9 2.9 scatter_custom_fusion.4
  153.6 2.7 select_maximum_fusion
  156.7 5.4 add_multiply_fusion
  163.9 3.5 fusion.73
  167.4 661.5 %reduce-scatter.2.cloned.1.call-done = f32[8,8,128]{2,0,1:T(8,128)} async-done(((f32[1024,8,128]{2,0,1:T(8,128)}), f32[8,8,128]{2,0,1:T(8,128)}) %reduce-scatter.2.cloned.1.call-update) | async-done | bytes 32784 | tf_op jit(solution)/shard_map/reduce_scatter | solution.py:137
  (113 shorter events, 33.1 us)
Async XLA Ops:
  7.2 115.2 %copy-start = (bf16[1,2,2048]{2,1,0:T(2,128)(2,1)S(1)}, bf16[1,2,2048]{2,1,0:T(2,128)(2,1)}, u32[]{:S(2)}) copy-start(bf16[1,2,2048]{2,1,0:T(2,128)(2,1)} %param.20) | copy-start | bytes 24580
  7.2 10.7 %copy-start.23 = (f32[1,32,64,128]{3,2,1,0:T(8,128)S(1)}, f32[1,32,64,128]{3,2,1,0:T(8,128)}, u32[]{:S(2)}) copy-start(f32[1,32,64,128]{3,2,1,0:T(8,128)} %param.18) | copy-start | bytes 3145732
  10.6 15.4 %copy-start.24 = (s32[128,1]{0,1:T(1,128)S(1)}, s32[128,1]{0,1:T(1,128)}, u32[]{:S(2)}) copy-start(s32[128,1]{0,1:T(1,128)} %param.21) | copy-start | bytes 1540
  10.6 67.0 %collective-permute-start.4 = (f32[32,64,1]{1,0,2:T(8,128)S(1)}, f32[32,64,1]{1,0,2:T(8,128)S(1)}, u32[]{:S(2)}, u32[]{:S(2)}) collective-permute-start(f32[32,64,1]{1,0,2:T(8,128)S(1)} %copy.38), channel_id=1, source_target_pairs={{0,1},{2,3},{4,5},{6,7},{8,9},{10,11},{12,13},{14,15},{16,17},{18,... | collective-permute-start | bytes 24584 | tf_op jit(solution)/shard_map/ppermute | solution.py:22
  14.8 29.7 %copy-start.3 = (f32[1,32,64,128]{3,2,1,0:T(8,128)S(1)}, f32[1,32,64,128]{3,2,1,0:T(8,128)}, u32[]{:S(2)}) copy-start(f32[1,32,64,128]{3,2,1,0:T(8,128)} %param.17) | copy-start | bytes 3145732
  14.8 29.7 %copy-start.16 = (f32[1,32,64,128]{3,2,1,0:T(8,128)S(1)}, f32[1,32,64,128]{3,2,1,0:T(8,128)}, u32[]{:S(2)}) copy-start(f32[1,32,64,128]{3,2,1,0:T(8,128)} %param.16) | copy-start | bytes 3145732
  16.5 61.5 %collective-permute-start.5 = (f32[32,64,1]{1,0,2:T(8,128)S(1)}, f32[32,64,1]{1,0,2:T(8,128)S(1)}, u32[]{:S(2)}, u32[]{:S(2)}) collective-permute-start(f32[32,64,1]{1,0,2:T(8,128)S(1)} %copy.39), channel_id=1, source_target_pairs={{1,0},{3,2},{5,4},{7,6},{9,8},{11,10},{13,12},{15,14},{17,16},{19,... | collective-permute-start | bytes 24584 | tf_op jit(solution)/shard_map/ppermute | solution.py:24
  19.9 52.9 %collective-permute-start = (bf16[32,64,1]{2,1,0:T(8,128)(2,1)}, bf16[32,64,1]{2,1,0:T(8,128)(2,1)}, u32[]{:S(2)}, u32[]{:S(2)}) collective-permute-start(bf16[32,64,1]{2,1,0:T(8,128)(2,1)} %get-tuple-element.39), channel_id=1, source_target_pairs={{0,1},{2,3},{4,5},{6,7},{8,9},{10,11},{12,13},{14,15},{16,17},{18,... | collective-permute-start | bytes 12296 | tf_op jit(solution)/shard_map/ppermute | solution.py:22
  24.7 49.8 %collective-permute-start.1 = (bf16[32,64,1]{2,1,0:T(8,128)(2,1)}, bf16[32,64,1]{2,1,0:T(8,128)(2,1)}, u32[]{:S(2)}, u32[]{:S(2)}) collective-permute-start(bf16[32,64,1]{2,1,0:T(8,128)(2,1)} %get-tuple-element.40), channel_id=1, source_target_pairs={{1,0},{3,2},{5,4},{7,6},{9,8},{11,10},{13,12},{15,14},{17,16},{19,... | collective-permute-start | bytes 12296 | tf_op jit(solution)/shard_map/ppermute | solution.py:24
  28.3 27.9 %all-to-all-start = ((s32[128,1,2]{2,1,0:T(1,128)}), s32[128,1,2]{2,1,0:T(1,128)S(1)}, u32[]{:S(2)}, u32[]{:S(2)}) async-start(s32[128,1,2]{2,1,0:T(1,128)} %bitcast.14), calls=%async_computation | async-start | bytes 131072 | tf_op jit(solution)/shard_map/all_to_all | solution.py:88
  44.7 6.2 copy-start.26
  46.4 52.9 %collective-permute-start.2 = (f32[32,64,1]{1,0,2:T(8,128)S(1)}, f32[32,64,1]{1,0,2:T(8,128)S(1)}, u32[]{:S(2)}, u32[]{:S(2)}) collective-permute-start(f32[32,64,1]{1,0,2:T(8,128)S(1)} %copy.32), channel_id=1, source_target_pairs={{0,1},{2,3},{4,5},{6,7},{8,9},{10,11},{12,13},{14,15},{16,17},{18,... | collective-permute-start | bytes 24584 | tf_op jit(solution)/shard_map/ppermute | solution.py:22
  53.1 21.4 %copy-start.21 = (bf16[32,64,128]{2,1,0:T(8,128)(2,1)S(1)}, bf16[32,64,128]{2,1,0:T(8,128)(2,1)}, u32[]{:S(2)}) copy-start(bf16[32,64,128]{2,1,0:T(8,128)(2,1)} %copy-done.20) | copy-start | bytes 1572868
  56.2 64.7 %all-to-all-start.1 = ((bf16[128,2,2048]{2,1,0:T(2,128)(2,1)}), bf16[128,2,2048]{2,1,0:T(2,128)(2,1)}, u32[]{:S(2)}, u32[]{:S(2)}) async-start(bf16[128,2,2048]{2,1,0:T(2,128)(2,1)} %reshape.103), calls=%async_computation.1 | async-start | bytes 2097152 | tf_op jit(solution)/shard_map/all_to_all | solution.py:84
  71.3 757.7 %reduce-scatter.2.cloned.1.call-start = ((), (), s32[]{:S(2)}) async-start(), calls=%async_computation.3 | async-start | bytes 4227072 | tf_op jit(solution)/shard_map/reduce_scatter | solution.py:137
  72.8 6.6 copy-start.1
  72.8 27.8 %collective-permute-start.3 = (f32[32,64,1]{1,0,2:T(8,128)S(1)}, f32[32,64,1]{1,0,2:T(8,128)S(1)}, u32[]{:S(2)}, u32[]{:S(2)}) collective-permute-start(f32[32,64,1]{1,0,2:T(8,128)S(1)} %copy.33), channel_id=1, source_target_pairs={{1,0},{3,2},{5,4},{7,6},{9,8},{11,10},{13,12},{15,14},{17,16},{19,... | collective-permute-start | bytes 24584 | tf_op jit(solution)/shard_map/ppermute | solution.py:24
  79.5 2.8 copy-start.22
  92.4 13.7 %collective-permute-start.6 = (f32[32,64,1]{1,0,2:T(8,128)S(1)}, f32[32,64,1]{1,0,2:T(8,128)S(1)}, u32[]{:S(2)}, u32[]{:S(2)}) collective-permute-start(f32[32,64,1]{1,0,2:T(8,128)S(1)} %copy.44), channel_id=1, source_target_pairs={{0,1},{2,3},{4,5},{6,7},{8,9},{10,11},{12,13},{14,15},{16,17},{18,... | collective-permute-start | bytes 24584 | tf_op jit(solution)/shard_map/ppermute | solution.py:22
  97.9 9.5 %collective-permute-start.7 = (f32[32,64,1]{1,0,2:T(8,128)S(1)}, f32[32,64,1]{1,0,2:T(8,128)S(1)}, u32[]{:S(2)}, u32[]{:S(2)}) collective-permute-start(f32[32,64,1]{1,0,2:T(8,128)S(1)} %copy.45), channel_id=1, source_target_pairs={{1,0},{3,2},{5,4},{7,6},{9,8},{11,10},{13,12},{15,14},{17,16},{19,... | collective-permute-start | bytes 24584 | tf_op jit(solution)/shard_map/ppermute | solution.py:24
  108.9 2.8 copy-start.10
  108.9 3.1 copy-start.12
  137.5 8.6 %copy-start.27 = (s32[256,1]{0,1:T(1,128)S(1)}, s32[256,1]{0,1:T(1,128)}, u32[]{:S(2)}) copy-start(s32[256,1]{0,1:T(1,128)} %param.24) | copy-start | bytes 3076
  137.5 8.6 %copy-start.25 = (s32[256]{0:T(256)S(1)}, s32[256]{0:T(256)}, u32[]{:S(2)}) copy-start(s32[256]{0:T(256)} %param.25) | copy-start | bytes 3076
  140.5 10.3 %collective-permute-start.8 = (f32[32,64,1]{1,0,2:T(8,128)S(1)}, f32[32,64,1]{1,0,2:T(8,128)S(1)}, u32[]{:S(2)}, u32[]{:S(2)}) collective-permute-start(f32[32,64,1]{1,0,2:T(8,128)S(1)} %copy.52), channel_id=1, source_target_pairs={{0,1},{2,3},{4,5},{6,7},{8,9},{10,11},{12,13},{14,15},{16,17},{18,... | collective-permute-start | bytes 24584 | tf_op jit(solution)/shard_map/ppermute | solution.py:22
  144.8 7.4 collective-permute-start.9
  150.8 5.5 copy-start.17
  152.2 4.1 copy-start.15
  153.6 2.8 copy-start.9
  153.6 2.8 copy-start.11
  153.6 2.8 copy-start.13
  153.6 3.1 copy-start.14
  (9 other events, 20.5 us)
Sparse Core Ops, SparseCore 0:
  167.5 661.3 reduce-scatter.1
where the time goes:
time: 844 us; the launch traced here: 837 us
  waiting for transfers between devices  662 us (78%)
  starting transfers between devices  59.4 us (7%)
  other arithmetic  51.5 us (6%)
  local copies, waits for them, and re-layouts  46.1 us (5%)
  between operations  14.6 us (2%)
    reduce_scatter x1, waiting for transfers between devices, local(): lax.psum_scatter(summed.reshape(lax.axis_size('shot') * MT_DEV, TILE_CELL...  662 us
    ppermute x5, starting transfers between devices, padded(): lax.ppermute(tail, axis, [(i, (i + 1) % count) for i in range(ends)])  21.3 us
  transfers between devices with their start and end apart: 13, of which 1 were waited for; matrix products, arithmetic and copies ran while one was open for 7% of the time, Pallas kernels for 0%

commit v1 on v0

--- a/solution.py
+++ b/solution.py
@@ -127,19 +127,30 @@
     tile_total = cells_x * (cells_y // TILE_CELLS_SECOND)
     tile_rows = image.reshape(tile_total, TILE_CELLS_SECOND, depth)
     owners = tile_owner[:, 0]
-    model_ids = owners * MT_DEV + tile_slot
+    tile_cap = 4
+    slot_at = owners * tile_cap + ranking(owners, shot_count)
     flat_tiles = tile_rows.reshape(tile_total, TILE_CELLS_SECOND * depth)
-    wanted = jnp.arange(lax.axis_size("shot") * MT_DEV, dtype=jnp.int32)
-    selector = (wanted[:, None] == model_ids[None, :]).astype(jnp.float32)
+    send_slots = jnp.full((shot_count * tile_cap,), MT_DEV, jnp.int32).at[slot_at].set(tile_slot)
+    got_slots = lax.all_to_all(
+        send_slots.reshape(shot_count, tile_cap), "shot", split_axis=0, concat_axis=0, tiled=True
+    ).reshape(-1)
+    send_tiles = jnp.zeros((shot_count * tile_cap, TILE_CELLS_SECOND * depth), jnp.float32)
+    send_tiles = send_tiles.at[slot_at].set(flat_tiles)
+    got_tiles = lax.all_to_all(
+        send_tiles.reshape(shot_count, tile_cap * TILE_CELLS_SECOND, depth),
+        "shot",
+        split_axis=0,
+        concat_axis=0,
+        tiled=True,
+    ).reshape(shot_count * tile_cap, TILE_CELLS_SECOND * depth)
+    selector = (jnp.arange(MT_DEV, dtype=jnp.int32)[:, None] == got_slots[None, :])
     summed = jnp.dot(
-        selector, flat_tiles, precision=lax.Precision.HIGHEST, preferred_element_type=jnp.float32
+        selector.astype(jnp.float32),
+        got_tiles,
+        precision=lax.Precision.HIGHEST,
+        preferred_element_type=jnp.float32,
     )
-    model_grad = lax.psum_scatter(
-        summed.reshape(lax.axis_size("shot") * MT_DEV, TILE_CELLS_SECOND, depth),
-        "shot",
-        scatter_dimension=0,
-        tiled=True,
-    )
+    model_grad = summed.reshape(MT_DEV, TILE_CELLS_SECOND, depth)
     return (model_grad, wave_end[None], adjoint_end[None])
 
 

time: 844 us -> 250 us (0.30)
  waiting for transfers between devices: 662 us -> 50.8 us
  starting transfers between devices: 59.4 us -> 88.1 us
  between operations: 14.6 us -> 1.28 us
    reduce_scatter x1 -> x0, waiting for transfers between devices: 662 us -> none  [local(): lax.psum_scatter(summed.reshape(lax.axis_size('shot') * MT_DEV, TILE_CELL...]
    all_to_all x0 -> x2, waiting for transfers between devices: none -> 50.8 us  [the longest x1 50.8 us: local(): lax.all_to_all(send_tiles.reshape(shot_count, tile_cap * TILE_CELLS_SECON...]
    all_to_all x0 -> x2, starting transfers between devices: none -> 28.6 us  [the longest x1 14.8 us: local(): lax.all_to_all(send_slots.reshape(shot_count, tile_cap), 'shot', split_ax...]
  transfers between devices with their start and end apart: 13 -> 14, of which waited for: 1 -> 1; matrix products, arithmetic and copies ran while one was open for 7% -> 31% of each run, Pallas kernels for 0% -> 0%
where the time goes in v1:
time: 250 us; the launch traced here: 248 us
  starting transfers between devices  88.1 us (35%)
  other arithmetic  54.3 us (22%)
  local copies, waits for them, and re-layouts  51.6 us (21%)
  waiting for transfers between devices  50.8 us (20%)
    all_to_all x1, waiting for transfers between devices, local(): lax.all_to_all(send_tiles.reshape(shot_count, tile_cap * TILE_CELLS_SECON...  50.8 us
    ppermute x5, starting transfers between devices, padded(): lax.ppermute(tail, axis, [(i, (i + 1) % count) for i in range(ends)])  21.4 us
    all_to_all x1, starting transfers between devices, local(): lax.all_to_all(send_ids, 'shot', split_axis=0, concat_axis=0, tiled=True)  16.1 us
    all_to_all x1, starting transfers between devices, local(): lax.all_to_all(send_rows, 'shot', split_axis=0, concat_axis=0, tiled=True)  15.1 us
    all_to_all x1, starting transfers between devices, local(): lax.all_to_all(send_slots.reshape(shot_count, tile_cap), 'shot', split_ax...  14.8 us
    all_to_all x1, starting transfers between devices, local(): lax.all_to_all(send_tiles.reshape(shot_count, tile_cap * TILE_CELLS_SECON...  13.7 us
    concatenate x4, other arithmetic, padded(): jnp.concatenate([lax.ppermute(tail, axis, [(i, (i + 1) % count) for i in...  11.8 us
    slice x8, local copies, waits for them, and re-layouts, padded(): head = lax.slice_in_dim(cells, 0, width, axis=dim)  10.4 us
  transfers between devices with their start and end apart: 14, of which 1 were waited for; matrix products, arithmetic and copies ran while one was open for 31% of the time, Pallas kernels for 0%

profile of v1, /device:TPU:1, one launch (start us, length us, event | category | flops | bytes accessed | tf_op | source)
XLA Modules:
  0.0 247.6 jit_solution(13802079907984741728)
XLA Ops:
  0.6 2.1 fusion.111
  3.1 4.2 %collective-permute-start.4 = (f32[32,64,1]{1,0,2:T(8,128)S(1)}, f32[32,64,1]{1,0,2:T(8,128)S(1)}, u32[]{:S(2)}, u32[]{:S(2)}) collective-permute-start(f32[32,64,1]{1,0,2:T(8,128)S(1)} %copy.47), channel_id=1, source_target_pairs={{0,1},{2,3},{4,5},{6,7},{8,9},{10,11},{12,13},{14,15},{16,17},{18,... | collective-permute-start | bytes 24584 | tf_op jit(solution)/shard_map/ppermute | solution.py:22
  11.6 4.8 %collective-permute-start = (bf16[32,64,1]{2,1,0:T(8,128)(2,1)}, bf16[32,64,1]{2,1,0:T(8,128)(2,1)}, u32[]{:S(2)}, u32[]{:S(2)}) collective-permute-start(bf16[32,64,1]{2,1,0:T(8,128)(2,1)} %get-tuple-element.39), channel_id=1, source_target_pairs={{0,1},{2,3},{4,5},{6,7},{8,9},{10,11},{12,13},{14,15},{16,17},{18,... | collective-permute-start | bytes 12296 | tf_op jit(solution)/shard_map/ppermute | solution.py:22
  20.0 16.1 %all-to-all-start.1 = ((s32[128,1,2]{2,1,0:T(1,128)}), s32[128,1,2]{2,1,0:T(1,128)S(1)}, u32[]{:S(2)}, u32[]{:S(2)}) async-start(s32[128,1,2]{2,1,0:T(1,128)} %bitcast.21), calls=%async_computation.1 | async-start | bytes 131072 | tf_op jit(solution)/shard_map/all_to_all | solution.py:88
  38.0 4.5 %collective-permute-start.2 = (f32[32,64,1]{1,0,2:T(8,128)S(1)}, f32[32,64,1]{1,0,2:T(8,128)S(1)}, u32[]{:S(2)}, u32[]{:S(2)}) collective-permute-start(f32[32,64,1]{1,0,2:T(8,128)S(1)} %copy.41), channel_id=1, source_target_pairs={{0,1},{2,3},{4,5},{6,7},{8,9},{10,11},{12,13},{14,15},{16,17},{18,... | collective-permute-start | bytes 24584 | tf_op jit(solution)/shard_map/ppermute | solution.py:22
  43.1 2.2 scatter_custom_fusion.2
  46.9 1.6 copy.42
  48.5 15.1 %all-to-all-start.2 = ((bf16[128,2,2048]{2,1,0:T(2,128)(2,1)}), bf16[128,2,2048]{2,1,0:T(2,128)(2,1)}, u32[]{:S(2)}, u32[]{:S(2)}) async-start(bf16[128,2,2048]{2,1,0:T(2,128)(2,1)} %reshape.138), calls=%async_computation.2 | async-start | bytes 2097152 | tf_op jit(solution)/shard_map/all_to_all | solution.py:84
  65.1 1.6 collective-permute-start.3
  66.7 3.1 %maximum_convert_fusion = f32[32,64,130]{2,1,0:T(8,128)} fusion(bf16[32,64,1]{2,1,0:T(8,128)(2,1)} %collective-permute-done.1, bf16[32,64,128]{2,1,0:T(8,128)(2,1)S(1)} %copy-done.20, bf16[32,64,1]{2,1,0:T(8,128)(2,1)} %collective-permute-done), kind=kLoop, calls=%fused_computation.122 | loop fusion | flops 1597440 | bytes 1597440 | tf_op jit(solution)/shard_map/convert_element_type | solution.py:100
  71.7 2.4 select_maximum_fusion.4
  74.5 6.9 %fusion.71 = (f32[32,64,128]{2,1,0:T(8,128)S(1)}, f32[32,64,128]{2,1,0:T(8,128)}, f32[32,64,128]{2,1,0:T(8,128)}, f32[32,64,128]{2,1,0:T(8,128)}, f32[32,64,128]...) fusion(f32[1,32,64,128]{3,2,1,0:T(8,128)S(1)} %copy-done.21, ...), kind=kLoop, calls=%fused_computation.124 | loop fusion | flops 9437184 | bytes 23076864 | tf_op jit(solution)/shard_map/add | solution.py:104
  81.4 1.7 fusion.110
  84.6 4.0 %collective-permute-start.6 = (f32[32,64,1]{1,0,2:T(8,128)S(1)}, f32[32,64,1]{1,0,2:T(8,128)S(1)}, u32[]{:S(2)}, u32[]{:S(2)}) collective-permute-start(f32[32,64,1]{1,0,2:T(8,128)S(1)} %copy.53), channel_id=1, source_target_pairs={{0,1},{2,3},{4,5},{6,7},{8,9},{10,11},{12,13},{14,15},{16,17},{18,... | collective-permute-start | bytes 24584 | tf_op jit(solution)/shard_map/ppermute | solution.py:22
  88.6 1.6 copy.54
  94.3 4.0 %select_maximum_fusion.6 = f32[34,66,130]{2,1,0:T(8,128)} fusion(f32[32,64,1]{2,1,0:T(8,128)} %copy.44, f32[32,64,128]{2,1,0:T(8,128)S(1)} %bitcast_multiply_fusion.2, f32[32,64,1]{2,1,0:T(8,128)} %copy.43), kind=kLoop, calls=%fused_computation.23 | loop fusion | flops 4375800 | bytes 2231840 | tf_op jit(solution)/shard_map/concatenate | solution.py:20
  101.2 2.7 %select_maximum_fusion.2 = f32[34,66,130]{2,1,0:T(8,128)S(1)} fusion(f32[32,64,1]{2,1,0:T(8,128)} %copy.56, f32[32,64,128]{2,1,0:T(8,128)S(1)} %get-tuple-element.23, f32[32,64,1]{2,1,0:T(8,128)} %copy.55), kind=kLoop, calls=%fused_computation.19 | loop fusion | flops 4375800 | bytes 2231840 | tf_op jit(solution)/shard_map/concatenate | solution.py:20
  104.3 5.5 %multiply_add_fusion = (f32[32,64,128]{2,1,0:T(8,128)}, f32[32,64,128]{2,1,0:T(8,128)}) fusion(f32[32,64,128]{2,1,0:T(8,128)} %get-tuple-element.24, f32[1,32,64,128]{3,2,1,0:T(8,128)} %param.13, f32[1,32,64,128]{3,2,1,0:T(8,128)S(1)} %copy-done.6, f32[1,32,64,128]{3,2,1,0:T(8,128)S(1)} %copy-done.2, f32[32,64,128]{2,1,0:T(8,128)} %get-tuple-element.30, ...), kind=kLoop, calls=%fused_computation.133 | loop fusion | flops 7340032 | bytes 17842176 | tf_op jit(solution)/shard_map/add | solution.py:106
  109.7 3.5 %gather_fusion = f32[256]{0:T(256)S(1)} fusion(f32[262144]{0:T(1024)} %bitcast.96, s32[1024]{0:T(1024)S(1)} %pad_clamp_fusion), kind=kCustom, calls=%fused_computation | custom fusion | bytes 3072 | tf_op jit(solution)/shard_map/gather | solution.py:108
  115.1 1.8 scatter_custom_fusion.3
  117.2 2.9 %scatter_custom_fusion.4 = f32[262144]{0:T(1024)} fusion(s32[256]{0:T(256)S(1)} %bitcast.107, f32[256]{0:T(256)S(1)} %sub.127, f32[]{:T(128)} %constant.18.clone.1), kind=kCustom, calls=%fused_computation.140 | custom fusion | flops 256 | bytes 1048580 | tf_op jit(solution)/shard_map/scatter-add | solution.py:112
  120.1 9.6 %bitcast_multiply_fusion = (f32[32,64,128]{2,1,0:T(8,128)S(1)}, f32[32,64,128]{2,1,0:T(8,128)}) fusion(f32[1,32,64,128]{3,2,1,0:T(8,128)} %param.17, f32[32,64,128]{2,1,0:T(8,128)} %bitcast.99, f32[32,64,128]{2,1,0:T(8,128)} %get-tuple-element.30, f32[32,64,128]{2,1,0:T(8,128)S(1)} %bitcast_multiply_fusion.2, f32[32,64,1]{2,1,0:T(8,128)} %copy.43, ...), kind=kLoop, calls=%fused_computation.125 | loop fusion | flops 6553600 | bytes 17842176 | tf_op jit(solution)/shard_map/mul | solution.py:123
  132.7 4.0 %collective-permute-start.8 = (f32[32,64,1]{1,0,2:T(8,128)S(1)}, f32[32,64,1]{1,0,2:T(8,128)S(1)}, u32[]{:S(2)}, u32[]{:S(2)}) collective-permute-start(f32[32,64,1]{1,0,2:T(8,128)S(1)} %copy.61), channel_id=1, source_target_pairs={{0,1},{2,3},{4,5},{6,7},{8,9},{10,11},{12,13},{14,15},{16,17},{18,... | collective-permute-start | bytes 24584 | tf_op jit(solution)/shard_map/ppermute | solution.py:22
  140.7 14.8 %all-to-all-start = ((s32[128,1,4]{2,1,0:T(1,128)}), s32[128,1,4]{2,1,0:T(1,128)S(1)}, u32[]{:S(2)}, u32[]{:S(2)}) async-start(s32[128,1,4]{2,1,0:T(1,128)} %bitcast.7), calls=%async_computation | async-start | bytes 131072 | tf_op jit(solution)/shard_map/all_to_all | solution.py:134
  155.6 1.7 gather_fusion.1
  157.3 3.0 %scatter_custom_fusion.5 = f32[262144]{0:T(1024)} fusion(s32[256]{0:T(256)S(1)} %bitcast.108, f32[256]{0:T(256)S(1)} %sub.135, f32[]{:T(128)} %constant.18.clone.1), kind=kCustom, calls=%fused_computation.138 | custom fusion | flops 256 | bytes 1048580 | tf_op jit(solution)/shard_map/scatter-add | solution.py:112
  163.1 2.7 %select_maximum_fusion = f32[34,66,130]{2,1,0:T(8,128)S(1)} fusion(f32[32,64,1]{2,1,0:T(8,128)} %copy.64, f32[32,64,128]{2,1,0:T(8,128)S(1)} %get-tuple-element.19, f32[32,64,1]{2,1,0:T(8,128)} %copy.63), kind=kLoop, calls=%fused_computation.17 | loop fusion | flops 4375800 | bytes 2231840 | tf_op jit(solution)/shard_map/concatenate | solution.py:20
  166.2 5.7 %add_multiply_fusion = (f32[32,64,128]{2,1,0:T(8,128)}, f32[32,64,128]{2,1,0:T(8,128)}) fusion(f32[32,64,128]{2,1,0:T(8,128)} %get-tuple-element.24, f32[32,64,128]{2,1,0:T(8,128)} %get-tuple-element.20, f32[32,64,128]{2,1,0:T(8,128)} %get-tuple-element.22, f32[32,64,128]{2,1,0:T(8,128)} %bitcast.98, f32[32,64,128]{2,1,0:T(8,128)} %get-tuple-element.30, ...), kind=kLoop, calls=%fused_computation.132 | loop fusion | flops 7340032 | bytes 18890752 | tf_op jit(solution)/shard_map/mul | solution.py:126
  173.3 2.2 scatter_custom_fusion.6
  177.0 13.7 %all-to-all-start.3 = ((f32[128,32,128]{2,1,0:T(8,128)}), f32[128,32,128]{2,1,0:T(8,128)S(1)}, u32[]{:S(2)}, u32[]{:S(2)}) async-start(f32[128,32,128]{2,1,0:T(8,128)} %reshape.142), calls=%async_computation.3 | async-start | bytes 4194304 | tf_op jit(solution)/shard_map/all_to_all | solution.py:139
  191.7 50.8 %all-to-all-done.3 = f32[128,32,128]{2,1,0:T(8,128)S(1)} async-done(((f32[128,32,128]{2,1,0:T(8,128)}), f32[128,32,128]{2,1,0:T(8,128)S(1)}, u32[]{:S(2)}, u32[]{:S(2)}) %all-to-all-start.3) | async-done | bytes 2097184 | tf_op jit(solution)/shard_map/all_to_all | solution.py:139
  244.0 1.9 copy.67
  (124 shorter events, 43.9 us)
Async XLA Ops:
  0.6 114.0 %copy-start = (bf16[1,2,2048]{2,1,0:T(2,128)(2,1)S(1)}, bf16[1,2,2048]{2,1,0:T(2,128)(2,1)}, u32[]{:S(2)}) copy-start(bf16[1,2,2048]{2,1,0:T(2,128)(2,1)} %param.20) | copy-start | bytes 24580
  3.1 14.6 %copy-start.23 = (s32[128,1]{0,1:T(1,128)S(1)}, s32[128,1]{0,1:T(1,128)}, u32[]{:S(2)}) copy-start(s32[128,1]{0,1:T(1,128)} %param.21) | copy-start | bytes 1540
  3.1 66.8 %collective-permute-start.4 = (f32[32,64,1]{1,0,2:T(8,128)S(1)}, f32[32,64,1]{1,0,2:T(8,128)S(1)}, u32[]{:S(2)}, u32[]{:S(2)}) collective-permute-start(f32[32,64,1]{1,0,2:T(8,128)S(1)} %copy.47), channel_id=1, source_target_pairs={{0,1},{2,3},{4,5},{6,7},{8,9},{10,11},{12,13},{14,15},{16,17},{18,... | collective-permute-start | bytes 24584 | tf_op jit(solution)/shard_map/ppermute | solution.py:22
  7.3 28.9 %copy-start.4 = (f32[1,32,64,128]{3,2,1,0:T(8,128)S(1)}, f32[1,32,64,128]{3,2,1,0:T(8,128)}, u32[]{:S(2)}) copy-start(f32[1,32,64,128]{3,2,1,0:T(8,128)} %param.17) | copy-start | bytes 3145732
  7.3 28.9 %copy-start.16 = (f32[1,32,64,128]{3,2,1,0:T(8,128)S(1)}, f32[1,32,64,128]{3,2,1,0:T(8,128)}, u32[]{:S(2)}) copy-start(f32[1,32,64,128]{3,2,1,0:T(8,128)} %param.16) | copy-start | bytes 3145732
  7.7 62.6 %collective-permute-start.5 = (f32[32,64,1]{1,0,2:T(8,128)S(1)}, f32[32,64,1]{1,0,2:T(8,128)S(1)}, u32[]{:S(2)}, u32[]{:S(2)}) collective-permute-start(f32[32,64,1]{1,0,2:T(8,128)S(1)} %copy.48), channel_id=1, source_target_pairs={{1,0},{3,2},{5,4},{7,6},{9,8},{11,10},{13,12},{15,14},{17,16},{19,... | collective-permute-start | bytes 24584 | tf_op jit(solution)/shard_map/ppermute | solution.py:24
  10.4 9.6 %copy-start.19 = (bf16[32,64,128]{2,1,0:T(8,128)(2,1)}, bf16[32,64,128]{2,1,0:T(8,128)(2,1)S(1)}, u32[]{:S(2)}) copy-start(bf16[32,64,128]{2,1,0:T(8,128)(2,1)S(1)} %bitcast_convert_fusion) | copy-start | bytes 1572868
  11.6 53.5 %collective-permute-start = (bf16[32,64,1]{2,1,0:T(8,128)(2,1)}, bf16[32,64,1]{2,1,0:T(8,128)(2,1)}, u32[]{:S(2)}, u32[]{:S(2)}) collective-permute-start(bf16[32,64,1]{2,1,0:T(8,128)(2,1)} %get-tuple-element.39), channel_id=1, source_target_pairs={{0,1},{2,3},{4,5},{6,7},{8,9},{10,11},{12,13},{14,15},{16,17},{18,... | collective-permute-start | bytes 12296 | tf_op jit(solution)/shard_map/ppermute | solution.py:22
  16.4 50.3 %collective-permute-start.1 = (bf16[32,64,1]{2,1,0:T(8,128)(2,1)}, bf16[32,64,1]{2,1,0:T(8,128)(2,1)}, u32[]{:S(2)}, u32[]{:S(2)}) collective-permute-start(bf16[32,64,1]{2,1,0:T(8,128)(2,1)} %get-tuple-element.40), channel_id=1, source_target_pairs={{1,0},{3,2},{5,4},{7,6},{9,8},{11,10},{13,12},{15,14},{17,16},{19,... | collective-permute-start | bytes 12296 | tf_op jit(solution)/shard_map/ppermute | solution.py:24
  20.0 28.5 %all-to-all-start.1 = ((s32[128,1,2]{2,1,0:T(1,128)}), s32[128,1,2]{2,1,0:T(1,128)S(1)}, u32[]{:S(2)}, u32[]{:S(2)}) async-start(s32[128,1,2]{2,1,0:T(1,128)} %bitcast.21), calls=%async_computation.1 | async-start | bytes 131072 | tf_op jit(solution)/shard_map/all_to_all | solution.py:88
  36.3 6.2 %copy-start.24 = (s32[1,256]{1,0:T(1,128)S(1)}, s32[1,256]{1,0:T(1,128)}, u32[]{:S(2)}) copy-start(s32[1,256]{1,0:T(1,128)} %param.23) | copy-start | bytes 3076
  36.3 6.2 %copy-start.22 = (s32[256,1]{0,1:T(1,128)S(1)}, s32[256,1]{0,1:T(1,128)}, u32[]{:S(2)}) copy-start(s32[256,1]{0,1:T(1,128)} %param.24) | copy-start | bytes 3076
  38.0 53.5 %collective-permute-start.2 = (f32[32,64,1]{1,0,2:T(8,128)S(1)}, f32[32,64,1]{1,0,2:T(8,128)S(1)}, u32[]{:S(2)}, u32[]{:S(2)}) collective-permute-start(f32[32,64,1]{1,0,2:T(8,128)S(1)} %copy.41), channel_id=1, source_target_pairs={{0,1},{2,3},{4,5},{6,7},{8,9},{10,11},{12,13},{14,15},{16,17},{18,... | collective-permute-start | bytes 24584 | tf_op jit(solution)/shard_map/ppermute | solution.py:22
  45.4 21.4 %copy-start.20 = (bf16[32,64,128]{2,1,0:T(8,128)(2,1)S(1)}, bf16[32,64,128]{2,1,0:T(8,128)(2,1)}, u32[]{:S(2)}) copy-start(bf16[32,64,128]{2,1,0:T(8,128)(2,1)} %copy-done.19) | copy-start | bytes 1572868
  48.5 64.7 %all-to-all-start.2 = ((bf16[128,2,2048]{2,1,0:T(2,128)(2,1)}), bf16[128,2,2048]{2,1,0:T(2,128)(2,1)}, u32[]{:S(2)}, u32[]{:S(2)}) async-start(bf16[128,2,2048]{2,1,0:T(2,128)(2,1)} %reshape.138), calls=%async_computation.2 | async-start | bytes 2097152 | tf_op jit(solution)/shard_map/all_to_all | solution.py:84
  65.1 6.6 %copy-start.2 = (f32[1,32,64,128]{3,2,1,0:T(8,128)S(1)}, f32[1,32,64,128]{3,2,1,0:T(8,128)}, u32[]{:S(2)}) copy-start(f32[1,32,64,128]{3,2,1,0:T(8,128)} %param.14) | copy-start | bytes 3145732
  65.1 27.8 %collective-permute-start.3 = (f32[32,64,1]{1,0,2:T(8,128)S(1)}, f32[32,64,1]{1,0,2:T(8,128)S(1)}, u32[]{:S(2)}, u32[]{:S(2)}) collective-permute-start(f32[32,64,1]{1,0,2:T(8,128)S(1)} %copy.42), channel_id=1, source_target_pairs={{1,0},{3,2},{5,4},{7,6},{9,8},{11,10},{13,12},{15,14},{17,16},{19,... | collective-permute-start | bytes 24584 | tf_op jit(solution)/shard_map/ppermute | solution.py:24
  71.7 2.8 %copy-start.21 = (f32[1,32,64,128]{3,2,1,0:T(8,128)S(1)}, f32[1,32,64,128]{3,2,1,0:T(8,128)}, u32[]{:S(2)}) copy-start(f32[1,32,64,128]{3,2,1,0:T(8,128)} %param.13) | copy-start | bytes 3145732
  84.6 13.7 %collective-permute-start.6 = (f32[32,64,1]{1,0,2:T(8,128)S(1)}, f32[32,64,1]{1,0,2:T(8,128)S(1)}, u32[]{:S(2)}, u32[]{:S(2)}) collective-permute-start(f32[32,64,1]{1,0,2:T(8,128)S(1)} %copy.53), channel_id=1, source_target_pairs={{0,1},{2,3},{4,5},{6,7},{8,9},{10,11},{12,13},{14,15},{16,17},{18,... | collective-permute-start | bytes 24584 | tf_op jit(solution)/shard_map/ppermute | solution.py:22
  90.2 9.5 %collective-permute-start.7 = (f32[32,64,1]{1,0,2:T(8,128)S(1)}, f32[32,64,1]{1,0,2:T(8,128)S(1)}, u32[]{:S(2)}, u32[]{:S(2)}) collective-permute-start(f32[32,64,1]{1,0,2:T(8,128)S(1)} %copy.54), channel_id=1, source_target_pairs={{1,0},{3,2},{5,4},{7,6},{9,8},{11,10},{13,12},{15,14},{17,16},{19,... | collective-permute-start | bytes 24584 | tf_op jit(solution)/shard_map/ppermute | solution.py:24
  101.1 2.7 %copy-start.7 = (f32[32,64,128]{2,1,0:T(8,128)S(1)}, f32[32,64,128]{2,1,0:T(8,128)}, u32[]{:S(2)}) copy-start(f32[32,64,128]{2,1,0:T(8,128)} %get-tuple-element.25) | copy-start | bytes 3145732
  101.1 2.7 %copy-start.9 = (f32[32,64,128]{2,1,0:T(8,128)S(1)}, f32[32,64,128]{2,1,0:T(8,128)}, u32[]{:S(2)}) copy-start(f32[32,64,128]{2,1,0:T(8,128)} %get-tuple-element.26) | copy-start | bytes 3145732
  101.1 2.8 %copy-start.11 = (f32[32,64,128]{2,1,0:T(8,128)S(1)}, f32[32,64,128]{2,1,0:T(8,128)}, u32[]{:S(2)}) copy-start(f32[32,64,128]{2,1,0:T(8,128)} %get-tuple-element.27) | copy-start | bytes 3145732
  101.1 3.1 %copy-start.13 = (f32[32,64,128]{2,1,0:T(8,128)S(1)}, f32[32,64,128]{2,1,0:T(8,128)}, u32[]{:S(2)}) copy-start(f32[32,64,128]{2,1,0:T(8,128)} %get-tuple-element.28) | copy-start | bytes 3145732
  132.7 27.6 %collective-permute-start.8 = (f32[32,64,1]{1,0,2:T(8,128)S(1)}, f32[32,64,1]{1,0,2:T(8,128)S(1)}, u32[]{:S(2)}, u32[]{:S(2)}) collective-permute-start(f32[32,64,1]{1,0,2:T(8,128)S(1)} %copy.61), channel_id=1, source_target_pairs={{0,1},{2,3},{4,5},{6,7},{8,9},{10,11},{12,13},{14,15},{16,17},{18,... | collective-permute-start | bytes 24584 | tf_op jit(solution)/shard_map/ppermute | solution.py:22
  137.1 24.6 %collective-permute-start.9 = (f32[32,64,1]{1,0,2:T(8,128)S(1)}, f32[32,64,1]{1,0,2:T(8,128)S(1)}, u32[]{:S(2)}, u32[]{:S(2)}) collective-permute-start(f32[32,64,1]{1,0,2:T(8,128)S(1)} %copy.62), channel_id=1, source_target_pairs={{1,0},{3,2},{5,4},{7,6},{9,8},{11,10},{13,12},{15,14},{17,16},{19,... | collective-permute-start | bytes 24584 | tf_op jit(solution)/shard_map/ppermute | solution.py:24
  140.7 36.3 %all-to-all-start = ((s32[128,1,4]{2,1,0:T(1,128)}), s32[128,1,4]{2,1,0:T(1,128)S(1)}, u32[]{:S(2)}, u32[]{:S(2)}) async-start(s32[128,1,4]{2,1,0:T(1,128)} %bitcast.7), calls=%async_computation | async-start | bytes 131072 | tf_op jit(solution)/shard_map/all_to_all | solution.py:134
  163.1 2.7 %copy-start.12 = (f32[32,64,128]{2,1,0:T(8,128)S(1)}, f32[32,64,128]{2,1,0:T(8,128)}, u32[]{:S(2)}) copy-start(f32[32,64,128]{2,1,0:T(8,128)} %get-tuple-element.27) | copy-start | bytes 3145732
  163.1 2.8 %copy-start.14 = (f32[32,64,128]{2,1,0:T(8,128)S(1)}, f32[32,64,128]{2,1,0:T(8,128)}, u32[]{:S(2)}) copy-start(f32[32,64,128]{2,1,0:T(8,128)} %get-tuple-element.28) | copy-start | bytes 3145732
  163.1 3.1 %copy-start.15 = (f32[32,64,128]{2,1,0:T(8,128)S(1)}, f32[32,64,128]{2,1,0:T(8,128)}, u32[]{:S(2)}) copy-start(f32[32,64,128]{2,1,0:T(8,128)} %get-tuple-element.29) | copy-start | bytes 3145732
  177.0 65.5 %all-to-all-start.3 = ((f32[128,32,128]{2,1,0:T(8,128)}), f32[128,32,128]{2,1,0:T(8,128)S(1)}, u32[]{:S(2)}, u32[]{:S(2)}) async-start(f32[128,32,128]{2,1,0:T(8,128)} %reshape.142), calls=%async_computation.3 | async-start | bytes 4194304 | tf_op jit(solution)/shard_map/all_to_all | solution.py:139
  244.0 3.6 %copy-start.1 = (bf16[1,2,2048]{2,1,0:T(2,128)(2,1)S(1)}, bf16[1,2,2048]{2,1,0:T(2,128)(2,1)}, u32[]{:S(2)}) copy-start(bf16[1,2,2048]{2,1,0:T(2,128)(2,1)} %param.20) | copy-start | bytes 24580
  (7 other events, 16.9 us)

commit v2 on v0

v2 whole, which is shorter than its diff:
```python
import functools

import jax
import jax.numpy as jnp
from jax import lax
from jax.experimental import pallas as pl
from jax.experimental.pallas import tpu as pltpu
from jax.sharding import PartitionSpec as P

STEP = 0.08
MT_DEV = 8
CAP = 2
CAPT = 4
CLASSES = 16
CODE_ZERO = 4096.0
VMEM_LIMIT = 56 * 1024 * 1024

F32 = jnp.float32
BF16 = jnp.bfloat16
I32 = jnp.int32


def call(kernel, name, out_shape, scratch=(), smem=()):
    def run(*args):
        specs = [
            pl.BlockSpec(memory_space=pltpu.SMEM if i in smem else pltpu.VMEM)
            for i in range(len(args))
        ]
        outs = jax.tree.map(lambda s: pl.BlockSpec(memory_space=pltpu.VMEM), out_shape)
        return pl.pallas_call(
            kernel,
            out_shape=out_shape,
            in_specs=specs,
            out_specs=outs,
            scratch_shapes=list(scratch),
            name=name,
            compiler_params=pltpu.CompilerParams(vmem_limit_bytes=VMEM_LIMIT),
        )(*args)

    return run


def sds(shape, dtype=F32):
    return jax.ShapeDtypeStruct(shape, dtype)


def iota(shape, dim):
    return lax.broadcasted_iota(I32, shape, dim)


def pieces(value):
    first = value.astype(BF16)
    rest = value - first.astype(F32)
    second = rest.astype(BF16)
    third = (rest - second.astype(F32)).astype(BF16)
    return first, second, third


def exact_dot(onehot, value):
    first, second, third = pieces(value)
    out = jnp.dot(onehot, third, preferred_element_type=F32)
    out = out + jnp.dot(onehot, second, preferred_element_type=F32)
    return out + jnp.dot(onehot, first, preferred_element_type=F32)


def as_column(row):
    size = row.shape[1]
    eye = iota((size, size), 0) == iota((size, size), 1)
    return jnp.sum(jnp.where(eye, row, 0), axis=1, keepdims=True)


def rank_row(keys):
    size = keys.shape[1]
    first, second = iota((size, size), 0), iota((size, size), 1)
    same = (as_column(keys) == keys) & (first < second)
    return jnp.sum(same.astype(F32), axis=0, keepdims=True)


def face_row(plane, half, high):
    rows, lanes = plane.shape
    column = jnp.where(high, plane[:, lanes - 1 : lanes], plane[:, 0:1])
    here = iota((rows, lanes), 1) == iota((rows, lanes), 0) + half * rows
    return jnp.sum(jnp.where(here, column, 0.0), axis=0, keepdims=True)


def face_planes(stored, kind, pair, half, low, rows):
    lanes = stored.shape[1]
    target = jnp.where(low, lanes - 1, 0)
    shift = lax.rem(target - (kind * 16 + pair) + 2 * lanes, lanes)
    return pltpu.roll(stored[half * rows : (half + 1) * rows, :], shift, 1)


def along_second(plane):
    rows, lanes = plane.shape
    place = iota((rows, lanes), 0)
    up = jnp.where(place == rows - 1, 0.0, pltpu.roll(plane, rows - 1, 0))
    down = jnp.where(place == 0, 0.0, pltpu.roll(plane, 1, 0))
    return up, down


def along_depth(plane, halo, is_low, is_high):
    rows, lanes = plane.shape
    place = iota((rows, lanes), 1)
    up = jnp.where(place == lanes - 1, halo * is_low, pltpu.roll(plane, lanes - 1, 1))
    down = jnp.where(place == 0, halo * is_high, pltpu.roll(plane, 1, 1))
    return up, down


def around(load, x, last, halo, is_low, is_high):
    here = load(x)
    after = load(jnp.minimum(x + 1, last)) * (x < last).astype(F32)
    before = load(jnp.maximum(x - 1, 0)) * (x > 0).astype(F32)
    return here, (
        after,
        before,
        *along_second(here),
        *along_depth(here, halo, is_low, is_high),
    )


def weights(load, x, last, halo, is_low, is_high):
    here, sides = around(load, x, last, halo, is_low, is_high)
    return [0.5 * (here + side) for side in sides]


def operate(load, x, last, halo, is_low, is_high, factors):
    here, sides = around(load, x, last, halo, is_low, is_high)
    total = factors[0] * (sides[0] - here)
    for factor, side in zip(factors[1:], sides[1:]):
        total = total + factor * (side - here)
    return here, total


def which_half():
    half = lax.axis_index("ap")
    low = half == 0
    return low, low.astype(F32), (half == 1).astype(F32)


def faces_kernel(now, buoy, bulk, nxt, out):
    low, _, _ = which_half()
    out[...] = jnp.zeros_like(out)

    def body(pair, carry):
        for kind in range(3):
            row = jnp.zeros((1, now.shape[2]), F32)
            for half in range(2):
                x = 2 * pair + half
                plane = (now[x], buoy[x], None)[kind] if kind < 2 else bulk[x] * nxt[x]
                row = row + face_row(plane, half, low)
            out[pl.ds(kind * 16 + pair, 1), :] = row
        return carry

    lax.fori_loop(0, now.shape[0] // 2, body, 0)


def stored_faces(faces, scratch):
    copies = scratch.shape[0] // faces.shape[0]
    scratch[...] = jnp.transpose(jnp.concatenate([faces[...]] * copies, axis=0))


def first_kernel(
    faces, now, prev, bulk, buoy, nxt, late, lap_out, mid_out, base_out, face_out, stored
):
    low, is_low, is_high = which_half()
    stored_faces(faces, stored)
    count, rows, lanes = now.shape
    last = count - 1

    def body(pair, carry):
        row = jnp.zeros((1, lanes), F32)
        for half in range(2):
            x = 2 * pair + half
            halos = [face_planes(stored, k, pair, half, low, rows) for k in range(3)]
            factors = weights(lambda i: buoy[i], x, last, halos[1], is_low, is_high)
            here, lap = operate(lambda i: now[i], x, last, halos[0], is_low, is_high, factors)
            lap_out[x] = lap
            scale = STEP * bulk[x]
            mid = 2.0 * here - prev[x] + scale * lap
            mid_out[x] = mid
            row = row + face_row(mid, half, low)
            _, lap_adj = operate(
                lambda i: bulk[i] * nxt[i], x, last, halos[2], is_low, is_high, factors
            )
            base_out[x] = 2.0 * nxt[x] - late[x] + STEP * lap_adj
        face_out[pl.ds(pair, 1), :] = row
        return carry

    lax.fori_loop(0, count // 2, body, 0)


def second_kernel(faces, mid_face, mid, now, bulk, buoy, lap_out, end_out, stored, stored_mid):
    low, is_low, is_high = which_half()
    stored_faces(faces, stored)
    stored_faces(mid_face, stored_mid)
    count, rows, lanes = now.shape
    last = count - 1

    def body(pair, carry):
        for half in range(2):
            x = 2 * pair + half
            halo_b = face_planes(stored, 1, pair, half, low, rows)
            halo_v = face_planes(stored_mid, 0, pair, half, low, rows)
            factors = weights(lambda i: buoy[i], x, last, halo_b, is_low, is_high)
            here, lap = operate(lambda i: mid[i], x, last, halo_v, is_low, is_high, factors)
            lap_out[x] = lap
            end_out[x] = 2.0 * here - now[x] + (STEP * bulk[x]) * lap
        return carry

    lax.fori_loop(0, count // 2, body, 0)


def pack_traces_kernel(groups, receivers, traces, out):
    keys = groups[...]
    place = keys.astype(F32) * CAP + rank_row(keys)
    slots = out.shape[0]
    count, samples = traces.shape
    chosen = (iota((slots, count), 0).astype(F32) == place).astype(F32).astype(BF16)
    ids = as_column(receivers[...].astype(F32))
    ids = jnp.where(iota((count, 128), 1) == 0, ids, 0.0).astype(BF16)
    out[:, :samples] = jnp.dot(chosen, traces[...], preferred_element_type=F32).astype(BF16)
    out[:, samples:] = jnp.dot(chosen, ids, preferred_element_type=F32).astype(BF16)


def places_kernel(
    cells, mid, end, owners, slots, seen_out, hot_depth_out, hot_rows_out, place_out, cls_out,
    spot_out, ids_out,
):
    lanes = 128
    count = cells.shape[1]
    rows = hot_rows_out.shape[0]
    cell_row = cells[...]
    row_of = lax.shift_right_logical(cell_row, 7)
    hot_rows_out[...] = (iota((rows, count), 0) == row_of).astype(F32).astype(BF16)
    cell_col = as_column(cell_row)
    hot_depth = (iota((count, lanes), 1) == (cell_col & (lanes - 1))).astype(F32)
    hot_depth_out[...] = hot_depth
    row_col = lax.shift_right_logical(cell_col, 7)
    picked = jnp.zeros((count, 2 * lanes), F32)
    chunk = 256
    for start in range(0, rows, chunk):
        hot = (iota((count, chunk), 1) + start == row_col).astype(F32).astype(BF16)
        planes = slice(start // 64, (start + chunk) // 64)
        both = jnp.concatenate(
            [mid[planes].reshape(chunk, lanes), end[planes].reshape(chunk, lanes)], axis=1
        )
        picked = picked + exact_dot(hot, both)
    seen_mid = jnp.sum(picked[:, :lanes] * hot_depth, axis=1, keepdims=True)
    seen_end = jnp.sum(picked[:, lanes:] * hot_depth, axis=1, keepdims=True)
    seen_out[...] = jnp.where(iota((count, lanes), 1) == 0, seen_mid, seen_end)

    owner = owners[...]
    tiles = owner.shape[1]
    rank = rank_row(owner).astype(I32)
    cls = owner & (CLASSES - 1)
    spot = lax.shift_right_logical(owner, 4) * CAPT + rank
    per_class = 8 * CAPT
    place_out[...] = cls * (per_class + 1) + spot
    cls_hot = (iota((CLASSES, tiles), 0) == cls).astype(F32).astype(BF16)
    cls_out[...] = cls_hot
    spot_hot = (iota((tiles, lanes), 1) == as_column(spot)).astype(F32)
    spot_out[...] = spot_hot
    slot_col = as_column(slots[...]).astype(F32)
    ids_out[...] = jnp.dot(
        cls_hot, (spot_hot * slot_col).astype(BF16), preferred_element_type=F32
    )


def inject_kernel(
    rows_in, filters, seen, hot_depth, hot_rows, base, bulk, mid_out, add_out, face_out
):
    low, _, _ = which_half()
    samples = filters.shape[1]
    count, lanes = hot_depth.shape
    slots = rows_in.shape[0]
    last_dims = (((1,), (1,)), ((), ()))
    values = lax.dot_general(
        rows_in[:, :samples], filters[...], last_dims, preferred_element_type=F32
    )
    pick = ((iota((8, 128), 0) == 0) & (iota((8, 128), 1) == 0)).astype(F32).astype(BF16)
    ids = lax.dot_general(pick, rows_in[:, samples:], last_dims, preferred_element_type=F32)
    hot = (iota((count, slots), 0).astype(F32) == ids[0:1, :]).astype(F32).astype(BF16)
    observed = exact_dot(hot, values)
    resid_mid = seen[:, 0:1] - observed[:, 0:1]
    resid_end = seen[:, 1:2] - observed[:, 1:2]
    spread = jnp.concatenate([hot_depth[...] * resid_end, hot_depth[...] * resid_mid], axis=1)
    first, second, third = pieces(spread)

    def body(pair, carry):
        hot_here = hot_rows[pl.ds(pl.multiple_of(pair * 128, 128), 128), :]
        added = jnp.dot(hot_here, third, preferred_element_type=F32)
        added = added + jnp.dot(hot_here, second, preferred_element_type=F32)
        added = added + jnp.dot(hot_here, first, preferred_element_type=F32)
        row = jnp.zeros((1, lanes), F32)
        for half in range(2):
            x = 2 * pair + half
            field = base[x] + added[half * 64 : (half + 1) * 64, :lanes]
            mid_out[x] = field
            add_out[x] = added[half * 64 : (half + 1) * 64, lanes:]
            row = row + face_row(bulk[x] * field, half, low)
        face_out[pl.ds(pair, 1), :] = row
        return carry

    lax.fori_loop(0, base.shape[0] // 2, body, 0)


def image_kernel(
    faces, adj_face, mid, add, nxt, bulk, buoy, lap_mid, lap_now, place, cls_hot, spot_hot, ids,
    last_out, send_out, stored, stored_adj, codes,
):
    low, is_low, is_high = which_half()
    stored_faces(faces, stored)
    stored_faces(adj_face, stored_adj)
    count, rows, lanes = mid.shape
    last = count - 1
    tiles = rows // 8
    per_class = send_out.shape[0] // CLASSES

    def clear(c, carry):
        send_out[pl.ds(c * per_class, per_class)] = jnp.zeros((per_class, 8, lanes), jnp.int16)
        return carry

    lax.fori_loop(0, CLASSES, clear, 0)

    def body(pair, carry):
        for half in range(2):
            x = 2 * pair + half
            halo_b = face_planes(stored, 1, pair, half, low, rows)
            halo_v = face_planes(stored_adj, 0, pair, half, low, rows)
            factors = weights(lambda i: buoy[i], x, last, halo_b, is_low, is_high)
            _, lap = operate(
                lambda i: bulk[i] * mid[i], x, last, halo_v, is_low, is_high, factors
            )
            here = mid[x]
            end = 2.0 * here - nxt[x] + STEP * lap + add[x]
            last_out[x] = end
            image = (STEP * (here * lap_mid[x] + end * lap_now[x])).reshape(tiles, 8, lanes)
            peak = jnp.max(jnp.max(jnp.abs(image), axis=1), axis=1, keepdims=True)
            code = jnp.ceil(16.0 * jnp.log2(jnp.maximum(peak, 1e-30))) + 1.0
            codes[pl.ds(pl.multiple_of(x * tiles, tiles), tiles), :] = jnp.broadcast_to(
                code + CODE_ZERO, (tiles, lanes)
            )
            gain = jnp.broadcast_to(32767.0 * jnp.exp2(code * (-1.0 / 16.0)), (tiles, lanes))
            whole = jnp.round(image * gain[:, None, :]).astype(I32).astype(jnp.int16)
            for t in range(tiles):
                send_out[place[0, x * tiles + t]] = whole[t]
        return carry

    lax.fori_loop(0, count // 2, body, 0)
    code = codes[...]
    upper = jnp.floor(code * (1.0 / 64.0))
    lower = code - 64.0 * upper
    hot = cls_hot[...]
    spread = spot_hot[...]
    sent = 64.0 * jnp.dot(hot, (spread * upper).astype(BF16), preferred_element_type=F32)
    sent = sent + jnp.dot(hot, (spread * lower).astype(BF16), preferred_element_type=F32)
    place_row = iota((8, lanes), 0)
    for c in range(CLASSES):
        tile = jnp.where(
            place_row == 0,
            ids[c : c + 1, :],
            jnp.where(place_row == 1, sent[c : c + 1, :], 0.0),
        )
        send_out[c * per_class + per_class - 1] = tile.astype(I32).astype(jnp.int16)


def combine_kernel(slots, gains, got, out, *partial):
    per_class = got.shape[0] // CLASSES
    used = per_class - 1
    for part in partial:
        part[...] = jnp.zeros_like(part)

    def body(src, carry):
        for s in range(used):
            part = partial[s % CAPT]
            at = (s // CAPT) * MT_DEV + slots[src, s]
            value = got[src * per_class + s].astype(I32).astype(F32) * gains[src, s]
            part[at] = part[at] + value
        return carry

    lax.fori_loop(0, CLASSES, body, 0)
    total = partial[0][...]
    for part in partial[1:]:
        total = total + part[...]
    out[...] = total


def swap(face):
    return lax.ppermute(face, "ap", [(0, 1), (1, 0)])


def local(
    wave_prev,
    wave_now,
    adjoint_late,
    adjoint_next,
    bulk,
    buoyancy,
    traces,
    group_filter,
    trace_group,
    trace_receiver,
    receiver_cell,
    tile_owner,
    tile_slot,
):
    shots = lax.axis_size("shot")
    rings = shots // CLASSES
    prev, now, late, nxt = wave_prev[0], wave_now[0], adjoint_late[0], adjoint_next[0]
    bulk, buoy = bulk[0], buoyancy[0]
    count, rows, lanes = now.shape
    field = sds(now.shape)
    samples = traces.shape[1]
    face = sds((16, lanes))
    square = pltpu.VMEM((lanes, lanes), F32)

    packed = call(pack_traces_kernel, "pack_traces", sds((shots * CAP, samples + 128), BF16))(
        trace_group.reshape(1, -1), trace_receiver.reshape(1, -1), traces
    )
    got_rows = lax.all_to_all(
        packed.reshape(shots, CAP, samples + 128), "shot", split_axis=0, concat_axis=0, tiled=True
    ).reshape(shots * CAP, samples + 128)

    faces = swap(call(faces_kernel, "faces", sds((64, lanes)))(now, buoy, bulk, nxt))
    lap_now, wave_mid, adj_base, mid_face = call(
        first_kernel, "first_step", (field, field, field, face), [square]
    )(faces, now, prev, bulk, buoy, nxt, late)
    lap_mid, wave_end = call(second_kernel, "second_step", (field, field), [square, square])(
        faces, swap(mid_face), wave_mid, now, bulk, buoy
    )
    receivers = receiver_cell.shape[1]
    tiles = tile_owner.shape[0]
    seen, hot_depth, hot_rows, place, cls_hot, spot_hot, ids = call(
        places_kernel,
        "places",
        (
            sds((receivers, lanes)),
            sds((receivers, lanes)),
            sds((count * rows, receivers), BF16),
            sds((1, tiles), I32),
            sds((CLASSES, tiles), BF16),
            sds((tiles, lanes)),
            sds((CLASSES, lanes)),
        ),
    )(receiver_cell, wave_mid, wave_end, tile_owner.reshape(1, -1), tile_slot.reshape(1, -1))
    filters = jnp.pad(group_filter[0], ((0, 14), (0, 0)))
    adj_mid, adj_add, adj_face = call(inject_kernel, "inject", (field, field, face))(
        got_rows, filters, seen, hot_depth, hot_rows, adj_base, bulk
    )
    per_class = (shots // CLASSES) * CAPT + 1
    adj_end, send = call(
        image_kernel,
        "image",
        (field, sds((CLASSES * per_class, 8, lanes), jnp.int16)),
        [square, square, pltpu.VMEM((tiles, lanes), F32)],
        smem=(9,),
    )(
        faces, swap(adj_face), adj_mid, adj_add, nxt, bulk, buoy, lap_mid, lap_now, place,
        cls_hot, spot_hot, ids,
    )
    near = [[r * CLASSES + c for c in range(CLASSES)] for r in range(rings)]
    far = [[r * CLASSES + c for r in range(rings)] for c in range(CLASSES)]
    got = lax.all_to_all(
        send.reshape(CLASSES, per_class * 8, lanes),
        "shot",
        split_axis=0,
        concat_axis=0,
        axis_index_groups=near,
        tiled=True,
    ).reshape(CLASSES, per_class, 8, lanes)
    used = per_class - 1
    slots = got[:, used, 0, :used].astype(I32)
    code = got[:, used, 1, :used].astype(F32)
    gains = jnp.where(code > 0, jnp.exp2((code - CODE_ZERO) * (1.0 / 16.0)) * (1.0 / 32767.0), 0.0)
    owned = rings * MT_DEV
    dense = call(
        combine_kernel,
        "combine",
        sds((owned, 8, lanes)),
        [pltpu.VMEM((owned, 8, lanes), F32)] * CAPT,
        smem=(0, 1),
    )(slots, gains, got.reshape(CLASSES * per_class, 8, lanes))
    shared = lax.all_to_all(
        dense.reshape(rings, MT_DEV * 8, lanes),
        "shot",
        split_axis=0,
        concat_axis=0,
        axis_index_groups=far,
        tiled=True,
    )
    model_grad = jnp.sum(shared, axis=0).reshape(MT_DEV, 8, lanes)
    return (model_grad, wave_end[None], adj_end[None])


def solution(mesh):
    placed = (
        P("shot", None, None, "ap"),
        P("shot", None, None, "ap"),
        P("shot", None, None, "ap"),
        P("shot", None, None, "ap"),
        P("shot", None, None, "ap"),
        P("shot", None, None, "ap"),
        P(("shot", "ap"), None),
        P("shot", None, None),
        P(("shot", "ap"), None),
        P(("shot", "ap")),
        P("shot", "ap"),
        P("shot", None),
        P("shot"),
    )
    return jax.shard_map(
        local,
        mesh=mesh,
        in_specs=placed,
        out_specs=(P("shot", None, "ap"), P("shot", None, None, "ap"), P("shot", None, None, "ap")),
        check_vma=False,
    )
```

time: 844 us -> 135 us (0.16)
  waiting for transfers between devices: 662 us -> 8.64 us
  Pallas kernels: 0 us -> 54 us
  other arithmetic: 51.5 us -> 1.84 us
  blocking collectives: 0 us -> 45.6 us
  starting transfers between devices: 59.4 us -> 16.8 us
  local copies, waits for them, and re-layouts: 46.1 us -> 6.98 us
  between operations: 14.6 us -> 0.67 us
    reduce_scatter x1 -> x0, waiting for transfers between devices: 662 us -> none  [local(): lax.psum_scatter(summed.reshape(lax.axis_size('shot') * MT_DEV, TILE_CELL...]
    pallas_call x0 -> x8, Pallas kernels: none -> 54 us  [run(): pl.pallas_call(kernel, out_shape=out_shape, in_specs=specs, out_specs=out...]
    all_to_all x0 -> x2, blocking collectives: none -> 45.6 us  [the longest x1 28.2 us: local(): lax.all_to_all(send.reshape(CLASSES, per_class * 8, lanes), 'shot', split...]
    ppermute x10 -> x3, starting transfers between devices: 28.1 us -> 0.4 us  [swap(): return lax.ppermute(face, 'ap', [(0, 1), (1, 0)])]
    slice x14 -> x0, local copies, waits for them, and re-layouts: 18 us -> none  [the longest x8 12.7 us: padded(): head = lax.slice_in_dim(cells, 0, width, axis=dim)]
    mul x4 -> x0, other arithmetic: 15.2 us -> none  [the longest x1 9.62 us: local(): bulk_here * adjoint_mid]
    all_to_all x2 -> x1, starting transfers between devices: 31.2 us -> 16.4 us  [local(): lax.all_to_all(packed.reshape(shots, CAP, samples + 128), 'shot', split_a...]
    add x3 -> x0, other arithmetic: 12.3 us -> none  [the longest x1 6.87 us: local(): wave_mid = 2.0 * wave_cur - wave_old + STEP * bulk_here * lap_now]
  transfers between devices with their start and end apart: 13 -> 4, of which waited for: 1 -> 3; matrix products, arithmetic and copies ran while one was open for 7% -> 0% of each run, Pallas kernels for 0% -> 21%
where the time goes in v2:
time: 135 us
  Pallas kernels  54 us (40%)
  blocking collectives  45.6 us (34%)
  starting transfers between devices  16.8 us (12%)
  waiting for transfers between devices  8.64 us (6%)
  local copies, waits for them, and re-layouts  6.98 us (5%)
  other arithmetic  1.84 us (1%)
    pallas_call x8, Pallas kernels, run(): pl.pallas_call(kernel, out_shape=out_shape, in_specs=specs, out_specs=out...  54 us
    all_to_all x1, blocking collectives, local(): lax.all_to_all(send.reshape(CLASSES, per_class * 8, lanes), 'shot', split...  28.2 us
    all_to_all x1, blocking collectives, local(): lax.all_to_all(dense.reshape(rings, MT_DEV * 8, lanes), 'shot', split_axi...  17.5 us
    all_to_all x1, starting transfers between devices, local(): lax.all_to_all(packed.reshape(shots, CAP, samples + 128), 'shot', split_a...  16.4 us
    ppermute x3, waiting for transfers between devices, swap(): return lax.ppermute(face, 'ap', [(0, 1), (1, 0)])  8.64 us
  transfers between devices with their start and end apart: 4, of which 3 were waited for; matrix products, arithmetic and copies ran while one was open for 0% of the time, Pallas kernels for 21%

profile of v2, /device:TPU:1, one launch (start us, length us, event | category | flops | bytes accessed | tf_op | source)
XLA Modules:
  0.0 134.6 jit_solution(4054698155525501604)
XLA Ops:
  0.6 2.6 %pack_traces.1 = bf16[256,2176]{1,0:T(8,128)(2,1)} custom-call(s32[1,128]{1,0:T(1,128)} %bitcast.52, s32[1,128]{1,0:T(1,128)} %bitcast.53, bf16[128,2048]{1,0:T(8,128)(2,1)} %traces.1), custom_call_target="tpu_custom_call" | custom-call | tf_op jit(solution)/shard_map/pack_traces/pallas_call | solution.py:30
  3.3 2.3 %reshape.48 = bf16[128,2,2176]{2,1,0:T(2,128)(2,1)} reshape(bf16[256,2176]{1,0:T(8,128)(2,1)} %pack_traces.1) | data formatting | bytes 2228224 | tf_op jit(solution)/shard_map/reshape | solution.py:421
  5.6 16.4 %all-to-all-start = ((bf16[128,2,2176]{2,1,0:T(2,128)(2,1)}), bf16[128,2,2176]{2,1,0:T(2,128)(2,1)S(1)}, u32[]{:S(2)}, u32[]{:S(2)}) async-start(bf16[128,2,2176]{2,1,0:T(2,128)(2,1)} %reshape.48), calls=%async_computation | async-start | bytes 2228224 | tf_op jit(solution)/shard_map/all_to_all | solution.py:420
  22.0 6.6 %faces.1 = f32[64,128]{1,0:T(8,128)} custom-call(f32[32,64,128]{2,1,0:T(8,128)} %bitcast.38, f32[32,64,128]{2,1,0:T(8,128)} %bitcast.30, f32[32,64,128]{2,1,0:T(8,128)} %bitcast.25, f32[32,64,128]{2,1,0:T(8,128)} %bitcast.35), custom_call_target="tpu_custom_call" | custom-call | tf_op jit(solution)/shard_map/faces/pallas_call | solution.py:30
  28.5 0.4 collective-permute-start
  28.9 3.5 %collective-permute-done.faces = f32[64,128]{1,0:T(8,128)S(1)} collective-permute-done((f32[64,128]{1,0:T(8,128)}, f32[64,128]{1,0:T(8,128)S(1)}, u32[]{:S(2)}, u32[]{:S(2)}) %collective-permute-start) | collective-permute-done | bytes 32800 | tf_op jit(solution)/shard_map/ppermute | solution.py:389
  32.4 0.0 copy-start.1
  32.4 0.6 copy-done.1
  33.1 0.0 copy-start.4
  33.1 11.3 %first_step.1 = (f32[32,64,128]{2,1,0:T(8,128)}, f32[32,64,128]{2,1,0:T(8,128)}, f32[32,64,128]{2,1,0:T(8,128)}, f32[16,128]{1,0:T(8,128)}) custom-call(f32[64,128]{1,0:T(8,128)} %copy-done.1, f32[32,64,128]{2,1,0:T(8,128)} %bitcast.39, f32[32,64,128]{2,1,0:T(8,128)} %bitcast.46, f32[32,64,128]{2,1,0:T(8,128)} %bitcast.26, f32[32,64,128]{2,1,0:T(8,128)} %bitcast.31, ...), custom_call_target="tpu_custom_call" | custom-call | tf_op jit(solution)/shard_map/first_step/pallas_call | solution.py:30
  44.4 0.0 collective-permute-start.1
  44.4 0.0 copy-done.4
  44.4 0.6 pad.4.filters
  45.0 2.4 %collective-permute-done.1.mid_face = f32[16,128]{1,0:T(8,128)S(1)} collective-permute-done((f32[16,128]{1,0:T(8,128)}, f32[16,128]{1,0:T(8,128)S(1)}, u32[]{:S(2)}, u32[]{:S(2)}) %collective-permute-start.1) | collective-permute-done | bytes 8224 | tf_op jit(solution)/shard_map/ppermute | solution.py:389
  47.5 0.6 copy-done.3
  48.1 6.6 %second_step.1 = (f32[32,64,128]{2,1,0:T(8,128)}, f32[32,64,128]{2,1,0:T(8,128)}) custom-call(f32[64,128]{1,0:T(8,128)} %copy-done.1, f32[16,128]{1,0:T(8,128)} %copy-done.3, f32[32,64,128]{2,1,0:T(8,128)} %get-tuple-element.21.mid, f32[32,64,128]{2,1,0:T(8,128)} %bitcast.40, f32[32,64,128]{2,1,0:T(8,128)} %bitcast.27, f32[32,64,128]{2,1,0:T(8,128)} %bitcast.32), custom_call_target="tpu_custom_call" | custom-call | tf_op jit(solution)/shard_map/second_step/pallas_call | solution.py:30
  54.7 4.3 %places.1 = (f32[256,128]{1,0:T(8,128)}, f32[256,128]{1,0:T(8,128)}, bf16[2048,256]{1,0:T(8,128)(2,1)}, s32[1,256]{1,0:T(1,128)}, bf16[16,256]{1,0:T(8,128)(2,1)...) custom-call(s32[1,256]{1,0:T(1,128)} %cells.1, f32[32,64,128]{2,1,0:T(8,128)} %get-tuple-element.21.mid, ...), custom_call_target="tpu_custom_call" | custom-call | tf_op jit(solution)/shard_map/places/pallas_call | solution.py:30
  58.9 0.0 all-to-all-done
  58.9 1.3 reshape.49.rows_in
  60.2 10.3 %inject.1 = (f32[32,64,128]{2,1,0:T(8,128)}, f32[32,64,128]{2,1,0:T(8,128)}, f32[16,128]{1,0:T(8,128)}) custom-call(bf16[256,2176]{1,0:T(8,128)(2,1)} %reshape.49.rows_in, bf16[16,2048]{1,0:T(8,128)(2,1)} %pad.4.filters, f32[256,128]{1,0:T(8,128)} %get-tuple-element.24.seen, f32[256,128]{1,0:T(8,128)} %get-tuple-element.25.hot_depth, ...), custom_call_target="tpu_custom_call" | custom-call | tf_op jit(solution)/shard_map/inject/pallas_call | solution.py:30
  70.5 0.0 collective-permute-start.2
  70.5 2.7 %collective-permute-done.2.adj_face = f32[16,128]{1,0:T(8,128)S(1)} collective-permute-done((f32[16,128]{1,0:T(8,128)}, f32[16,128]{1,0:T(8,128)S(1)}, u32[]{:S(2)}, u32[]{:S(2)}) %collective-permute-start.2) | collective-permute-done | bytes 8224 | tf_op jit(solution)/shard_map/ppermute | solution.py:389
  73.2 0.6 copy-done.2
  73.8 9.5 %image.1 = (f32[32,64,128]{2,1,0:T(8,128)}, s16[528,8,128]{2,1,0:T(8,128)(2,1)}) custom-call(f32[64,128]{1,0:T(8,128)} %copy-done.1, f32[16,128]{1,0:T(8,128)} %copy-done.2, f32[32,64,128]{2,1,0:T(8,128)} %get-tuple-element.29.mid, f32[32,64,128]{2,1,0:T(8,128)} %get-tuple-element.30.add, f32[32,64,128]{2,1,0:T(8,128)} %bitcast.37, f32[32,64,128]{2,1,0:T(8,128)} %bitcast.29, ...), custom_call_target="tpu_custom_call" | custom-call | tf_op jit(solution)/shard_map/image/pallas_call | solution.py:30
  83.3 28.2 %all_to_all.15 = s16[16,264,128]{2,1,0:T(8,128)(2,1)S(1)} all-to-all(s16[16,264,128]{2,1,0:T(8,128)(2,1)} %bitcast.43), channel_id=1, replica_groups={{0,2,4,6,8,10,12,14,16,18,20,22,24,26,28,30},{32,34,36,38,40,42,44,46,4..., dimensions={0} | all-to-all | bytes 2162688 | tf_op jit(solution)/shard_map/all_to_all | solution.py:463
  111.5 0.1 copy.16
  111.6 0.8 copy-done
  112.4 0.6 fusion.4.gains
  113.1 0.6 fusion.5.slots
  113.7 2.9 %combine.1 = f32[64,8,128]{2,1,0:T(8,128)} custom-call(s32[16,32]{1,0:T(8,128)} %fusion.5.slots, f32[16,32]{1,0:T(8,128)} %fusion.4.gains, s16[528,8,128]{2,1,0:T(8,128)(2,1)} %bitcast.34), custom_call_target="tpu_custom_call" | custom-call | tf_op jit(solution)/shard_map/combine/pallas_call | solution.py:30
  116.5 17.5 %all_to_all.16 = f32[8,64,128]{2,1,0:T(8,128)S(1)} all-to-all(f32[8,64,128]{2,1,0:T(8,128)} %bitcast.45), channel_id=1, replica_groups={{0,32,64,96,128,160,192,224},{2,34,66,98,130,162,194,226},{4,36,68,100,..., dimensions={0} | all-to-all | bytes 524288 | tf_op jit(solution)/shard_map/all_to_all | solution.py:483
  134.0 0.6 reduce_sum.9
  (3 shorter events, 0.0 us)
Async XLA Ops:
  5.6 53.4 %all-to-all-start = ((bf16[128,2,2176]{2,1,0:T(2,128)(2,1)}), bf16[128,2,2176]{2,1,0:T(2,128)(2,1)S(1)}, u32[]{:S(2)}, u32[]{:S(2)}) async-start(bf16[128,2,2176]{2,1,0:T(2,128)(2,1)} %reshape.48), calls=%async_computation | async-start | bytes 2228224 | tf_op jit(solution)/shard_map/all_to_all | solution.py:420
  28.5 3.9 %collective-permute-start = (f32[64,128]{1,0:T(8,128)}, f32[64,128]{1,0:T(8,128)S(1)}, u32[]{:S(2)}, u32[]{:S(2)}) collective-permute-start(f32[64,128]{1,0:T(8,128)} %faces.1), channel_id=1, source_target_pairs={{0,1},{1,0},{2,3},{3,2},{4,5},{5,4},{6,7},{7,6},{8,9},{9,8},{10,11... | collective-permute-start | bytes 98312 | tf_op jit(solution)/shard_map/ppermute | solution.py:389
  32.4 0.6 copy-start.1
  33.1 11.3 %copy-start.4 = (bf16[1,2,2048]{2,1,0:T(2,128)(2,1)S(1)}, bf16[1,2,2048]{2,1,0:T(2,128)(2,1)}, u32[]{:S(2)}) copy-start(bf16[1,2,2048]{2,1,0:T(2,128)(2,1)} %param.20) | copy-start | bytes 24580
  44.4 3.1 %collective-permute-start.1 = (f32[16,128]{1,0:T(8,128)}, f32[16,128]{1,0:T(8,128)S(1)}, u32[]{:S(2)}, u32[]{:S(2)}) collective-permute-start(f32[16,128]{1,0:T(8,128)} %get-tuple-element.22), channel_id=1, source_target_pairs={{0,1},{1,0},{2,3},{3,2},{4,5},{5,4},{6,7},{7,6},{8,9},{9,8},{10,11... | collective-permute-start | bytes 24584 | tf_op jit(solution)/shard_map/ppermute | solution.py:389
  47.5 0.6 copy-start.3
  70.5 2.7 %collective-permute-start.2 = (f32[16,128]{1,0:T(8,128)}, f32[16,128]{1,0:T(8,128)S(1)}, u32[]{:S(2)}, u32[]{:S(2)}) collective-permute-start(f32[16,128]{1,0:T(8,128)} %get-tuple-element.28), channel_id=1, source_target_pairs={{0,1},{1,0},{2,3},{3,2},{4,5},{5,4},{6,7},{7,6},{8,9},{9,8},{10,11... | collective-permute-start | bytes 24584 | tf_op jit(solution)/shard_map/ppermute | solution.py:389
  73.2 0.6 copy-start.2
  111.5 1.0 copy-start

commit v3 on v2

v3 whole, which is shorter than its diff:
```python
import jax
import jax.numpy as jnp
from jax import lax
from jax.experimental import pallas as pl
from jax.experimental.pallas import tpu as pltpu
from jax.sharding import PartitionSpec as P

STEP = 0.08
MT_DEV = 8
CAP = 2
CAPT = 4
CLASSES = 16
CODE_ZERO = 4096.0
VMEM_LIMIT = 16 * 1024 * 1024

F32 = jnp.float32
BF16 = jnp.bfloat16
I32 = jnp.int32


def call(kernel, name, out_shape, scratch=(), smem=(), hbm_out=()):
    def run(*args):
        args = [
            x if i in smem else pltpu.with_memory_space_constraint(x, pltpu.VMEM)
            for i, x in enumerate(args)
        ]
        specs = [
            pl.BlockSpec(memory_space=pltpu.SMEM if i in smem else pltpu.VMEM)
            for i in range(len(args))
        ]
        flat, tree = jax.tree.flatten(out_shape)
        outs = [pl.BlockSpec(memory_space=pltpu.VMEM) for _ in flat]
        shapes = [
            s if i in hbm_out else pltpu.VMEM(s.shape, s.dtype) for i, s in enumerate(flat)
        ]
        return pl.pallas_call(
            kernel,
            out_shape=jax.tree.unflatten(tree, shapes),
            in_specs=specs,
            out_specs=jax.tree.unflatten(tree, outs),
            scratch_shapes=list(scratch),
            name=name,
            compiler_params=pltpu.CompilerParams(vmem_limit_bytes=VMEM_LIMIT),
        )(*args)

    return run


def sds(shape, dtype=F32):
    return jax.ShapeDtypeStruct(shape, dtype)


def iota(shape, dim):
    return lax.broadcasted_iota(I32, shape, dim)


def pieces(value):
    first = value.astype(BF16)
    rest = value - first.astype(F32)
    second = rest.astype(BF16)
    third = (rest - second.astype(F32)).astype(BF16)
    return first, second, third


def exact_dot(onehot, value):
    first, second, third = pieces(value)
    out = jnp.dot(onehot, third, preferred_element_type=F32)
    out = out + jnp.dot(onehot, second, preferred_element_type=F32)
    return out + jnp.dot(onehot, first, preferred_element_type=F32)


def as_column(row):
    size = row.shape[1]
    eye = iota((size, size), 0) == iota((size, size), 1)
    return jnp.sum(jnp.where(eye, row, 0), axis=1, keepdims=True)


def rank_row(keys):
    size = keys.shape[1]
    first, second = iota((size, size), 0), iota((size, size), 1)
    same = (as_column(keys) == keys) & (first < second)
    return jnp.sum(same.astype(F32), axis=0, keepdims=True)


def which_half():
    low = lax.axis_index("ap") == 0
    return low


def edge_lane(low, lanes):
    return jnp.where(low, lanes - 1, 0)


def put_face(held, plane, at, low):
    lanes = plane.shape[1]
    shift = lax.rem(at - edge_lane(low, lanes) + lanes, lanes)
    return jnp.where(iota(plane.shape, 1) == at, pltpu.roll(plane, shift, 1), held)


def take_face(held, at, low):
    lanes = held.shape[1]
    edge = edge_lane(low, lanes)
    shift = lax.rem(edge - at + lanes, lanes)
    return jnp.where(iota(held.shape, 1) == edge, pltpu.roll(held, shift, 1), 0.0)


def next_second(plane):
    rows = plane.shape[0]
    rolled = pltpu.roll(plane, rows - 1, 0)
    return jnp.where(iota(plane.shape, 0) == rows - 1, 0.0, rolled)


def next_depth(plane, halo):
    lanes = plane.shape[1]
    rolled = pltpu.roll(plane, lanes - 1, 1)
    return jnp.where(iota(plane.shape, 1) == lanes - 1, halo, rolled)


def sums(here, after, halo):
    return here, here + after, here + next_second(here), here + next_depth(here, halo), here + halo


def twice_operate(here, after, halo, before_flux, side_sums):
    buoy, along_x, along_y, along_z, low_z = side_sums
    flux = along_x * (after - here)
    total = flux - before_flux
    flux_y = along_y * (next_second(here) - here)
    under = jnp.where(iota(here.shape, 0) == 0, buoy * here, pltpu.roll(flux_y, 1, 0))
    total = total + (flux_y - under)
    flux_z = along_z * (next_depth(here, halo) - here)
    below = jnp.where(iota(here.shape, 1) == 0, low_z * (here - halo), pltpu.roll(flux_z, 1, 1))
    return total + (flux_z - below), flux


def following(x, count):
    return jnp.minimum(x + 1, count - 1), (x < count - 1).astype(F32)


def faces_kernel(now, buoy, bulk, nxt, out):
    low = which_half()
    count = now.shape[0]

    def body(x, held):
        held = put_face(held, now[x], x, low)
        held = put_face(held, buoy[x], 32 + x, low)
        return put_face(held, bulk[x] * nxt[x], 64 + x, low)

    out[...] = lax.fori_loop(0, count, body, jnp.zeros(now.shape[1:], F32), unroll=2)


def first_kernel(
    faces, now, prev, bulk, buoy, nxt, late, lap_out, mid_out, base_out, face_out
):
    low = which_half()
    count = now.shape[0]

    def body(x, carry):
        flux_v, flux_a, held = carry
        after, keep = following(x, count)
        side_sums = sums(buoy[x], keep * buoy[after], take_face(faces[...], 32 + x, low))
        here = now[x]
        lap, flux_v = twice_operate(
            here, keep * now[after], take_face(faces[...], x, low), flux_v, side_sums
        )
        lap = 0.5 * lap
        lap_out[x] = lap
        mid = 2.0 * here - prev[x] + (STEP * bulk[x]) * lap
        mid_out[x] = mid
        held = put_face(held, mid, x, low)
        scaled = bulk[x] * nxt[x]
        scaled_after = (keep * bulk[after]) * nxt[after]
        lap, flux_a = twice_operate(
            scaled, scaled_after, take_face(faces[...], 64 + x, low), flux_a, side_sums
        )
        base_out[x] = 2.0 * nxt[x] - late[x] + (0.5 * STEP) * lap
        return flux_v, flux_a, held

    start = (buoy[0] * now[0], buoy[0] * (bulk[0] * nxt[0]), jnp.zeros(now.shape[1:], F32))
    _, _, held = lax.fori_loop(0, count, body, start)
    face_out[...] = held


def second_kernel(faces, mid_face, mid, now, bulk, buoy, lap_out, end_out):
    low = which_half()
    count = now.shape[0]

    def body(x, flux):
        after, keep = following(x, count)
        side_sums = sums(buoy[x], keep * buoy[after], take_face(faces[...], 32 + x, low))
        here = mid[x]
        lap, flux = twice_operate(
            here, keep * mid[after], take_face(mid_face[...], x, low), flux, side_sums
        )
        lap = 0.5 * lap
        lap_out[x] = lap
        end_out[x] = 2.0 * here - now[x] + (STEP * bulk[x]) * lap
        return flux

    lax.fori_loop(0, count, body, buoy[0] * mid[0])


def pack_traces_kernel(groups, receivers, traces, out):
    keys = groups[...]
    place = keys.astype(F32) * CAP + rank_row(keys)
    slots = out.shape[0]
    count, samples = traces.shape
    chosen = (iota((slots, count), 0).astype(F32) == place).astype(F32).astype(BF16)
    ids = as_column(receivers[...].astype(F32))
    ids = jnp.where(iota((count, 128), 1) == 0, ids, 0.0).astype(BF16)
    out[:, :samples] = jnp.dot(chosen, traces[...], preferred_element_type=F32).astype(BF16)
    out[:, samples:] = jnp.dot(chosen, ids, preferred_element_type=F32).astype(BF16)


def places_kernel(
    at, cells, mid, end, owners, slots, seen_out, hot_depth_out, place_out, cls_out, spot_out,
    ids_out, rows_mid, rows_end,
):
    lanes = 128
    count = cells.shape[1]

    def body(r, carry):
        row = lax.shift_right_logical(at[0, r], 7)
        rows_mid[pl.ds(r, 1), :] = mid[pl.ds(row, 1), :]
        rows_end[pl.ds(r, 1), :] = end[pl.ds(row, 1), :]
        return carry

    lax.fori_loop(0, count, body, 0, unroll=8)
    cell_col = as_column(cells[...])
    here = iota((count, lanes), 1) == (cell_col & (lanes - 1))
    hot_depth_out[...] = here.astype(F32)
    seen_mid = jnp.sum(jnp.where(here, rows_mid[...], 0.0), axis=1, keepdims=True)
    seen_end = jnp.sum(jnp.where(here, rows_end[...], 0.0), axis=1, keepdims=True)
    seen_out[...] = jnp.where(iota((count, lanes), 1) == 0, seen_mid, seen_end)

    owner = owners[...]
    tiles = owner.shape[1]
    rank = rank_row(owner).astype(I32)
    cls = owner & (CLASSES - 1)
    spot = lax.shift_right_logical(owner, 4) * CAPT + rank
    per_class = 8 * CAPT
    place_out[...] = cls * (per_class + 1) + spot
    cls_hot = (iota((CLASSES, tiles), 0) == cls).astype(F32).astype(BF16)
    cls_out[...] = cls_hot
    spot_hot = (iota((tiles, lanes), 1) == as_column(spot)).astype(F32)
    spot_out[...] = spot_hot
    slot_col = as_column(slots[...]).astype(F32)
    ids_out[...] = jnp.dot(
        cls_hot, (spot_hot * slot_col).astype(BF16), preferred_element_type=F32
    )


def inject_kernel(
    at, rows_in, filters, seen, hot_depth, base, bulk, mid_out, add_out, face_out, sum_mid, sum_end
):
    low = which_half()
    samples = filters.shape[1]
    count, lanes = hot_depth.shape
    slots = rows_in.shape[0]
    last_dims = (((1,), (1,)), ((), ()))
    values = lax.dot_general(
        rows_in[:, :samples], filters[...], last_dims, preferred_element_type=F32
    )
    pick = ((iota((8, 128), 0) == 0) & (iota((8, 128), 1) == 0)).astype(F32).astype(BF16)
    ids = lax.dot_general(pick, rows_in[:, samples:], last_dims, preferred_element_type=F32)
    hot = (iota((count, slots), 0).astype(F32) == ids[0:1, :]).astype(F32).astype(BF16)
    observed = exact_dot(hot, values)
    sum_mid[...] = hot_depth[...] * (seen[:, 0:1] - observed[:, 0:1])
    sum_end[...] = hot_depth[...] * (seen[:, 1:2] - observed[:, 1:2])
    mid_out[...] = base[...]
    add_out[...] = jnp.zeros_like(add_out)

    def body(r, carry):
        row = lax.shift_right_logical(at[0, r], 7)
        mid_out[pl.ds(row, 1), :] = mid_out[pl.ds(row, 1), :] + sum_end[pl.ds(r, 1), :]
        add_out[pl.ds(row, 1), :] = add_out[pl.ds(row, 1), :] + sum_mid[pl.ds(r, 1), :]
        return carry

    lax.fori_loop(0, count, body, 0, unroll=8)
    rows = bulk.shape[1]

    def edge(x, held):
        field = mid_out[pl.ds(pl.multiple_of(x * rows, rows), rows), :]
        return put_face(held, bulk[x] * field, x, low)

    face_out[...] = lax.fori_loop(
        0, bulk.shape[0], edge, jnp.zeros(bulk.shape[1:], F32), unroll=2
    )


def image_kernel(
    faces, adj_face, mid, add, nxt, bulk, buoy, lap_mid, lap_now, place, cls_hot, spot_hot, ids,
    last_out, send_out, codes,
):
    low = which_half()
    count, rows, lanes = mid.shape
    tiles = rows // 8
    per_class = send_out.shape[0] // CLASSES

    def clear(c, carry):
        send_out[pl.ds(c * per_class, per_class)] = jnp.zeros((per_class, 8, lanes), jnp.int16)
        return carry

    lax.fori_loop(0, CLASSES, clear, 0)

    def body(x, flux):
        after, keep = following(x, count)
        side_sums = sums(buoy[x], keep * buoy[after], take_face(faces[...], 32 + x, low))
        here = mid[x]
        lap, flux = twice_operate(
            bulk[x] * here,
            (keep * bulk[after]) * mid[after],
            take_face(adj_face[...], x, low),
            flux,
            side_sums,
        )
        end = 2.0 * here - nxt[x] + (0.5 * STEP) * lap + add[x]
        last_out[x] = end
        image = (STEP * (here * lap_mid[x] + end * lap_now[x])).reshape(tiles, 8, lanes)
        peak = jnp.max(jnp.max(jnp.abs(image), axis=1), axis=1, keepdims=True)
        code = jnp.ceil(16.0 * jnp.log2(jnp.maximum(peak, 1e-30))) + 1.0
        codes[pl.ds(pl.multiple_of(x * tiles, tiles), tiles), :] = jnp.broadcast_to(
            code + CODE_ZERO, (tiles, lanes)
        )
        gain = jnp.broadcast_to(32767.0 * jnp.exp2(code * (-1.0 / 16.0)), (tiles, lanes))
        whole = jnp.round(image * gain[:, None, :]).astype(I32).astype(jnp.int16)
        for t in range(tiles):
            send_out[place[0, x * tiles + t]] = whole[t]
        return flux

    lax.fori_loop(0, count, body, buoy[0] * (bulk[0] * mid[0]))
    code = codes[...]
    upper = jnp.floor(code * (1.0 / 64.0))
    lower = code - 64.0 * upper
    hot = cls_hot[...]
    spread = spot_hot[...]
    sent = 64.0 * jnp.dot(hot, (spread * upper).astype(BF16), preferred_element_type=F32)
    sent = sent + jnp.dot(hot, (spread * lower).astype(BF16), preferred_element_type=F32)
    place_row = iota((8, lanes), 0)
    for c in range(CLASSES):
        tile = jnp.where(
            place_row == 0,
            ids[c : c + 1, :],
            jnp.where(place_row == 1, sent[c : c + 1, :], 0.0),
        )
        send_out[c * per_class + per_class - 1] = tile.astype(I32).astype(jnp.int16)


def combine_kernel(got, out, gains_v, slots_v, gains, slots, sems, *partial):
    per_class = got.shape[0] // CLASSES
    used = per_class - 1
    lanes = got.shape[2]
    for c in range(CLASSES):
        meta = got[c * per_class + used].astype(I32)
        slots_v[c : c + 1, :] = meta[0:1, :]
        code = meta[1:2, :].astype(F32)
        gain = jnp.exp2((code - CODE_ZERO) * (1.0 / 16.0)) * (1.0 / 32767.0)
        gains_v[c : c + 1, :] = jnp.where(code > 0, gain, 0.0)
    copies = [
        pltpu.make_async_copy(gains_v, gains, sems.at[0]),
        pltpu.make_async_copy(slots_v, slots, sems.at[1]),
    ]
    for copy in copies:
        copy.start()
    for part in partial:
        part[...] = jnp.zeros_like(part)
    for copy in copies:
        copy.wait()

    def body(src, carry):
        for s in range(used):
            part = partial[s % CAPT]
            at = (s // CAPT) * MT_DEV + slots[src, s]
            value = got[src * per_class + s].astype(I32).astype(F32) * gains[src, s]
            part[at] = part[at] + value
        return carry

    lax.fori_loop(0, CLASSES, body, 0)
    total = partial[0][...]
    for part in partial[1:]:
        total = total + part[...]
    out[...] = total


def swap(face):
    return lax.ppermute(face, "ap", [(0, 1), (1, 0)])


def local(
    wave_prev,
    wave_now,
    adjoint_late,
    adjoint_next,
    bulk,
    buoyancy,
    traces,
    group_filter,
    trace_group,
    trace_receiver,
    receiver_cell,
    tile_owner,
    tile_slot,
):
    shots = lax.axis_size("shot")
    rings = shots // CLASSES
    prev, now, late, nxt = wave_prev[0], wave_now[0], adjoint_late[0], adjoint_next[0]
    bulk, buoy = bulk[0], buoyancy[0]
    count, rows, lanes = now.shape
    field = sds(now.shape)
    flat = sds((count * rows, lanes))
    samples = traces.shape[1]
    face = sds((rows, lanes))

    packed = call(pack_traces_kernel, "pack_traces", sds((shots * CAP, samples + 128), BF16))(
        trace_group.reshape(1, -1), trace_receiver.reshape(1, -1), traces
    )
    got_rows = lax.all_to_all(
        packed.reshape(shots, CAP, samples + 128), "shot", split_axis=0, concat_axis=0, tiled=True
    ).reshape(shots * CAP, samples + 128)

    faces = swap(call(faces_kernel, "faces", face)(now, buoy, bulk, nxt))
    lap_now, wave_mid, adj_base, mid_face = call(
        first_kernel, "first_step", (field, field, field, face)
    )(faces, now, prev, bulk, buoy, nxt, late)
    lap_mid, wave_end = call(second_kernel, "second_step", (field, field))(
        faces, swap(mid_face), wave_mid, now, bulk, buoy
    )
    receivers = receiver_cell.shape[1]
    tiles = tile_owner.shape[0]
    per_receiver = pltpu.VMEM((receivers, lanes), F32)
    seen, hot_depth, place, cls_hot, spot_hot, ids = call(
        places_kernel,
        "places",
        (
            sds((receivers, lanes)),
            sds((receivers, lanes)),
            sds((1, tiles), I32),
            sds((CLASSES, tiles), BF16),
            sds((tiles, lanes)),
            sds((CLASSES, lanes)),
        ),
        [per_receiver, per_receiver],
        smem=(0,),
        hbm_out=(2,),
    )(
        receiver_cell,
        receiver_cell,
        wave_mid.reshape(flat.shape),
        wave_end.reshape(flat.shape),
        tile_owner.reshape(1, -1),
        tile_slot.reshape(1, -1),
    )
    filters = jnp.pad(group_filter[0], ((0, 14), (0, 0)))
    adj_mid, adj_add, adj_face = call(
        inject_kernel, "inject", (flat, flat, face), [per_receiver, per_receiver], smem=(0,)
    )(receiver_cell, got_rows, filters, seen, hot_depth, adj_base.reshape(flat.shape), bulk)
    per_class = (shots // CLASSES) * CAPT + 1
    adj_end, send = call(
        image_kernel,
        "image",
        (field, sds((CLASSES * per_class, 8, lanes), jnp.int16)),
        [pltpu.VMEM((tiles, lanes), F32)],
        smem=(9,),
    )(
        faces, swap(adj_face), adj_mid.reshape(now.shape), adj_add.reshape(now.shape), nxt, bulk,
        buoy, lap_mid, lap_now, place, cls_hot, spot_hot, ids,
    )
    near = [[r * CLASSES + c for c in range(CLASSES)] for r in range(rings)]
    far = [[r * CLASSES + c for r in range(rings)] for c in range(CLASSES)]
    got = lax.all_to_all(
        send.reshape(CLASSES, per_class * 8, lanes),
        "shot",
        split_axis=0,
        concat_axis=0,
        axis_index_groups=near,
        tiled=True,
    )
    owned = rings * MT_DEV
    table = (CLASSES, lanes)
    dense = call(
        combine_kernel,
        "combine",
        sds((owned, 8, lanes)),
        [
            pltpu.VMEM(table, F32),
            pltpu.VMEM(table, I32),
            pltpu.SMEM(table, F32),
            pltpu.SMEM(table, I32),
            pltpu.SemaphoreType.DMA((2,)),
        ]
        + [pltpu.VMEM((owned, 8, lanes), F32)] * CAPT,
    )(got.reshape(CLASSES * per_class, 8, lanes))
    shared = lax.all_to_all(
        dense.reshape(rings, MT_DEV * 8, lanes),
        "shot",
        split_axis=0,
        concat_axis=0,
        axis_index_groups=far,
        tiled=True,
    )
    model_grad = jnp.sum(shared, axis=0).reshape(MT_DEV, 8, lanes)
    return (model_grad, wave_end[None], adj_end[None])


def solution(mesh):
    placed = (
        P("shot", None, None, "ap"),
        P("shot", None, None, "ap"),
        P("shot", None, None, "ap"),
        P("shot", None, None, "ap"),
        P("shot", None, None, "ap"),
        P("shot", None, None, "ap"),
        P(("shot", "ap"), None),
        P("shot", None, None),
        P(("shot", "ap"), None),
        P(("shot", "ap")),
        P("shot", "ap"),
        P("shot", None),
        P("shot"),
    )
    return jax.shard_map(
        local,
        mesh=mesh,
        in_specs=placed,
        out_specs=(P("shot", None, "ap"), P("shot", None, None, "ap"), P("shot", None, None, "ap")),
        check_vma=False,
    )
```

time: 135 us -> 122 us (0.904)
  blocking collectives: 45.6 us -> 24.5 us
  Pallas kernels: 54 us -> 34.4 us
  waiting for transfers between devices: 8.64 us -> 21 us
  local copies, waits for them, and re-layouts: 6.98 us -> 15.1 us
  starting transfers between devices: 16.8 us -> 24.8 us
    pallas_call x8, Pallas kernels: 54 us -> 34.4 us  [run(): pl.pallas_call(kernel, out_shape=jax.tree.unflatten(tree, shapes), in_spe...]
    all_to_all x1 -> x0, blocking collectives: 17.5 us -> none  [local(): lax.all_to_all(dense.reshape(rings, MT_DEV * 8, lanes), 'shot', split_axi...]
    all_to_all x0 -> x1, waiting for transfers between devices: none -> 9.04 us  [local(): lax.all_to_all(dense.reshape(rings, MT_DEV * 8, lanes), 'shot', split_axi...]
    unnamed x10 -> x54, local copies, waits for them, and re-layouts: 2.65 us -> 11.6 us
    all_to_all x0 -> x1, starting transfers between devices: none -> 6.51 us  [local(): lax.all_to_all(dense.reshape(rings, MT_DEV * 8, lanes), 'shot', split_axi...]
    all_to_all x1, blocking collectives: 28.2 us -> 24.5 us  [local(): lax.all_to_all(send.reshape(CLASSES, per_class * 8, lanes), 'shot', split...]
    all_to_all x1, waiting for transfers between devices: 0.01 us -> 3.55 us  [local(): lax.all_to_all(packed.reshape(shots, CAP, samples + 128), 'shot', split_a...]
  transfers between devices with their start and end apart: 4 -> 5, of which waited for: 3 -> 5; matrix products, arithmetic and copies ran while one was open for 0% -> 2% of each run, Pallas kernels for 21% -> 14%
where the time goes in v3:
time: 122 us; the launch traced here: 121 us
  Pallas kernels  34.4 us (28%)
  starting transfers between devices  24.8 us (20%)
  blocking collectives  24.5 us (20%)
  waiting for transfers between devices  21 us (17%)
  local copies, waits for them, and re-layouts  15.1 us (12%)
    pallas_call x8, Pallas kernels, run(): pl.pallas_call(kernel, out_shape=jax.tree.unflatten(tree, shapes), in_spe...  34.4 us
    all_to_all x1, blocking collectives, local(): lax.all_to_all(send.reshape(CLASSES, per_class * 8, lanes), 'shot', split...  24.5 us
    all_to_all x1, starting transfers between devices, local(): lax.all_to_all(packed.reshape(shots, CAP, samples + 128), 'shot', split_a...  16.9 us
    unnamed x54, local copies, waits for them, and re-layouts  11.6 us
    all_to_all x1, waiting for transfers between devices, local(): lax.all_to_all(dense.reshape(rings, MT_DEV * 8, lanes), 'shot', split_axi...  9.04 us
    ppermute x3, waiting for transfers between devices, swap(): return lax.ppermute(face, 'ap', [(0, 1), (1, 0)])  8.39 us
    all_to_all x1, starting transfers between devices, local(): lax.all_to_all(dense.reshape(rings, MT_DEV * 8, lanes), 'shot', split_axi...  6.51 us
    all_to_all x1, waiting for transfers between devices, local(): lax.all_to_all(packed.reshape(shots, CAP, samples + 128), 'shot', split_a...  3.55 us
  transfers between devices with their start and end apart: 5, of which 5 were waited for; matrix products, arithmetic and copies ran while one was open for 2% of the time, Pallas kernels for 14%

profile of v3, /device:TPU:1, one launch (start us, length us, event | category | flops | bytes accessed | tf_op | source)
XLA Modules:
  0.0 121.3 jit_solution(17974506173091159495)
XLA Ops:
  0.6 1.0 copy-done.17
  1.7 0.7 copy-done.23
  2.3 0.7 copy-done.24
  3.0 0.6 pack_traces.1
  3.6 1.3 %reshape.53 = bf16[128,2,2176]{2,1,0:T(2,128)(2,1)} reshape(bf16[256,2176]{1,0:T(8,128)(2,1)S(1)} %pack_traces.1) | data formatting | bytes 2228224 | tf_op jit(solution)/shard_map/reshape | solution.py:417
  4.8 16.9 %all-to-all-start = ((bf16[128,2,2176]{2,1,0:T(2,128)(2,1)}), bf16[128,2,2176]{2,1,0:T(2,128)(2,1)}, u32[]{:S(2)}, u32[]{:S(2)}) async-start(bf16[128,2,2176]{2,1,0:T(2,128)(2,1)} %reshape.53), calls=%async_computation | async-start | bytes 2228224 | tf_op jit(solution)/shard_map/all_to_all | solution.py:416
  21.8 1.2 %copy-done.5 = f32[1,32,64,128]{3,2,1,0:T(8,128)S(1)} copy-done((f32[1,32,64,128]{3,2,1,0:T(8,128)S(1)}, f32[1,32,64,128]{3,2,1,0:T(8,128)}, u32[]{:S(2)}) %copy-start.5) | copy-done | bytes 1048600
  23.0 1.9 %faces.1 = f32[64,128]{1,0:T(8,128)S(1)} custom-call(f32[32,64,128]{2,1,0:T(8,128)S(1)} %bitcast.34, f32[32,64,128]{2,1,0:T(8,128)S(1)} %bitcast.30, f32[32,64,128]{2,1,0:T(8,128)S(1)} %bitcast.25, f32[32,64,128]{2,1,0:T(8,128)S(1)} %bitcast.37), custom_call_target="tpu_custom_call" | custom-call | tf_op jit(solution)/shard_map/faces/pallas_call | solution.py:36
  24.9 0.5 collective-permute-start
  25.4 3.0 %collective-permute-done.faces = f32[64,128]{1,0:T(8,128)S(1)} collective-permute-done((f32[64,128]{1,0:T(8,128)S(1)}, f32[64,128]{1,0:T(8,128)S(1)}, u32[]{:S(2)}, u32[]{:S(2)}) %collective-permute-start) | collective-permute-done | bytes 32800 | tf_op jit(solution)/shard_map/ppermute | solution.py:385
  28.4 8.0 %first_step.1 = (f32[32,64,128]{2,1,0:T(8,128)S(1)}, f32[32,64,128]{2,1,0:T(8,128)S(1)}, f32[32,64,128]{2,1,0:T(8,128)S(1)}, f32[64,128]{1,0:T(8,128)S(1)}) custom-call(f32[64,128]{1,0:T(8,128)S(1)} %collective-permute-done.faces, f32[32,64,128]{2,1,0:T(8,128)S(1)} %bitcast.35, f32[32,64,128]{2,1,0:T(8,128)S(1)} %bitcast.43, f32[32,64,128]{2,1,0:T(8,128)S(1)} %bitcast.26, ...), custom_call_target="tpu_custom_call" | custom-call | tf_op jit(solution)/shard_map/first_step/pallas_call | solution.py:36
  36.5 1.0 copy-done.11
  37.9 3.0 %collective-permute-done.1.mid_face = f32[64,128]{1,0:T(8,128)S(1)} collective-permute-done((f32[64,128]{1,0:T(8,128)S(1)}, f32[64,128]{1,0:T(8,128)S(1)}, u32[]{:S(2)}, u32[]{:S(2)}) %collective-permute-start.1) | collective-permute-done | bytes 32800 | tf_op jit(solution)/shard_map/ppermute | solution.py:385
  40.9 5.7 %second_step.1 = (f32[32,64,128]{2,1,0:T(8,128)S(1)}, f32[32,64,128]{2,1,0:T(8,128)S(1)}) custom-call(f32[64,128]{1,0:T(8,128)S(1)} %collective-permute-done.faces, f32[64,128]{1,0:T(8,128)S(1)} %collective-permute-done.1.mid_face, f32[32,64,128]{2,1,0:T(8,128)S(1)} %get-tuple-element.20.mid, f32[32,64,128]{2,1,0:T(8,128)S(1)} %bitcast.36, ...), custom_call_target="tpu_custom_call" | custom-call | tf_op jit(solution)/shard_map/second_step/pallas_call | solution.py:36
  46.7 1.0 copy-done.13
  47.7 1.6 %places.1 = (f32[256,128]{1,0:T(8,128)S(1)}, f32[256,128]{1,0:T(8,128)S(1)}, s32[1,256]{1,0:T(1,128)S(1)}, bf16[16,256]{1,0:T(8,128)(2,1)S(1)}, f32[256,128]{1,0:T(8,128)S(1)}, /*index=5*/f32[16,128]{1,0:T(8,128)S(1)}) custom-call(s32[1,256]{1,0:T(1,128)S(1)} %copy-done.20, s32[1,256]{1,0:T(1,128)S(1)} %copy-done.20, f32[2048,128]{1,0:T(8,128)S(1)} %bitcast.41, ...), custom_call_target="tpu_custom_call" | custom-call | tf_op jit(solution)/shard_map/places/pallas_call | solution.py:36
  49.3 0.7 copy-done.18
  49.9 3.6 %all-to-all-done = bf16[128,2,2176]{2,1,0:T(2,128)(2,1)} async-done(((bf16[128,2,2176]{2,1,0:T(2,128)(2,1)}), bf16[128,2,2176]{2,1,0:T(2,128)(2,1)}, u32[]{:S(2)}, u32[]{:S(2)}) %all-to-all-start) | async-done | bytes 1114144 | tf_op jit(solution)/shard_map/all_to_all | solution.py:416
  53.5 2.3 %reshape.54.rows_in = bf16[256,2176]{1,0:T(8,128)(2,1)} reshape(bf16[128,2,2176]{2,1,0:T(2,128)(2,1)} %all-to-all-done) | data formatting | bytes 2228224 | tf_op jit(solution)/shard_map/reshape | solution.py:418
  55.8 1.2 %copy-done.8 = bf16[256,2176]{1,0:T(8,128)(2,1)S(1)} copy-done((bf16[256,2176]{1,0:T(8,128)(2,1)S(1)}, bf16[256,2176]{1,0:T(8,128)(2,1)}, u32[]{:S(2)}) %copy-start.8) | copy-done | bytes 1114136
  57.0 0.9 copy-done.19
  57.9 3.9 %inject.1 = (f32[2048,128]{1,0:T(8,128)S(1)}, f32[2048,128]{1,0:T(8,128)S(1)}, f32[64,128]{1,0:T(8,128)S(1)}) custom-call(s32[1,256]{1,0:T(1,128)S(1)} %copy-done.20, bf16[256,2176]{1,0:T(8,128)(2,1)S(1)} %copy-done.8, bf16[16,2048]{1,0:T(8,128)(2,1)S(1)} %pad.4.filters, f32[256,128]{1,0:T(8,128)S(1)} %get-tuple-element.23.seen, f32[256,128]{1,0:T(8,128)S(1)} %copy-done.19, ...), custom_call_target="tpu_custom_call" | custom-call | tf_op jit(solution)/shard_map/inject/pallas_call | solution.py:36
  62.3 2.4 %collective-permute-done.2.adj_face = f32[64,128]{1,0:T(8,128)S(1)} collective-permute-done((f32[64,128]{1,0:T(8,128)S(1)}, f32[64,128]{1,0:T(8,128)S(1)}, u32[]{:S(2)}, u32[]{:S(2)}) %collective-permute-start.2) | collective-permute-done | bytes 32800 | tf_op jit(solution)/shard_map/ppermute | solution.py:385
  64.7 1.2 %copy-done.14 = f32[32,64,128]{2,1,0:T(8,128)S(1)} copy-done((f32[32,64,128]{2,1,0:T(8,128)S(1)}, f32[32,64,128]{2,1,0:T(8,128)}, u32[]{:S(2)}) %copy-start.14) | copy-done | bytes 1048600
  65.9 10.3 %image.1 = (f32[32,64,128]{2,1,0:T(8,128)S(1)}, s16[528,8,128]{2,1,0:T(8,128)(2,1)S(1)}) custom-call(f32[64,128]{1,0:T(8,128)S(1)} %collective-permute-done.faces, f32[64,128]{1,0:T(8,128)S(1)} %collective-permute-done.2.adj_face, f32[32,64,128]{2,1,0:T(8,128)S(1)} %bitcast.46, f32[32,64,128]{2,1,0:T(8,128)S(1)} %bitcast.47, f32[32,64,128]{2,1,0:T(8,128)S(1)} %bitcast.39, ...), custom_call_target="tpu_custom_call" | custom-call | tf_op jit(solution)/shard_map/image/pallas_call | solution.py:36
  76.2 24.5 %all_to_all.15 = s16[16,264,128]{2,1,0:T(8,128)(2,1)S(1)} all-to-all(s16[16,264,128]{2,1,0:T(8,128)(2,1)S(1)} %bitcast.42), channel_id=1, replica_groups={{0,2,4,6,8,10,12,14,16,18,20,22,24,26,28,30},{32,34,36,38,40,42,44,46,4..., dimensions={0} | all-to-all | bytes 2162688 | tf_op jit(solution)/shard_map/all_to_all | solution.py:469
  100.8 2.4 %combine.1 = f32[64,8,128]{2,1,0:T(8,128)} custom-call(s16[528,8,128]{2,1,0:T(8,128)(2,1)S(1)} %bitcast.40), custom_call_target="tpu_custom_call" | custom-call | tf_op jit(solution)/shard_map/combine/pallas_call | solution.py:36
  103.2 6.5 %all-to-all-start.2 = ((f32[8,64,128]{2,1,0:T(8,128)}), f32[8,64,128]{2,1,0:T(8,128)S(1)}, u32[]{:S(2)}, u32[]{:S(2)}) async-start(f32[8,64,128]{2,1,0:T(8,128)} %bitcast.18), calls=%async_computation.2 | async-start | bytes 524288 | tf_op jit(solution)/shard_map/all_to_all | solution.py:492
  109.7 1.0 copy.16
  110.7 1.0 copy.17
  111.6 9.0 %all-to-all-done.2 = f32[8,64,128]{2,1,0:T(8,128)S(1)} async-done(((f32[8,64,128]{2,1,0:T(8,128)}), f32[8,64,128]{2,1,0:T(8,128)S(1)}, u32[]{:S(2)}, u32[]{:S(2)}) %all-to-all-start.2) | async-done | bytes 262176 | tf_op jit(solution)/shard_map/all_to_all | solution.py:492
  120.7 0.6 reduce_sum.9
  (45 shorter events, 0.9 us)
Async XLA Ops:
  0.6 1.0 copy-start.17
  1.7 0.7 copy-start.23
  2.3 0.7 copy-start.24
  3.5 18.2 %copy-start.3 = (f32[1,32,64,128]{3,2,1,0:T(8,128)S(1)}, f32[1,32,64,128]{3,2,1,0:T(8,128)}, u32[]{:S(2)}) copy-start(f32[1,32,64,128]{3,2,1,0:T(8,128)} %param.14) | copy-start | bytes 3145732
  4.8 17.0 %copy-start = (f32[1,32,64,128]{3,2,1,0:T(8,128)S(1)}, f32[1,32,64,128]{3,2,1,0:T(8,128)}, u32[]{:S(2)}) copy-start(f32[1,32,64,128]{3,2,1,0:T(8,128)} %param.17) | copy-start | bytes 3145732
  4.8 17.0 %copy-start.1 = (f32[1,32,64,128]{3,2,1,0:T(8,128)S(1)}, f32[1,32,64,128]{3,2,1,0:T(8,128)}, u32[]{:S(2)}) copy-start(f32[1,32,64,128]{3,2,1,0:T(8,128)} %param.18) | copy-start | bytes 3145732
  4.8 48.6 %all-to-all-start = ((bf16[128,2,2176]{2,1,0:T(2,128)(2,1)}), bf16[128,2,2176]{2,1,0:T(2,128)(2,1)}, u32[]{:S(2)}, u32[]{:S(2)}) async-start(bf16[128,2,2176]{2,1,0:T(2,128)(2,1)} %reshape.53), calls=%async_computation | async-start | bytes 2228224 | tf_op jit(solution)/shard_map/all_to_all | solution.py:416
  21.8 1.2 %copy-start.5 = (f32[1,32,64,128]{3,2,1,0:T(8,128)S(1)}, f32[1,32,64,128]{3,2,1,0:T(8,128)}, u32[]{:S(2)}) copy-start(f32[1,32,64,128]{3,2,1,0:T(8,128)} %param.16) | copy-start | bytes 3145732
  23.0 5.4 %copy-start.6 = (f32[1,32,64,128]{3,2,1,0:T(8,128)S(1)}, f32[1,32,64,128]{3,2,1,0:T(8,128)}, u32[]{:S(2)}) copy-start(f32[1,32,64,128]{3,2,1,0:T(8,128)} %param.16) | copy-start | bytes 3145732
  23.0 5.4 %copy-start.9 = (f32[1,32,64,128]{3,2,1,0:T(8,128)S(1)}, f32[1,32,64,128]{3,2,1,0:T(8,128)}, u32[]{:S(2)}) copy-start(f32[1,32,64,128]{3,2,1,0:T(8,128)} %param.13) | copy-start | bytes 3145732
  23.0 5.4 %copy-start.10 = (f32[1,32,64,128]{3,2,1,0:T(8,128)S(1)}, f32[1,32,64,128]{3,2,1,0:T(8,128)}, u32[]{:S(2)}) copy-start(f32[1,32,64,128]{3,2,1,0:T(8,128)} %param.15) | copy-start | bytes 3145732
  24.9 3.5 %collective-permute-start = (f32[64,128]{1,0:T(8,128)S(1)}, f32[64,128]{1,0:T(8,128)S(1)}, u32[]{:S(2)}, u32[]{:S(2)}) collective-permute-start(f32[64,128]{1,0:T(8,128)S(1)} %faces.1), channel_id=1, source_target_pairs={{0,1},{1,0},{2,3},{3,2},{4,5},{5,4},{6,7},{7,6},{8,9},{9,8},{10,11... | collective-permute-start | bytes 98312 | tf_op jit(solution)/shard_map/ppermute | solution.py:385
  28.4 9.4 %copy-start.25 = (bf16[1,2,2048]{2,1,0:T(2,128)(2,1)S(1)}, bf16[1,2,2048]{2,1,0:T(2,128)(2,1)}, u32[]{:S(2)}) copy-start(bf16[1,2,2048]{2,1,0:T(2,128)(2,1)} %param.20) | copy-start | bytes 24580
  28.4 12.5 %copy-start.4 = (f32[1,32,64,128]{3,2,1,0:T(8,128)S(1)}, f32[1,32,64,128]{3,2,1,0:T(8,128)}, u32[]{:S(2)}) copy-start(f32[1,32,64,128]{3,2,1,0:T(8,128)} %param.14) | copy-start | bytes 3145732
  36.5 1.0 copy-start.11
  37.5 9.2 %copy-start.15 = (f32[32,64,128]{2,1,0:T(8,128)}, f32[32,64,128]{2,1,0:T(8,128)S(1)}, u32[]{:S(2)}) copy-start(f32[32,64,128]{2,1,0:T(8,128)S(1)} %get-tuple-element.25) | copy-start | bytes 3145732
  37.5 3.4 %collective-permute-start.1 = (f32[64,128]{1,0:T(8,128)S(1)}, f32[64,128]{1,0:T(8,128)S(1)}, u32[]{:S(2)}, u32[]{:S(2)}) collective-permute-start(f32[64,128]{1,0:T(8,128)S(1)} %get-tuple-element.21), channel_id=1, source_target_pairs={{0,1},{1,0},{2,3},{3,2},{4,5},{5,4},{6,7},{7,6},{8,9},{9,8},{10,11... | collective-permute-start | bytes 98312 | tf_op jit(solution)/shard_map/ppermute | solution.py:385
  40.9 6.7 %copy-start.20 = (s32[1,256]{1,0:T(1,128)S(1)}, s32[1,256]{1,0:T(1,128)}, u32[]{:S(2)}) copy-start(s32[1,256]{1,0:T(1,128)} %at.3) | copy-start | bytes 3076
  40.9 6.7 %copy-start.21 = (s32[256,1]{0,1:T(1,128)S(1)}, s32[256,1]{0,1:T(1,128)}, u32[]{:S(2)}) copy-start(s32[256,1]{0,1:T(1,128)} %param.24) | copy-start | bytes 3076
  40.9 6.7 %copy-start.22 = (s32[256]{0:T(256)S(1)}, s32[256]{0:T(256)}, u32[]{:S(2)}) copy-start(s32[256]{0:T(256)} %param.25) | copy-start | bytes 3076
  46.7 1.0 copy-start.13
  49.3 0.7 copy-start.18
  49.9 5.8 %copy-start.16 = (f32[32,64,128]{2,1,0:T(8,128)S(1)}, f32[32,64,128]{2,1,0:T(8,128)}, u32[]{:S(2)}) copy-start(f32[32,64,128]{2,1,0:T(8,128)} %copy-done.15) | copy-start | bytes 3145732
  55.8 1.2 %copy-start.8 = (bf16[256,2176]{1,0:T(8,128)(2,1)S(1)}, bf16[256,2176]{1,0:T(8,128)(2,1)}, u32[]{:S(2)}) copy-start(bf16[256,2176]{1,0:T(8,128)(2,1)} %reshape.54.rows_in) | copy-start | bytes 3342340
  57.0 0.9 copy-start.19
  57.9 6.8 %copy-start.2 = (f32[1,32,64,128]{3,2,1,0:T(8,128)S(1)}, f32[1,32,64,128]{3,2,1,0:T(8,128)}, u32[]{:S(2)}) copy-start(f32[1,32,64,128]{3,2,1,0:T(8,128)} %param.18) | copy-start | bytes 3145732
  57.9 6.8 %copy-start.7 = (f32[1,32,64,128]{3,2,1,0:T(8,128)S(1)}, f32[1,32,64,128]{3,2,1,0:T(8,128)}, u32[]{:S(2)}) copy-start(f32[1,32,64,128]{3,2,1,0:T(8,128)} %param.16) | copy-start | bytes 3145732
  57.9 6.8 %copy-start.12 = (f32[32,64,128]{2,1,0:T(8,128)S(1)}, f32[32,64,128]{2,1,0:T(8,128)}, u32[]{:S(2)}) copy-start(f32[32,64,128]{2,1,0:T(8,128)} %copy-done.11) | copy-start | bytes 3145732
  61.8 2.9 %collective-permute-start.2 = (f32[64,128]{1,0:T(8,128)S(1)}, f32[64,128]{1,0:T(8,128)S(1)}, u32[]{:S(2)}, u32[]{:S(2)}) collective-permute-start(f32[64,128]{1,0:T(8,128)S(1)} %get-tuple-element.26), channel_id=1, source_target_pairs={{0,1},{1,0},{2,3},{3,2},{4,5},{5,4},{6,7},{7,6},{8,9},{9,8},{10,11... | collective-permute-start | bytes 98312 | tf_op jit(solution)/shard_map/ppermute | solution.py:385
  64.7 1.2 %copy-start.14 = (f32[32,64,128]{2,1,0:T(8,128)S(1)}, f32[32,64,128]{2,1,0:T(8,128)}, u32[]{:S(2)}) copy-start(f32[32,64,128]{2,1,0:T(8,128)} %copy-done.13) | copy-start | bytes 3145732
  103.2 17.5 %all-to-all-start.2 = ((f32[8,64,128]{2,1,0:T(8,128)}), f32[8,64,128]{2,1,0:T(8,128)S(1)}, u32[]{:S(2)}, u32[]{:S(2)}) async-start(f32[8,64,128]{2,1,0:T(8,128)} %bitcast.18), calls=%async_computation.2 | async-start | bytes 524288 | tf_op jit(solution)/shard_map/all_to_all | solution.py:492

commit v4 on v3

--- a/solution.py
+++ b/solution.py
@@ -11,27 +11,31 @@
 CAPT = 4
 CLASSES = 16
 CODE_ZERO = 4096.0
-VMEM_LIMIT = 16 * 1024 * 1024
+VMEM_LIMIT = 6 * 1024 * 1024
 
 F32 = jnp.float32
 BF16 = jnp.bfloat16
 I32 = jnp.int32
 
 
-def call(kernel, name, out_shape, scratch=(), smem=(), hbm_out=()):
+def call(kernel, name, out_shape, scratch=(), smem=(), hbm_out=(), free=(), hbm=()):
     def run(*args):
-        args = [
-            x if i in smem else pltpu.with_memory_space_constraint(x, pltpu.VMEM)
-            for i, x in enumerate(args)
-        ]
-        specs = [
-            pl.BlockSpec(memory_space=pltpu.SMEM if i in smem else pltpu.VMEM)
+        spaces = [
+            pltpu.SMEM if i in smem else pltpu.HBM if i in hbm else pltpu.VMEM
             for i in range(len(args))
         ]
+        args = [
+            pltpu.with_memory_space_constraint(x, space)
+            if space is not pltpu.SMEM and i not in free
+            else x
+            for i, (x, space) in enumerate(zip(args, spaces))
+        ]
+        specs = [pl.BlockSpec(memory_space=space) for space in spaces]
         flat, tree = jax.tree.flatten(out_shape)
         outs = [pl.BlockSpec(memory_space=pltpu.VMEM) for _ in flat]
         shapes = [
-            s if i in hbm_out else pltpu.VMEM(s.shape, s.dtype) for i, s in enumerate(flat)
+            (pltpu.HBM if i in hbm_out else pltpu.VMEM)(s.shape, s.dtype)
+            for i, s in enumerate(flat)
         ]
         return pl.pallas_call(
             kernel,
@@ -176,7 +180,7 @@
         return flux_v, flux_a, held
 
     start = (buoy[0] * now[0], buoy[0] * (bulk[0] * nxt[0]), jnp.zeros(now.shape[1:], F32))
-    _, _, held = lax.fori_loop(0, count, body, start)
+    _, _, held = lax.fori_loop(0, count, body, start, unroll=4)
     face_out[...] = held
 
 
@@ -196,19 +200,33 @@
         end_out[x] = 2.0 * here - now[x] + (STEP * bulk[x]) * lap
         return flux
 
-    lax.fori_loop(0, count, body, buoy[0] * mid[0])
-
-
-def pack_traces_kernel(groups, receivers, traces, out):
+    lax.fori_loop(0, count, body, buoy[0] * mid[0], unroll=4)
+
+
+def pack_traces_kernel(groups_in, receivers_in, traces_in, out, groups, receivers, traces, sems):
+    copies = [
+        pltpu.make_async_copy(src, dst, sems.at[i])
+        for i, (src, dst) in enumerate(
+            ((groups_in, groups), (receivers_in, receivers), (traces_in, traces))
+        )
+    ]
+    for copy in copies:
+        copy.start()
+    shots, cap, wide = out.shape
+    slots = shots * cap
+    count, samples = traces.shape
+    copies[0].wait()
     keys = groups[...]
     place = keys.astype(F32) * CAP + rank_row(keys)
-    slots = out.shape[0]
-    count, samples = traces.shape
     chosen = (iota((slots, count), 0).astype(F32) == place).astype(F32).astype(BF16)
+    copies[1].wait()
     ids = as_column(receivers[...].astype(F32))
     ids = jnp.where(iota((count, 128), 1) == 0, ids, 0.0).astype(BF16)
-    out[:, :samples] = jnp.dot(chosen, traces[...], preferred_element_type=F32).astype(BF16)
-    out[:, samples:] = jnp.dot(chosen, ids, preferred_element_type=F32).astype(BF16)
+    named = jnp.dot(chosen, ids, preferred_element_type=F32).astype(BF16)
+    out[:, :, samples:] = named.reshape(shots, cap, wide - samples)
+    copies[2].wait()
+    moved = jnp.dot(chosen, traces[...], preferred_element_type=F32).astype(BF16)
+    out[:, :, :samples] = moved.reshape(shots, cap, samples)
 
 
 def places_kernel(
@@ -255,13 +273,18 @@
     low = which_half()
     samples = filters.shape[1]
     count, lanes = hot_depth.shape
-    slots = rows_in.shape[0]
+    slots = rows_in.shape[0] * rows_in.shape[1]
     last_dims = (((1,), (1,)), ((), ()))
     values = lax.dot_general(
-        rows_in[:, :samples], filters[...], last_dims, preferred_element_type=F32
+        rows_in[:, :, :samples].reshape(slots, samples), filters[...], last_dims, preferred_element_type=F32
     )
     pick = ((iota((8, 128), 0) == 0) & (iota((8, 128), 1) == 0)).astype(F32).astype(BF16)
-    ids = lax.dot_general(pick, rows_in[:, samples:], last_dims, preferred_element_type=F32)
+    ids = lax.dot_general(
+        pick,
+        rows_in[:, :, samples:].reshape(slots, rows_in.shape[2] - samples),
+        last_dims,
+        preferred_element_type=F32,
+    )
     hot = (iota((count, slots), 0).astype(F32) == ids[0:1, :]).astype(F32).astype(BF16)
     observed = exact_dot(hot, values)
     sum_mid[...] = hot_depth[...] * (seen[:, 0:1] - observed[:, 0:1])
@@ -327,7 +350,7 @@
             send_out[place[0, x * tiles + t]] = whole[t]
         return flux
 
-    lax.fori_loop(0, count, body, buoy[0] * (bulk[0] * mid[0]))
+    lax.fori_loop(0, count, body, buoy[0] * (bulk[0] * mid[0]), unroll=4)
     code = codes[...]
     upper = jnp.floor(code * (1.0 / 64.0))
     lower = code - 64.0 * upper
@@ -410,18 +433,31 @@
     samples = traces.shape[1]
     face = sds((rows, lanes))
 
-    packed = call(pack_traces_kernel, "pack_traces", sds((shots * CAP, samples + 128), BF16))(
+    own_rows = traces.shape[0]
+    packed = call(
+        pack_traces_kernel,
+        "pack_traces",
+        sds((shots, CAP, samples + 128), BF16),
+        [
+            pltpu.VMEM((1, own_rows), I32),
+            pltpu.VMEM((1, own_rows), I32),
+            pltpu.VMEM((own_rows, samples), BF16),
+            pltpu.SemaphoreType.DMA((3,)),
+        ],
+        hbm=(0, 1, 2),
+        hbm_out=(0,),
+    )(
         trace_group.reshape(1, -1), trace_receiver.reshape(1, -1), traces
     )
     got_rows = lax.all_to_all(
-        packed.reshape(shots, CAP, samples + 128), "shot", split_axis=0, concat_axis=0, tiled=True
-    ).reshape(shots * CAP, samples + 128)
+        packed, "shot", split_axis=0, concat_axis=0, tiled=True
+    )
 
     faces = swap(call(faces_kernel, "faces", face)(now, buoy, bulk, nxt))
     lap_now, wave_mid, adj_base, mid_face = call(
-        first_kernel, "first_step", (field, field, field, face)
+        first_kernel, "first_step", (field, field, field, face), hbm_out=(0, 2)
     )(faces, now, prev, bulk, buoy, nxt, late)
-    lap_mid, wave_end = call(second_kernel, "second_step", (field, field))(
+    lap_mid, wave_end = call(second_kernel, "second_step", (field, field), hbm_out=(0,))(
         faces, swap(mid_face), wave_mid, now, bulk, buoy
     )
     receivers = receiver_cell.shape[1]
@@ -440,7 +476,7 @@
         ),
         [per_receiver, per_receiver],
         smem=(0,),
-        hbm_out=(2,),
+        hbm_out=(1, 2, 3, 4, 5),
     )(
         receiver_cell,
         receiver_cell,
@@ -451,7 +487,7 @@
     )
     filters = jnp.pad(group_filter[0], ((0, 14), (0, 0)))
     adj_mid, adj_add, adj_face = call(
-        inject_kernel, "inject", (flat, flat, face), [per_receiver, per_receiver], smem=(0,)
+        inject_kernel, "inject", (flat, flat, face), [per_receiver, per_receiver], smem=(0,), free=(1,)
     )(receiver_cell, got_rows, filters, seen, hot_depth, adj_base.reshape(flat.shape), bulk)
     per_class = (shots // CLASSES) * CAPT + 1
     adj_end, send = call(

time: 122 us -> 109 us (0.89)
  local copies, waits for them, and re-layouts: 15.1 us -> 5.37 us
  waiting for transfers between devices: 21 us -> 27.5 us
  Pallas kernels: 34.4 us -> 29.1 us
  starting transfers between devices: 24.8 us -> 21.7 us
    unnamed x54 -> x44, local copies, waits for them, and re-layouts: 11.6 us -> 5.36 us
    pallas_call x8, Pallas kernels: 34.4 us -> 29.1 us  [run(): pl.pallas_call(kernel, out_shape=jax.tree.unflatten(tree, shapes), in_spe...]
    all_to_all x1, waiting for transfers between devices: 3.55 us -> 8.59 us  [local(): lax.all_to_all(packed, 'shot', split_axis=0, concat_axis=0, tiled=True)]
    reshape x2 -> x0, local copies, waits for them, and re-layouts: 3.55 us -> none  [the longest x1 2.29 us: local(): got_rows = lax.all_to_all(packed.reshape(shots, CAP, samples + 128), 'sho...]
    all_to_all x1, starting transfers between devices: 6.51 us -> 3.42 us  [local(): lax.all_to_all(dense.reshape(rings, MT_DEV * 8, lanes), 'shot', split_axi...]
    all_to_all x1, waiting for transfers between devices: 9.04 us -> 10.3 us  [local(): lax.all_to_all(dense.reshape(rings, MT_DEV * 8, lanes), 'shot', split_axi...]
  transfers between devices with their start and end apart: 5 -> 5, of which waited for: 5 -> 5; matrix products, arithmetic and copies ran while one was open for 2% -> 2% of each run, Pallas kernels for 14% -> 13%
where the time goes in v4:
time: 109 us
  Pallas kernels  29.1 us (27%)
  waiting for transfers between devices  27.5 us (25%)
  blocking collectives  23.8 us (22%)
  starting transfers between devices  21.7 us (20%)
  local copies, waits for them, and re-layouts  5.37 us (5%)
    pallas_call x8, Pallas kernels, run(): pl.pallas_call(kernel, out_shape=jax.tree.unflatten(tree, shapes), in_spe...  29.1 us
    all_to_all x1, blocking collectives, local(): lax.all_to_all(send.reshape(CLASSES, per_class * 8, lanes), 'shot', split...  23.8 us
    all_to_all x1, starting transfers between devices, local(): lax.all_to_all(packed, 'shot', split_axis=0, concat_axis=0, tiled=True)  17 us
    all_to_all x1, waiting for transfers between devices, local(): lax.all_to_all(dense.reshape(rings, MT_DEV * 8, lanes), 'shot', split_axi...  10.3 us
    ppermute x3, waiting for transfers between devices, swap(): return lax.ppermute(face, 'ap', [(0, 1), (1, 0)])  8.63 us
    all_to_all x1, waiting for transfers between devices, local(): lax.all_to_all(packed, 'shot', split_axis=0, concat_axis=0, tiled=True)  8.59 us
    unnamed x44, local copies, waits for them, and re-layouts  5.36 us
    all_to_all x1, starting transfers between devices, local(): lax.all_to_all(dense.reshape(rings, MT_DEV * 8, lanes), 'shot', split_axi...  3.42 us
  transfers between devices with their start and end apart: 5, of which 5 were waited for; matrix products, arithmetic and copies ran while one was open for 2% of the time, Pallas kernels for 13%

profile of v4, /device:TPU:1, one launch (start us, length us, event | category | flops | bytes accessed | tf_op | source)
XLA Modules:
  0.0 109.0 jit_solution(7942939212795071828)
XLA Ops:
  0.6 0.0 copy-start.3
  0.6 2.6 %pack_traces.1 = bf16[128,2,2176]{2,1,0:T(2,128)(2,1)} custom-call(s32[1,128]{1,0:T(1,128)} %bitcast.52, s32[1,128]{1,0:T(1,128)} %bitcast.53, bf16[128,2048]{1,0:T(8,128)(2,1)} %traces_in.1), custom_call_target="tpu_custom_call" | custom-call | tf_op jit(solution)/shard_map/pack_traces/pallas_call | solution.py:40
  3.3 0.0 copy-start
  3.3 0.0 copy-start.1
  3.3 17.0 %all-to-all-start = ((bf16[128,2,2176]{2,1,0:T(2,128)(2,1)}), bf16[128,2,2176]{2,1,0:T(2,128)(2,1)}, u32[]{:S(2)}, u32[]{:S(2)}) async-start(bf16[128,2,2176]{2,1,0:T(2,128)(2,1)} %pack_traces.1), calls=%async_computation | async-start | bytes 2228224 | tf_op jit(solution)/shard_map/all_to_all | solution.py:452
  20.3 0.0 copy-start.5
  20.3 1.2 %copy-done.5 = f32[1,32,64,128]{3,2,1,0:T(8,128)S(1)} copy-done((f32[1,32,64,128]{3,2,1,0:T(8,128)S(1)}, f32[1,32,64,128]{3,2,1,0:T(8,128)}, u32[]{:S(2)}) %copy-start.5) | copy-done | bytes 1048600
  21.5 1.9 %faces.1 = f32[64,128]{1,0:T(8,128)S(1)} custom-call(f32[32,64,128]{2,1,0:T(8,128)S(1)} %bitcast.34, f32[32,64,128]{2,1,0:T(8,128)S(1)} %bitcast.30, f32[32,64,128]{2,1,0:T(8,128)S(1)} %bitcast.25, f32[32,64,128]{2,1,0:T(8,128)S(1)} %bitcast.37), custom_call_target="tpu_custom_call" | custom-call | tf_op jit(solution)/shard_map/faces/pallas_call | solution.py:40
  23.4 0.5 collective-permute-start
  23.9 3.0 %collective-permute-done.faces = f32[64,128]{1,0:T(8,128)S(1)} collective-permute-done((f32[64,128]{1,0:T(8,128)S(1)}, f32[64,128]{1,0:T(8,128)S(1)}, u32[]{:S(2)}, u32[]{:S(2)}) %collective-permute-start) | collective-permute-done | bytes 32800 | tf_op jit(solution)/shard_map/ppermute | solution.py:408
  26.9 6.7 %first_step.1 = (f32[32,64,128]{2,1,0:T(8,128)}, f32[32,64,128]{2,1,0:T(8,128)S(1)}, f32[32,64,128]{2,1,0:T(8,128)}, f32[64,128]{1,0:T(8,128)S(1)}) custom-call(f32[64,128]{1,0:T(8,128)S(1)} %collective-permute-done.faces, f32[32,64,128]{2,1,0:T(8,128)S(1)} %bitcast.35, f32[32,64,128]{2,1,0:T(8,128)S(1)} %bitcast.43, f32[32,64,128]{2,1,0:T(8,128)S(1)} %bitcast.26, ...), custom_call_target="tpu_custom_call" | custom-call | tf_op jit(solution)/shard_map/first_step/pallas_call | solution.py:40
  33.6 0.3 collective-permute-start.1
  33.9 0.0 copy-done.20
  33.9 3.3 %collective-permute-done.1.mid_face = f32[64,128]{1,0:T(8,128)S(1)} collective-permute-done((f32[64,128]{1,0:T(8,128)S(1)}, f32[64,128]{1,0:T(8,128)S(1)}, u32[]{:S(2)}, u32[]{:S(2)}) %collective-permute-start.1) | collective-permute-done | bytes 32800 | tf_op jit(solution)/shard_map/ppermute | solution.py:408
  37.2 3.9 %second_step.1 = (f32[32,64,128]{2,1,0:T(8,128)}, f32[32,64,128]{2,1,0:T(8,128)S(1)}) custom-call(f32[64,128]{1,0:T(8,128)S(1)} %collective-permute-done.faces, f32[64,128]{1,0:T(8,128)S(1)} %collective-permute-done.1.mid_face, f32[32,64,128]{2,1,0:T(8,128)S(1)} %get-tuple-element.20.mid, f32[32,64,128]{2,1,0:T(8,128)S(1)} %bitcast.36, ...), custom_call_target="tpu_custom_call" | custom-call | tf_op jit(solution)/shard_map/second_step/pallas_call | solution.py:40
  41.2 0.0 copy-done.18
  41.2 2.2 %places.1 = (f32[256,128]{1,0:T(8,128)S(1)}, f32[256,128]{1,0:T(8,128)}, s32[1,256]{1,0:T(1,128)}, bf16[16,256]{1,0:T(8,128)(2,1)}, f32[256,128]{1,0:T(8,128)}, /*index=5*/f32[16,128]{1,0:T(8,128)}) custom-call(s32[1,256]{1,0:T(1,128)S(1)} %copy-done.14, s32[1,256]{1,0:T(1,128)S(1)} %copy-done.14, f32[2048,128]{1,0:T(8,128)S(1)} %bitcast.41, ...), custom_call_target="tpu_custom_call" | custom-call | tf_op jit(solution)/shard_map/places/pallas_call | solution.py:40
  43.4 8.6 %all-to-all-done.rows_in = bf16[128,2,2176]{2,1,0:T(2,128)(2,1)} async-done(((bf16[128,2,2176]{2,1,0:T(2,128)(2,1)}), bf16[128,2,2176]{2,1,0:T(2,128)(2,1)}, u32[]{:S(2)}, u32[]{:S(2)}) %all-to-all-start) | async-done | bytes 1114144 | tf_op jit(solution)/shard_map/all_to_all | solution.py:452
  52.0 0.9 copy-done.13
  52.9 0.0 copy-start.15
  52.9 4.8 %inject.1 = (f32[2048,128]{1,0:T(8,128)S(1)}, f32[2048,128]{1,0:T(8,128)S(1)}, f32[64,128]{1,0:T(8,128)S(1)}) custom-call(s32[1,256]{1,0:T(1,128)S(1)} %copy-done.14, bf16[128,2,2176]{2,1,0:T(2,128)(2,1)} %all-to-all-done.rows_in, bf16[16,2048]{1,0:T(8,128)(2,1)S(1)} %pad.4.filters, f32[256,128]{1,0:T(8,128)S(1)} %get-tuple-element.23.seen, ...), custom_call_target="tpu_custom_call" | custom-call | tf_op jit(solution)/shard_map/inject/pallas_call | solution.py:40
  57.7 0.5 collective-permute-start.2
  58.2 2.4 %collective-permute-done.2.adj_face = f32[64,128]{1,0:T(8,128)S(1)} collective-permute-done((f32[64,128]{1,0:T(8,128)S(1)}, f32[64,128]{1,0:T(8,128)S(1)}, u32[]{:S(2)}, u32[]{:S(2)}) %collective-permute-start.2) | collective-permute-done | bytes 32800 | tf_op jit(solution)/shard_map/ppermute | solution.py:408
  60.6 1.2 %copy-done.10 = f32[32,64,128]{2,1,0:T(8,128)S(1)} copy-done((f32[32,64,128]{2,1,0:T(8,128)S(1)}, f32[32,64,128]{2,1,0:T(8,128)}, u32[]{:S(2)}) %copy-start.10) | copy-done | bytes 1048600
  61.9 4.6 %image.1 = (f32[32,64,128]{2,1,0:T(8,128)S(1)}, s16[528,8,128]{2,1,0:T(8,128)(2,1)S(1)}) custom-call(f32[64,128]{1,0:T(8,128)S(1)} %collective-permute-done.faces, f32[64,128]{1,0:T(8,128)S(1)} %collective-permute-done.2.adj_face, f32[32,64,128]{2,1,0:T(8,128)S(1)} %bitcast.46, f32[32,64,128]{2,1,0:T(8,128)S(1)} %bitcast.47, f32[32,64,128]{2,1,0:T(8,128)S(1)} %bitcast.39, ...), custom_call_target="tpu_custom_call" | custom-call | tf_op jit(solution)/shard_map/image/pallas_call | solution.py:40
  66.5 23.8 %all_to_all.15 = s16[16,264,128]{2,1,0:T(8,128)(2,1)S(1)} all-to-all(s16[16,264,128]{2,1,0:T(8,128)(2,1)S(1)} %bitcast.42), channel_id=1, replica_groups={{0,2,4,6,8,10,12,14,16,18,20,22,24,26,28,30},{32,34,36,38,40,42,44,46,4..., dimensions={0} | all-to-all | bytes 2162688 | tf_op jit(solution)/shard_map/all_to_all | solution.py:505
  90.3 2.4 %combine.1 = f32[64,8,128]{2,1,0:T(8,128)} custom-call(s16[528,8,128]{2,1,0:T(8,128)(2,1)S(1)} %bitcast.40), custom_call_target="tpu_custom_call" | custom-call | tf_op jit(solution)/shard_map/combine/pallas_call | solution.py:40
  92.7 3.4 %all-to-all-start.2 = ((f32[8,64,128]{2,1,0:T(8,128)}), f32[8,64,128]{2,1,0:T(8,128)S(1)}, u32[]{:S(2)}, u32[]{:S(2)}) async-start(f32[8,64,128]{2,1,0:T(8,128)} %bitcast.18), calls=%async_computation.2 | async-start | bytes 524288 | tf_op jit(solution)/shard_map/all_to_all | solution.py:528
  96.2 1.0 copy.16
  97.1 1.0 copy.17
  98.1 10.3 %all-to-all-done.2 = f32[8,64,128]{2,1,0:T(8,128)S(1)} async-done(((f32[8,64,128]{2,1,0:T(8,128)}), f32[8,64,128]{2,1,0:T(8,128)S(1)}, u32[]{:S(2)}, u32[]{:S(2)}) %all-to-all-start.2) | async-done | bytes 262176 | tf_op jit(solution)/shard_map/all_to_all | solution.py:528
  108.4 0.6 reduce_sum.9
  (33 shorter events, 0.1 us)
Async XLA Ops:
  0.6 19.6 %copy-start.3 = (f32[1,32,64,128]{3,2,1,0:T(8,128)S(1)}, f32[1,32,64,128]{3,2,1,0:T(8,128)}, u32[]{:S(2)}) copy-start(f32[1,32,64,128]{3,2,1,0:T(8,128)} %param.14) | copy-start | bytes 3145732
  3.3 17.0 %copy-start = (f32[1,32,64,128]{3,2,1,0:T(8,128)S(1)}, f32[1,32,64,128]{3,2,1,0:T(8,128)}, u32[]{:S(2)}) copy-start(f32[1,32,64,128]{3,2,1,0:T(8,128)} %param.17) | copy-start | bytes 3145732
  3.3 17.0 %copy-start.1 = (f32[1,32,64,128]{3,2,1,0:T(8,128)S(1)}, f32[1,32,64,128]{3,2,1,0:T(8,128)}, u32[]{:S(2)}) copy-start(f32[1,32,64,128]{3,2,1,0:T(8,128)} %param.18) | copy-start | bytes 3145732
  3.3 48.7 %all-to-all-start = ((bf16[128,2,2176]{2,1,0:T(2,128)(2,1)}), bf16[128,2,2176]{2,1,0:T(2,128)(2,1)}, u32[]{:S(2)}, u32[]{:S(2)}) async-start(bf16[128,2,2176]{2,1,0:T(2,128)(2,1)} %pack_traces.1), calls=%async_computation | async-start | bytes 2228224 | tf_op jit(solution)/shard_map/all_to_all | solution.py:452
  20.3 1.2 %copy-start.5 = (f32[1,32,64,128]{3,2,1,0:T(8,128)S(1)}, f32[1,32,64,128]{3,2,1,0:T(8,128)}, u32[]{:S(2)}) copy-start(f32[1,32,64,128]{3,2,1,0:T(8,128)} %param.16) | copy-start | bytes 3145732
  21.5 5.4 %copy-start.7 = (f32[1,32,64,128]{3,2,1,0:T(8,128)S(1)}, f32[1,32,64,128]{3,2,1,0:T(8,128)}, u32[]{:S(2)}) copy-start(f32[1,32,64,128]{3,2,1,0:T(8,128)} %param.13) | copy-start | bytes 3145732
  21.5 5.4 %copy-start.8 = (f32[1,32,64,128]{3,2,1,0:T(8,128)S(1)}, f32[1,32,64,128]{3,2,1,0:T(8,128)}, u32[]{:S(2)}) copy-start(f32[1,32,64,128]{3,2,1,0:T(8,128)} %param.15) | copy-start | bytes 3145732
  23.4 3.5 %collective-permute-start = (f32[64,128]{1,0:T(8,128)S(1)}, f32[64,128]{1,0:T(8,128)S(1)}, u32[]{:S(2)}, u32[]{:S(2)}) collective-permute-start(f32[64,128]{1,0:T(8,128)S(1)} %faces.1), channel_id=1, source_target_pairs={{0,1},{1,0},{2,3},{3,2},{4,5},{5,4},{6,7},{7,6},{8,9},{9,8},{10,11... | collective-permute-start | bytes 98312 | tf_op jit(solution)/shard_map/ppermute | solution.py:408
  26.9 7.0 %copy-start.20 = (bf16[1,2,2048]{2,1,0:T(2,128)(2,1)S(1)}, bf16[1,2,2048]{2,1,0:T(2,128)(2,1)}, u32[]{:S(2)}) copy-start(bf16[1,2,2048]{2,1,0:T(2,128)(2,1)} %param.20) | copy-start | bytes 24580
  26.9 10.3 %copy-start.4 = (f32[1,32,64,128]{3,2,1,0:T(8,128)S(1)}, f32[1,32,64,128]{3,2,1,0:T(8,128)}, u32[]{:S(2)}) copy-start(f32[1,32,64,128]{3,2,1,0:T(8,128)} %param.14) | copy-start | bytes 3145732
  33.6 3.6 %collective-permute-start.1 = (f32[64,128]{1,0:T(8,128)S(1)}, f32[64,128]{1,0:T(8,128)S(1)}, u32[]{:S(2)}, u32[]{:S(2)}) collective-permute-start(f32[64,128]{1,0:T(8,128)S(1)} %get-tuple-element.21), channel_id=1, source_target_pairs={{0,1},{1,0},{2,3},{3,2},{4,5},{5,4},{6,7},{7,6},{8,9},{9,8},{10,11... | collective-permute-start | bytes 98312 | tf_op jit(solution)/shard_map/ppermute | solution.py:408
  37.2 3.9 %copy-start.14 = (s32[1,256]{1,0:T(1,128)S(1)}, s32[1,256]{1,0:T(1,128)}, u32[]{:S(2)}) copy-start(s32[1,256]{1,0:T(1,128)} %at.3) | copy-start | bytes 3076
  37.2 3.9 %copy-start.17 = (s32[256,1]{0,1:T(1,128)S(1)}, s32[256,1]{0,1:T(1,128)}, u32[]{:S(2)}) copy-start(s32[256,1]{0,1:T(1,128)} %param.24) | copy-start | bytes 3076
  37.2 3.9 %copy-start.18 = (s32[256]{0:T(256)S(1)}, s32[256]{0:T(256)}, u32[]{:S(2)}) copy-start(s32[256]{0:T(256)} %param.25) | copy-start | bytes 3076
  41.2 10.8 %copy-start.11 = (f32[32,64,128]{2,1,0:T(8,128)S(1)}, f32[32,64,128]{2,1,0:T(8,128)}, u32[]{:S(2)}) copy-start(f32[32,64,128]{2,1,0:T(8,128)} %get-tuple-element.25) | copy-start | bytes 3145732
  52.0 0.9 copy-start.13
  52.9 7.7 %copy-start.2 = (f32[1,32,64,128]{3,2,1,0:T(8,128)S(1)}, f32[1,32,64,128]{3,2,1,0:T(8,128)}, u32[]{:S(2)}) copy-start(f32[1,32,64,128]{3,2,1,0:T(8,128)} %param.18) | copy-start | bytes 3145732
  52.9 7.7 %copy-start.6 = (f32[1,32,64,128]{3,2,1,0:T(8,128)S(1)}, f32[1,32,64,128]{3,2,1,0:T(8,128)}, u32[]{:S(2)}) copy-start(f32[1,32,64,128]{3,2,1,0:T(8,128)} %param.16) | copy-start | bytes 3145732
  52.9 7.7 %copy-start.9 = (f32[32,64,128]{2,1,0:T(8,128)S(1)}, f32[32,64,128]{2,1,0:T(8,128)}, u32[]{:S(2)}) copy-start(f32[32,64,128]{2,1,0:T(8,128)} %get-tuple-element.30.lap_now) | copy-start | bytes 3145732
  52.9 7.7 %copy-start.12 = (f32[256,128]{1,0:T(8,128)S(1)}, f32[256,128]{1,0:T(8,128)}, u32[]{:S(2)}) copy-start(f32[256,128]{1,0:T(8,128)} %get-tuple-element.33.spot_hot) | copy-start | bytes 393220
  52.9 7.7 %copy-start.15 = (bf16[16,256]{1,0:T(8,128)(2,1)S(1)}, bf16[16,256]{1,0:T(8,128)(2,1)}, u32[]{:S(2)}) copy-start(bf16[16,256]{1,0:T(8,128)(2,1)} %get-tuple-element.32.cls_hot) | copy-start | bytes 24580
  52.9 7.7 %copy-start.16 = (f32[16,128]{1,0:T(8,128)S(1)}, f32[16,128]{1,0:T(8,128)}, u32[]{:S(2)}) copy-start(f32[16,128]{1,0:T(8,128)} %get-tuple-element.34.ids) | copy-start | bytes 24580
  52.9 7.7 %copy-start.19 = (s32[1,256]{1,0:T(1,128)S(1)}, s32[1,256]{1,0:T(1,128)}, u32[]{:S(2)}) copy-start(s32[1,256]{1,0:T(1,128)} %get-tuple-element.31.place) | copy-start | bytes 3076
  57.7 2.9 %collective-permute-start.2 = (f32[64,128]{1,0:T(8,128)S(1)}, f32[64,128]{1,0:T(8,128)S(1)}, u32[]{:S(2)}, u32[]{:S(2)}) collective-permute-start(f32[64,128]{1,0:T(8,128)S(1)} %get-tuple-element.26), channel_id=1, source_target_pairs={{0,1},{1,0},{2,3},{3,2},{4,5},{5,4},{6,7},{7,6},{8,9},{9,8},{10,11... | collective-permute-start | bytes 98312 | tf_op jit(solution)/shard_map/ppermute | solution.py:408
  60.6 1.2 %copy-start.10 = (f32[32,64,128]{2,1,0:T(8,128)S(1)}, f32[32,64,128]{2,1,0:T(8,128)}, u32[]{:S(2)}) copy-start(f32[32,64,128]{2,1,0:T(8,128)} %get-tuple-element.29.lap_mid) | copy-start | bytes 3145732
  92.7 15.7 %all-to-all-start.2 = ((f32[8,64,128]{2,1,0:T(8,128)}), f32[8,64,128]{2,1,0:T(8,128)S(1)}, u32[]{:S(2)}, u32[]{:S(2)}) async-start(f32[8,64,128]{2,1,0:T(8,128)} %bitcast.18), calls=%async_computation.2 | async-start | bytes 524288 | tf_op jit(solution)/shard_map/all_to_all | solution.py:528

commit v5 on v4

--- a/solution.py
+++ b/solution.py
@@ -1,3 +1,5 @@
+import functools
+
 import jax
 import jax.numpy as jnp
 from jax import lax
@@ -18,31 +20,62 @@
 I32 = jnp.int32
 
 
-def call(kernel, name, out_shape, scratch=(), smem=(), hbm_out=(), free=(), hbm=()):
+def staged_kernel(kernel, stage, late, count_in, count_out, *refs):
+    inputs, rest = list(refs[:count_in]), refs[count_in : len(refs) - len(stage) - 1]
+    sems, buffers = refs[len(refs) - len(stage) - 1], refs[len(refs) - len(stage) :]
+    copies = []
+    for n, (i, buffer) in enumerate(zip(stage, buffers)):
+        copies.append(pltpu.make_async_copy(inputs[i], buffer, sems.at[n]))
+        copies[-1].start()
+        inputs[i] = buffer
+
+    def arrived():
+        for copy in copies:
+            copy.wait()
+
+    if late:
+        kernel(arrived, *inputs, *rest)
+    else:
+        arrived()
+        kernel(*inputs, *rest)
+
+
+def call(
+    kernel, name, out_shape, scratch=(), smem=(), hbm_out=(), hbm=(), raw_out=(), stage=(),
+    late=False,
+):
     def run(*args):
         spaces = [
-            pltpu.SMEM if i in smem else pltpu.HBM if i in hbm else pltpu.VMEM
+            pltpu.SMEM if i in smem else pltpu.HBM if i in hbm or i in stage else pltpu.VMEM
             for i in range(len(args))
         ]
         args = [
-            pltpu.with_memory_space_constraint(x, space)
-            if space is not pltpu.SMEM and i not in free
-            else x
-            for i, (x, space) in enumerate(zip(args, spaces))
+            x if space is pltpu.SMEM else pltpu.with_memory_space_constraint(x, space)
+            for x, space in zip(args, spaces)
         ]
         specs = [pl.BlockSpec(memory_space=space) for space in spaces]
         flat, tree = jax.tree.flatten(out_shape)
-        outs = [pl.BlockSpec(memory_space=pltpu.VMEM) for _ in flat]
+        outs = [
+            pl.BlockSpec(memory_space=pltpu.HBM if i in raw_out else pltpu.VMEM)
+            for i in range(len(flat))
+        ]
         shapes = [
-            (pltpu.HBM if i in hbm_out else pltpu.VMEM)(s.shape, s.dtype)
+            (pltpu.HBM if i in hbm_out or i in raw_out else pltpu.VMEM)(s.shape, s.dtype)
             for i, s in enumerate(flat)
         ]
+        body, extra = kernel, []
+        if stage:
+            body = functools.partial(
+                staged_kernel, kernel, stage, late, len(args), len(flat)
+            )
+            extra = [pltpu.SemaphoreType.DMA((len(stage),))]
+            extra += [pltpu.VMEM(args[i].shape, args[i].dtype) for i in stage]
         return pl.pallas_call(
-            kernel,
+            body,
             out_shape=jax.tree.unflatten(tree, shapes),
             in_specs=specs,
             out_specs=jax.tree.unflatten(tree, outs),
-            scratch_shapes=list(scratch),
+            scratch_shapes=list(scratch) + extra,
             name=name,
             compiler_params=pltpu.CompilerParams(vmem_limit_bytes=VMEM_LIMIT),
         )(*args)
@@ -176,8 +209,9 @@
         lap, flux_a = twice_operate(
             scaled, scaled_after, take_face(faces[...], 64 + x, low), flux_a, side_sums
         )
-        base_out[x] = 2.0 * nxt[x] - late[x] + (0.5 * STEP) * lap
-        return flux_v, flux_a, held
+        base = 2.0 * nxt[x] - late[x] + (0.5 * STEP) * lap
+        base_out[x] = base
+        return flux_v, flux_a, put_face(held, bulk[x] * base, 32 + x, low)
 
     start = (buoy[0] * now[0], buoy[0] * (bulk[0] * nxt[0]), jnp.zeros(now.shape[1:], F32))
     _, _, held = lax.fori_loop(0, count, body, start, unroll=4)
@@ -203,36 +237,62 @@
     lax.fori_loop(0, count, body, buoy[0] * mid[0], unroll=4)
 
 
-def pack_traces_kernel(groups_in, receivers_in, traces_in, out, groups, receivers, traces, sems):
-    copies = [
-        pltpu.make_async_copy(src, dst, sems.at[i])
-        for i, (src, dst) in enumerate(
-            ((groups_in, groups), (receivers_in, receivers), (traces_in, traces))
-        )
-    ]
-    for copy in copies:
-        copy.start()
+PACK_CHUNK = 512
+
+
+def pack_traces_kernel(groups_in, receivers_in, traces_in, out, groups, receivers, traces, made, sems):
     shots, cap, wide = out.shape
     slots = shots * cap
     count, samples = traces.shape
-    copies[0].wait()
+    starts = range(0, samples, PACK_CHUNK)
+    small = [
+        pltpu.make_async_copy(groups_in, groups, sems.at[0]),
+        pltpu.make_async_copy(receivers_in, receivers, sems.at[1]),
+    ]
+    loads = []
+    for i, start in enumerate(starts):
+        part = pl.ds(start, PACK_CHUNK)
+        loads.append(
+            pltpu.make_async_copy(traces_in.at[:, part], traces.at[:, part], sems.at[2 + i])
+        )
+    for copy in small + loads:
+        copy.start()
+    small[0].wait()
     keys = groups[...]
     place = keys.astype(F32) * CAP + rank_row(keys)
     chosen = (iota((slots, count), 0).astype(F32) == place).astype(F32).astype(BF16)
-    copies[1].wait()
+    small[1].wait()
     ids = as_column(receivers[...].astype(F32))
     ids = jnp.where(iota((count, 128), 1) == 0, ids, 0.0).astype(BF16)
     named = jnp.dot(chosen, ids, preferred_element_type=F32).astype(BF16)
-    out[:, :, samples:] = named.reshape(shots, cap, wide - samples)
-    copies[2].wait()
-    moved = jnp.dot(chosen, traces[...], preferred_element_type=F32).astype(BF16)
-    out[:, :, :samples] = moved.reshape(shots, cap, samples)
+    made[:, :, samples:] = named.reshape(shots, cap, wide - samples)
+    stores = []
+
+    def send(start, width):
+        part = pl.ds(start, width)
+        copy = pltpu.make_async_copy(
+            made.at[:, :, part], out.at[:, :, part], sems.at[2 + len(loads) + len(stores)]
+        )
+        copy.start()
+        stores.append(copy)
+
+    send(samples, wide - samples)
+    for load, start in zip(loads, starts):
+        load.wait()
+        moved = jnp.dot(
+            chosen, traces[:, start : start + PACK_CHUNK], preferred_element_type=F32
+        ).astype(BF16)
+        made[:, :, start : start + PACK_CHUNK] = moved.reshape(shots, cap, PACK_CHUNK)
+        send(start, PACK_CHUNK)
+    for copy in stores:
+        copy.wait()
 
 
 def places_kernel(
-    at, cells, mid, end, owners, slots, seen_out, hot_depth_out, place_out, cls_out, spot_out,
-    ids_out, rows_mid, rows_end,
+    at, cells, mid, end, bulk, owners, slots, about_out, hot_second_out, place_out, cls_out,
+    spot_out, ids_out, rows_mid, rows_end, rows_bulk,
 ):
+    low = which_half()
     lanes = 128
     count = cells.shape[1]
 
@@ -240,15 +300,26 @@
         row = lax.shift_right_logical(at[0, r], 7)
         rows_mid[pl.ds(r, 1), :] = mid[pl.ds(row, 1), :]
         rows_end[pl.ds(r, 1), :] = end[pl.ds(row, 1), :]
+        rows_bulk[pl.ds(r, 1), :] = bulk[pl.ds(row, 1), :]
         return carry
 
     lax.fori_loop(0, count, body, 0, unroll=8)
-    cell_col = as_column(cells[...])
-    here = iota((count, lanes), 1) == (cell_col & (lanes - 1))
-    hot_depth_out[...] = here.astype(F32)
+    cell_row = cells[...]
+    cell_col = as_column(cell_row)
+    lane = iota((count, lanes), 1)
+    depth_col = cell_col & (lanes - 1)
+    here = lane == depth_col
     seen_mid = jnp.sum(jnp.where(here, rows_mid[...], 0.0), axis=1, keepdims=True)
     seen_end = jnp.sum(jnp.where(here, rows_end[...], 0.0), axis=1, keepdims=True)
-    seen_out[...] = jnp.where(iota((count, lanes), 1) == 0, seen_mid, seen_end)
+    at_edge = here & (lane == edge_lane(low, lanes))
+    edge_bulk = jnp.sum(jnp.where(at_edge, rows_bulk[...], 0.0), axis=1, keepdims=True)
+    about_out[:, :lanes] = jnp.where(lane == 0, seen_mid, seen_end)
+    about_out[:, lanes : 2 * lanes] = here.astype(F32)
+    first_col = lax.shift_right_logical(cell_col, 13)
+    about_out[:, 2 * lanes :] = jnp.where(lane == first_col + 32, edge_bulk, 0.0)
+    rows = hot_second_out.shape[0]
+    second_row = lax.shift_right_logical(cell_row, 7) & (rows - 1)
+    hot_second_out[...] = (iota((rows, count), 0) == second_row).astype(F32).astype(BF16)
 
     owner = owners[...]
     tiles = owner.shape[1]
@@ -267,16 +338,16 @@
     )
 
 
-def inject_kernel(
-    at, rows_in, filters, seen, hot_depth, base, bulk, mid_out, add_out, face_out, sum_mid, sum_end
-):
-    low = which_half()
+def residual_kernel(rows_in, filters, about, hot_second, sum_mid, sum_end, face_out):
     samples = filters.shape[1]
-    count, lanes = hot_depth.shape
+    count, lanes = sum_mid.shape
     slots = rows_in.shape[0] * rows_in.shape[1]
     last_dims = (((1,), (1,)), ((), ()))
     values = lax.dot_general(
-        rows_in[:, :, :samples].reshape(slots, samples), filters[...], last_dims, preferred_element_type=F32
+        rows_in[:, :, :samples].reshape(slots, samples),
+        filters[...],
+        last_dims,
+        preferred_element_type=F32,
     )
     pick = ((iota((8, 128), 0) == 0) & (iota((8, 128), 1) == 0)).astype(F32).astype(BF16)
     ids = lax.dot_general(
@@ -287,8 +358,15 @@
     )
     hot = (iota((count, slots), 0).astype(F32) == ids[0:1, :]).astype(F32).astype(BF16)
     observed = exact_dot(hot, values)
-    sum_mid[...] = hot_depth[...] * (seen[:, 0:1] - observed[:, 0:1])
-    sum_end[...] = hot_depth[...] * (seen[:, 1:2] - observed[:, 1:2])
+    resid_mid = about[:, 0:1] - observed[:, 0:1]
+    resid_end = about[:, 1:2] - observed[:, 1:2]
+    hot_depth = about[:, lanes : 2 * lanes]
+    sum_mid[...] = hot_depth * resid_mid
+    sum_end[...] = hot_depth * resid_end
+    face_out[...] = exact_dot(hot_second[...], about[:, 2 * lanes :] * resid_end)
+
+
+def inject_kernel(at, sum_mid, sum_end, base, mid_out, add_out):
     mid_out[...] = base[...]
     add_out[...] = jnp.zeros_like(add_out)
 
@@ -298,26 +376,18 @@
         add_out[pl.ds(row, 1), :] = add_out[pl.ds(row, 1), :] + sum_mid[pl.ds(r, 1), :]
         return carry
 
-    lax.fori_loop(0, count, body, 0, unroll=8)
-    rows = bulk.shape[1]
-
-    def edge(x, held):
-        field = mid_out[pl.ds(pl.multiple_of(x * rows, rows), rows), :]
-        return put_face(held, bulk[x] * field, x, low)
-
-    face_out[...] = lax.fori_loop(
-        0, bulk.shape[0], edge, jnp.zeros(bulk.shape[1:], F32), unroll=2
-    )
+    lax.fori_loop(0, sum_mid.shape[0], body, 0, unroll=8)
 
 
 def image_kernel(
-    faces, adj_face, mid, add, nxt, bulk, buoy, lap_mid, lap_now, place, cls_hot, spot_hot, ids,
-    last_out, send_out, codes,
+    arrived, faces, mid_face, adj_face, mid, add, nxt, bulk, buoy, lap_mid, lap_now, place, cls_hot, spot_hot, ids,
+    last_out, send_out, codes, scaled_face,
 ):
     low = which_half()
     count, rows, lanes = mid.shape
     tiles = rows // 8
     per_class = send_out.shape[0] // CLASSES
+    scaled_face[...] = mid_face[...] + adj_face[...]
 
     def clear(c, carry):
         send_out[pl.ds(c * per_class, per_class)] = jnp.zeros((per_class, 8, lanes), jnp.int16)
@@ -332,13 +402,19 @@
         lap, flux = twice_operate(
             bulk[x] * here,
             (keep * bulk[after]) * mid[after],
-            take_face(adj_face[...], x, low),
+            take_face(scaled_face[...], 32 + x, low),
             flux,
             side_sums,
         )
-        end = 2.0 * here - nxt[x] + (0.5 * STEP) * lap + add[x]
-        last_out[x] = end
-        image = (STEP * (here * lap_mid[x] + end * lap_now[x])).reshape(tiles, 8, lanes)
+        last_out[x] = 2.0 * here - nxt[x] + (0.5 * STEP) * lap + add[x]
+        return flux
+
+    lax.fori_loop(0, count, body, buoy[0] * (bulk[0] * mid[0]), unroll=4)
+    arrived()
+
+    def pack(x, carry):
+        image = mid[x] * lap_mid[x] + last_out[x] * lap_now[x]
+        image = (STEP * image).reshape(tiles, 8, lanes)
         peak = jnp.max(jnp.max(jnp.abs(image), axis=1), axis=1, keepdims=True)
         code = jnp.ceil(16.0 * jnp.log2(jnp.maximum(peak, 1e-30))) + 1.0
         codes[pl.ds(pl.multiple_of(x * tiles, tiles), tiles), :] = jnp.broadcast_to(
@@ -348,9 +424,9 @@
         whole = jnp.round(image * gain[:, None, :]).astype(I32).astype(jnp.int16)
         for t in range(tiles):
             send_out[place[0, x * tiles + t]] = whole[t]
-        return flux
-
-    lax.fori_loop(0, count, body, buoy[0] * (bulk[0] * mid[0]), unroll=4)
+        return carry
+
+    lax.fori_loop(0, count, pack, 0, unroll=4)
     code = codes[...]
     upper = jnp.floor(code * (1.0 / 64.0))
     lower = code - 64.0 * upper
@@ -442,10 +518,11 @@
             pltpu.VMEM((1, own_rows), I32),
             pltpu.VMEM((1, own_rows), I32),
             pltpu.VMEM((own_rows, samples), BF16),
-            pltpu.SemaphoreType.DMA((3,)),
+            pltpu.VMEM((shots, CAP, samples + 128), BF16),
+            pltpu.SemaphoreType.DMA((3 + 2 * (samples // PACK_CHUNK),)),
         ],
         hbm=(0, 1, 2),
-        hbm_out=(0,),
+        raw_out=(0,),
     )(
         trace_group.reshape(1, -1), trace_receiver.reshape(1, -1), traces
     )
@@ -457,24 +534,25 @@
     lap_now, wave_mid, adj_base, mid_face = call(
         first_kernel, "first_step", (field, field, field, face), hbm_out=(0, 2)
     )(faces, now, prev, bulk, buoy, nxt, late)
+    mid_face = swap(mid_face)
     lap_mid, wave_end = call(second_kernel, "second_step", (field, field), hbm_out=(0,))(
-        faces, swap(mid_face), wave_mid, now, bulk, buoy
+        faces, mid_face, wave_mid, now, bulk, buoy
     )
     receivers = receiver_cell.shape[1]
     tiles = tile_owner.shape[0]
     per_receiver = pltpu.VMEM((receivers, lanes), F32)
-    seen, hot_depth, place, cls_hot, spot_hot, ids = call(
+    about, hot_second, place, cls_hot, spot_hot, ids = call(
         places_kernel,
         "places",
         (
-            sds((receivers, lanes)),
-            sds((receivers, lanes)),
+            sds((receivers, 3 * lanes)),
+            sds((rows, receivers), BF16),
             sds((1, tiles), I32),
             sds((CLASSES, tiles), BF16),
             sds((tiles, lanes)),
             sds((CLASSES, lanes)),
         ),
-        [per_receiver, per_receiver],
+        [per_receiver] * 3,
         smem=(0,),
         hbm_out=(1, 2, 3, 4, 5),
     )(
@@ -482,23 +560,30 @@
         receiver_cell,
         wave_mid.reshape(flat.shape),
         wave_end.reshape(flat.shape),
+        bulk.reshape(flat.shape),
         tile_owner.reshape(1, -1),
         tile_slot.reshape(1, -1),
     )
-    filters = jnp.pad(group_filter[0], ((0, 14), (0, 0)))
-    adj_mid, adj_add, adj_face = call(
-        inject_kernel, "inject", (flat, flat, face), [per_receiver, per_receiver], smem=(0,), free=(1,)
-    )(receiver_cell, got_rows, filters, seen, hot_depth, adj_base.reshape(flat.shape), bulk)
+    spread = sds((receivers, lanes))
+    sum_mid, sum_end, adj_face = call(
+        residual_kernel, "residual", (spread, spread, face), stage=(0, 1, 3)
+    )(got_rows, group_filter[0], about, hot_second)
+    adj_face = swap(adj_face)
+    adj_mid, adj_add = call(inject_kernel, "inject", (flat, flat), smem=(0,))(
+        receiver_cell, sum_mid, sum_end, adj_base.reshape(flat.shape)
+    )
     per_class = (shots // CLASSES) * CAPT + 1
     adj_end, send = call(
         image_kernel,
         "image",
         (field, sds((CLASSES * per_class, 8, lanes), jnp.int16)),
-        [pltpu.VMEM((tiles, lanes), F32)],
-        smem=(9,),
+        [pltpu.VMEM((tiles, lanes), F32), pltpu.VMEM((rows, lanes), F32)],
+        smem=(10,),
+        stage=(8, 9),
+        late=True,
     )(
-        faces, swap(adj_face), adj_mid.reshape(now.shape), adj_add.reshape(now.shape), nxt, bulk,
-        buoy, lap_mid, lap_now, place, cls_hot, spot_hot, ids,
+        faces, mid_face, adj_face, adj_mid.reshape(now.shape), adj_add.reshape(now.shape), nxt,
+        bulk, buoy, lap_mid, lap_now, place, cls_hot, spot_hot, ids,
     )
     near = [[r * CLASSES + c for c in range(CLASSES)] for r in range(rings)]
     far = [[r * CLASSES + c for r in range(rings)] for c in range(CLASSES)]

time: 109 us -> 105 us (0.963)
  waiting for transfers between devices: 27.5 us -> 22.7 us
  local copies, waits for them, and re-layouts: 5.37 us -> 3.26 us
  Pallas kernels: 29.1 us -> 31.2 us
    ppermute x3, waiting for transfers between devices: 8.63 us -> 6.35 us  [swap(): return lax.ppermute(face, 'ap', [(0, 1), (1, 0)])]
    unnamed x44 -> x46, local copies, waits for them, and re-layouts: 5.36 us -> 3.26 us
    pallas_call x8 -> x9, Pallas kernels: 29.1 us -> 31.2 us  [run(): pl.pallas_call(body, out_shape=jax.tree.unflatten(tree, shapes), in_specs...]
    all_to_all x1, waiting for transfers between devices: 10.3 us -> 9.04 us  [local(): lax.all_to_all(dense.reshape(rings, MT_DEV * 8, lanes), 'shot', split_axi...]
    all_to_all x1, waiting for transfers between devices: 8.59 us -> 7.35 us  [local(): lax.all_to_all(packed, 'shot', split_axis=0, concat_axis=0, tiled=True)]
  transfers between devices with their start and end apart: 5 -> 5, of which waited for: 5 -> 5; matrix products, arithmetic and copies ran while one was open for 2% -> 2% of each run, Pallas kernels for 13% -> 17%
where the time goes in v5:
time: 105 us
  Pallas kernels  31.2 us (30%)
  blocking collectives  23.8 us (23%)
  waiting for transfers between devices  22.7 us (22%)
  starting transfers between devices  22 us (21%)
  local copies, waits for them, and re-layouts  3.26 us (3%)
    pallas_call x9, Pallas kernels, run(): pl.pallas_call(body, out_shape=jax.tree.unflatten(tree, shapes), in_specs...  31.2 us
    all_to_all x1, blocking collectives, local(): lax.all_to_all(send.reshape(CLASSES, per_class * 8, lanes), 'shot', split...  23.8 us
    all_to_all x1, starting transfers between devices, local(): lax.all_to_all(packed, 'shot', split_axis=0, concat_axis=0, tiled=True)  17 us
    all_to_all x1, waiting for transfers between devices, local(): lax.all_to_all(dense.reshape(rings, MT_DEV * 8, lanes), 'shot', split_axi...  9.04 us
    all_to_all x1, waiting for transfers between devices, local(): lax.all_to_all(packed, 'shot', split_axis=0, concat_axis=0, tiled=True)  7.35 us
    ppermute x3, waiting for transfers between devices, swap(): return lax.ppermute(face, 'ap', [(0, 1), (1, 0)])  6.35 us
    all_to_all x1, starting transfers between devices, local(): lax.all_to_all(dense.reshape(rings, MT_DEV * 8, lanes), 'shot', split_axi...  3.75 us
    unnamed x46, local copies, waits for them, and re-layouts  3.26 us
  transfers between devices with their start and end apart: 5, of which 5 were waited for; matrix products, arithmetic and copies ran while one was open for 2% of the time, Pallas kernels for 17%

profile of v5, /device:TPU:1, one launch (start us, length us, event | category | flops | bytes accessed | tf_op | source)
XLA Modules:
  0.0 104.5 jit_solution(983729011385087564)
XLA Ops:
  0.6 0.0 copy-start.3
  0.6 2.8 %pack_traces.1 = bf16[128,2,2176]{2,1,0:T(2,128)(2,1)} custom-call(s32[1,128]{1,0:T(1,128)} %bitcast.53, s32[1,128]{1,0:T(1,128)} %bitcast.54, bf16[128,2048]{1,0:T(8,128)(2,1)} %traces_in.1), custom_call_target="tpu_custom_call" | custom-call | tf_op jit(solution)/shard_map/pack_traces/pallas_call | solution.py:73
  3.5 0.0 copy-start
  3.5 0.0 copy-start.1
  3.5 17.0 %all-to-all-start = ((bf16[128,2,2176]{2,1,0:T(2,128)(2,1)}), bf16[128,2,2176]{2,1,0:T(2,128)(2,1)}, u32[]{:S(2)}, u32[]{:S(2)}) async-start(bf16[128,2,2176]{2,1,0:T(2,128)(2,1)} %pack_traces.1), calls=%async_computation | async-start | bytes 2228224 | tf_op jit(solution)/shard_map/all_to_all | solution.py:529
  20.5 0.0 copy-start.5
  20.5 1.2 %copy-done.5 = f32[1,32,64,128]{3,2,1,0:T(8,128)S(1)} copy-done((f32[1,32,64,128]{3,2,1,0:T(8,128)S(1)}, f32[1,32,64,128]{3,2,1,0:T(8,128)}, u32[]{:S(2)}) %copy-start.5) | copy-done | bytes 1048600
  21.7 1.9 %faces.1 = f32[64,128]{1,0:T(8,128)S(1)} custom-call(f32[32,64,128]{2,1,0:T(8,128)S(1)} %bitcast.35, f32[32,64,128]{2,1,0:T(8,128)S(1)} %bitcast.31, f32[32,64,128]{2,1,0:T(8,128)S(1)} %bitcast.26, f32[32,64,128]{2,1,0:T(8,128)S(1)} %bitcast.38), custom_call_target="tpu_custom_call" | custom-call | tf_op jit(solution)/shard_map/faces/pallas_call | solution.py:73
  23.7 0.5 collective-permute-start
  24.1 3.0 %collective-permute-done.faces.refs_0_ = f32[64,128]{1,0:T(8,128)S(1)} collective-permute-done((f32[64,128]{1,0:T(8,128)S(1)}, f32[64,128]{1,0:T(8,128)S(1)}, u32[]{:S(2)}, u32[]{:S(2)}) %collective-permute-start) | collective-permute-done | bytes 32800 | tf_op jit(solution)/shard_map/ppermute | solution.py:484
  27.1 0.0 copy-start.4
  27.2 8.1 %first_step.1 = (f32[32,64,128]{2,1,0:T(8,128)}, f32[32,64,128]{2,1,0:T(8,128)S(1)}, f32[32,64,128]{2,1,0:T(8,128)}, f32[64,128]{1,0:T(8,128)S(1)}) custom-call(f32[64,128]{1,0:T(8,128)S(1)} %collective-permute-done.faces.refs_0_, f32[32,64,128]{2,1,0:T(8,128)S(1)} %bitcast.36, f32[32,64,128]{2,1,0:T(8,128)S(1)} %bitcast.45, f32[32,64,128]{2,1,0:T(8,128)S(1)} %bitcast.27, ...), custom_call_target="tpu_custom_call" | custom-call | tf_op jit(solution)/shard_map/first_step/pallas_call | solution.py:73
  35.2 0.4 collective-permute-start.1
  35.6 2.9 %collective-permute-done.1.mid_face.refs_1_ = f32[64,128]{1,0:T(8,128)S(1)} collective-permute-done((f32[64,128]{1,0:T(8,128)S(1)}, f32[64,128]{1,0:T(8,128)S(1)}, u32[]{:S(2)}, u32[]{:S(2)}) %collective-permute-start.1) | collective-permute-done | bytes 32800 | tf_op jit(solution)/shard_map/ppermute | solution.py:484
  38.5 0.0 copy-start.19
  38.5 0.0 copy-start.20
  38.5 3.9 %second_step.1 = (f32[32,64,128]{2,1,0:T(8,128)}, f32[32,64,128]{2,1,0:T(8,128)S(1)}) custom-call(f32[64,128]{1,0:T(8,128)S(1)} %collective-permute-done.faces.refs_0_, f32[64,128]{1,0:T(8,128)S(1)} %collective-permute-done.1.mid_face.refs_1_, f32[32,64,128]{2,1,0:T(8,128)S(1)} %get-tuple-element.23.mid, f32[32,64,128]{2,1,0:T(8,128)S(1)} %bitcast.37, ...), custom_call_target="tpu_custom_call" | custom-call | tf_op jit(solution)/shard_map/second_step/pallas_call | solution.py:73
  42.4 0.0 copy-start.8
  42.4 2.4 %places.1 = (f32[256,384]{1,0:T(8,128)S(1)}, bf16[64,256]{1,0:T(8,128)(2,1)}, s32[1,256]{1,0:T(1,128)}, bf16[16,256]{1,0:T(8,128)(2,1)}, f32[256,128]{1,0:T(8,128)}, /*index=5*/f32[16,128]{1,0:T(8,128)}) custom-call(s32[1,256]{1,0:T(1,128)S(1)} %copy-done.16, s32[1,256]{1,0:T(1,128)S(1)} %copy-done.16, f32[2048,128]{1,0:T(8,128)S(1)} %bitcast.42, ...), custom_call_target="tpu_custom_call" | custom-call | tf_op jit(solution)/shard_map/places/pallas_call | solution.py:73
  44.8 7.3 %all-to-all-done.refs_0_ = bf16[128,2,2176]{2,1,0:T(2,128)(2,1)} async-done(((bf16[128,2,2176]{2,1,0:T(2,128)(2,1)}), bf16[128,2,2176]{2,1,0:T(2,128)(2,1)}, u32[]{:S(2)}, u32[]{:S(2)}) %all-to-all-start) | async-done | bytes 1114144 | tf_op jit(solution)/shard_map/all_to_all | solution.py:529
  52.2 2.5 %residual.1 = (f32[256,128]{1,0:T(8,128)S(1)}, f32[256,128]{1,0:T(8,128)S(1)}, f32[64,128]{1,0:T(8,128)S(1)}) custom-call(bf16[128,2,2176]{2,1,0:T(2,128)(2,1)} %all-to-all-done.refs_0_, bf16[2,2048]{1,0:T(2,128)(2,1)} %bitcast.52, f32[256,384]{1,0:T(8,128)S(1)} %get-tuple-element.25.refs_2_, bf16[64,256]{1,0:T(8,128)(2,1)} %get-tuple-element.26.refs_3_), custom_call_target="tpu_custom_call" | custom-call | tf_op jit(solution)/shard_map/residual/pallas_call | solution.py:73
  54.8 0.5 collective-permute-start.2
  55.3 1.9 %inject.1 = (f32[2048,128]{1,0:T(8,128)S(1)}, f32[2048,128]{1,0:T(8,128)S(1)}) custom-call(s32[1,256]{1,0:T(1,128)S(1)} %copy-done.16, f32[256,128]{1,0:T(8,128)S(1)} %get-tuple-element.28.sum_mid, f32[256,128]{1,0:T(8,128)S(1)} %get-tuple-element.29.sum_end, f32[2048,128]{1,0:T(8,128)S(1)} %bitcast.44), custom_call_target="tpu_custom_call" | custom-call | tf_op jit(solution)/shard_map/inject/pallas_call | solution.py:73
  57.1 0.5 collective-permute-done.2.refs_2_
  57.7 5.2 %image.1 = (f32[32,64,128]{2,1,0:T(8,128)S(1)}, s16[528,8,128]{2,1,0:T(8,128)(2,1)S(1)}) custom-call(f32[64,128]{1,0:T(8,128)S(1)} %copy-done.12, f32[64,128]{1,0:T(8,128)S(1)} %copy-done.15, f32[64,128]{1,0:T(8,128)S(1)} %collective-permute-done.2.refs_2_, f32[32,64,128]{2,1,0:T(8,128)S(1)} %bitcast.47, f32[32,64,128]{2,1,0:T(8,128)S(1)} %bitcast.48, ...), custom_call_target="tpu_custom_call" | custom-call | tf_op jit(solution)/shard_map/image/pallas_call | solution.py:73
  62.9 23.8 %all_to_all.15 = s16[16,264,128]{2,1,0:T(8,128)(2,1)S(1)} all-to-all(s16[16,264,128]{2,1,0:T(8,128)(2,1)S(1)} %bitcast.43), channel_id=1, replica_groups={{0,2,4,6,8,10,12,14,16,18,20,22,24,26,28,30},{32,34,36,38,40,42,44,46,4..., dimensions={0} | all-to-all | bytes 2162688 | tf_op jit(solution)/shard_map/all_to_all | solution.py:590
  86.8 2.4 %combine.1 = f32[64,8,128]{2,1,0:T(8,128)} custom-call(s16[528,8,128]{2,1,0:T(8,128)(2,1)S(1)} %bitcast.41), custom_call_target="tpu_custom_call" | custom-call | tf_op jit(solution)/shard_map/combine/pallas_call | solution.py:73
  89.2 3.8 %all-to-all-start.2 = ((f32[8,64,128]{2,1,0:T(8,128)}), f32[8,64,128]{2,1,0:T(8,128)S(1)}, u32[]{:S(2)}, u32[]{:S(2)}) async-start(f32[8,64,128]{2,1,0:T(8,128)} %bitcast.19), calls=%async_computation.2 | async-start | bytes 524288 | tf_op jit(solution)/shard_map/all_to_all | solution.py:613
  92.9 1.0 copy.16
  93.9 1.0 copy.17
  94.9 9.0 %all-to-all-done.2 = f32[8,64,128]{2,1,0:T(8,128)S(1)} async-done(((f32[8,64,128]{2,1,0:T(8,128)}), f32[8,64,128]{2,1,0:T(8,128)S(1)}, u32[]{:S(2)}, u32[]{:S(2)}) %all-to-all-start.2) | async-done | bytes 262176 | tf_op jit(solution)/shard_map/all_to_all | solution.py:613
  103.9 0.6 reduce_sum.9
  (35 shorter events, 0.1 us)
Async XLA Ops:
  0.6 19.8 %copy-start.3 = (f32[1,32,64,128]{3,2,1,0:T(8,128)S(1)}, f32[1,32,64,128]{3,2,1,0:T(8,128)}, u32[]{:S(2)}) copy-start(f32[1,32,64,128]{3,2,1,0:T(8,128)} %param.14) | copy-start | bytes 3145732
  3.5 17.0 %copy-start = (f32[1,32,64,128]{3,2,1,0:T(8,128)S(1)}, f32[1,32,64,128]{3,2,1,0:T(8,128)}, u32[]{:S(2)}) copy-start(f32[1,32,64,128]{3,2,1,0:T(8,128)} %param.17) | copy-start | bytes 3145732
  3.5 17.0 %copy-start.1 = (f32[1,32,64,128]{3,2,1,0:T(8,128)S(1)}, f32[1,32,64,128]{3,2,1,0:T(8,128)}, u32[]{:S(2)}) copy-start(f32[1,32,64,128]{3,2,1,0:T(8,128)} %param.18) | copy-start | bytes 3145732
  3.5 48.7 %all-to-all-start = ((bf16[128,2,2176]{2,1,0:T(2,128)(2,1)}), bf16[128,2,2176]{2,1,0:T(2,128)(2,1)}, u32[]{:S(2)}, u32[]{:S(2)}) async-start(bf16[128,2,2176]{2,1,0:T(2,128)(2,1)} %pack_traces.1), calls=%async_computation | async-start | bytes 2228224 | tf_op jit(solution)/shard_map/all_to_all | solution.py:529
  20.5 1.2 %copy-start.5 = (f32[1,32,64,128]{3,2,1,0:T(8,128)S(1)}, f32[1,32,64,128]{3,2,1,0:T(8,128)}, u32[]{:S(2)}) copy-start(f32[1,32,64,128]{3,2,1,0:T(8,128)} %param.16) | copy-start | bytes 3145732
  21.7 5.4 %copy-start.6 = (f32[1,32,64,128]{3,2,1,0:T(8,128)S(1)}, f32[1,32,64,128]{3,2,1,0:T(8,128)}, u32[]{:S(2)}) copy-start(f32[1,32,64,128]{3,2,1,0:T(8,128)} %param.16) | copy-start | bytes 3145732
  21.7 5.4 %copy-start.9 = (f32[1,32,64,128]{3,2,1,0:T(8,128)S(1)}, f32[1,32,64,128]{3,2,1,0:T(8,128)}, u32[]{:S(2)}) copy-start(f32[1,32,64,128]{3,2,1,0:T(8,128)} %param.13) | copy-start | bytes 3145732
  21.7 5.4 %copy-start.10 = (f32[1,32,64,128]{3,2,1,0:T(8,128)S(1)}, f32[1,32,64,128]{3,2,1,0:T(8,128)}, u32[]{:S(2)}) copy-start(f32[1,32,64,128]{3,2,1,0:T(8,128)} %param.15) | copy-start | bytes 3145732
  23.7 3.5 %collective-permute-start = (f32[64,128]{1,0:T(8,128)S(1)}, f32[64,128]{1,0:T(8,128)S(1)}, u32[]{:S(2)}, u32[]{:S(2)}) collective-permute-start(f32[64,128]{1,0:T(8,128)S(1)} %faces.1), channel_id=1, source_target_pairs={{0,1},{1,0},{2,3},{3,2},{4,5},{5,4},{6,7},{7,6},{8,9},{9,8},{10,11... | collective-permute-start | bytes 98312 | tf_op jit(solution)/shard_map/ppermute | solution.py:484
  27.1 11.3 %copy-start.11 = (f32[64,128]{1,0:T(8,128)}, f32[64,128]{1,0:T(8,128)S(1)}, u32[]{:S(2)}) copy-start(f32[64,128]{1,0:T(8,128)S(1)} %collective-permute-done.faces.refs_0_) | copy-start | bytes 98308
  27.1 11.3 %copy-start.4 = (f32[1,32,64,128]{3,2,1,0:T(8,128)S(1)}, f32[1,32,64,128]{3,2,1,0:T(8,128)}, u32[]{:S(2)}) copy-start(f32[1,32,64,128]{3,2,1,0:T(8,128)} %param.14) | copy-start | bytes 3145732
  35.2 3.2 %collective-permute-start.1 = (f32[64,128]{1,0:T(8,128)S(1)}, f32[64,128]{1,0:T(8,128)S(1)}, u32[]{:S(2)}, u32[]{:S(2)}) collective-permute-start(f32[64,128]{1,0:T(8,128)S(1)} %get-tuple-element.22), channel_id=1, source_target_pairs={{0,1},{1,0},{2,3},{3,2},{4,5},{5,4},{6,7},{7,6},{8,9},{9,8},{10,11... | collective-permute-start | bytes 98312 | tf_op jit(solution)/shard_map/ppermute | solution.py:484
  38.5 3.9 %copy-start.14 = (f32[64,128]{1,0:T(8,128)}, f32[64,128]{1,0:T(8,128)S(1)}, u32[]{:S(2)}) copy-start(f32[64,128]{1,0:T(8,128)S(1)} %collective-permute-done.1.mid_face.refs_1_) | copy-start | bytes 98308
  38.5 3.9 %copy-start.16 = (s32[1,256]{1,0:T(1,128)S(1)}, s32[1,256]{1,0:T(1,128)}, u32[]{:S(2)}) copy-start(s32[1,256]{1,0:T(1,128)} %at.3) | copy-start | bytes 3076
  38.5 3.9 %copy-start.19 = (s32[256,1]{0,1:T(1,128)S(1)}, s32[256,1]{0,1:T(1,128)}, u32[]{:S(2)}) copy-start(s32[256,1]{0,1:T(1,128)} %param.24) | copy-start | bytes 3076
  38.5 3.9 %copy-start.20 = (s32[256]{0:T(256)S(1)}, s32[256]{0:T(256)}, u32[]{:S(2)}) copy-start(s32[256]{0:T(256)} %param.25) | copy-start | bytes 3076
  42.4 12.9 %copy-start.8 = (f32[32,64,128]{2,1,0:T(8,128)S(1)}, f32[32,64,128]{2,1,0:T(8,128)}, u32[]{:S(2)}) copy-start(f32[32,64,128]{2,1,0:T(8,128)} %get-tuple-element.30) | copy-start | bytes 3145732
  52.2 5.4 %copy-start.2 = (f32[1,32,64,128]{3,2,1,0:T(8,128)S(1)}, f32[1,32,64,128]{3,2,1,0:T(8,128)}, u32[]{:S(2)}) copy-start(f32[1,32,64,128]{3,2,1,0:T(8,128)} %param.18) | copy-start | bytes 3145732
  52.2 5.4 %copy-start.7 = (f32[1,32,64,128]{3,2,1,0:T(8,128)S(1)}, f32[1,32,64,128]{3,2,1,0:T(8,128)}, u32[]{:S(2)}) copy-start(f32[1,32,64,128]{3,2,1,0:T(8,128)} %param.16) | copy-start | bytes 3145732
  52.2 5.4 %copy-start.12 = (f32[64,128]{1,0:T(8,128)S(1)}, f32[64,128]{1,0:T(8,128)}, u32[]{:S(2)}) copy-start(f32[64,128]{1,0:T(8,128)} %copy-done.11) | copy-start | bytes 98308
  52.2 5.5 %copy-start.13 = (f32[256,128]{1,0:T(8,128)S(1)}, f32[256,128]{1,0:T(8,128)}, u32[]{:S(2)}) copy-start(f32[256,128]{1,0:T(8,128)} %get-tuple-element.37.refs_12_) | copy-start | bytes 393220
  52.2 5.5 %copy-start.15 = (f32[64,128]{1,0:T(8,128)S(1)}, f32[64,128]{1,0:T(8,128)}, u32[]{:S(2)}) copy-start(f32[64,128]{1,0:T(8,128)} %copy-done.14) | copy-start | bytes 98308
  52.2 5.5 %copy-start.17 = (bf16[16,256]{1,0:T(8,128)(2,1)S(1)}, bf16[16,256]{1,0:T(8,128)(2,1)}, u32[]{:S(2)}) copy-start(bf16[16,256]{1,0:T(8,128)(2,1)} %get-tuple-element.36.refs_11_) | copy-start | bytes 24580
  52.2 5.5 %copy-start.18 = (f32[16,128]{1,0:T(8,128)S(1)}, f32[16,128]{1,0:T(8,128)}, u32[]{:S(2)}) copy-start(f32[16,128]{1,0:T(8,128)} %get-tuple-element.38.refs_13_) | copy-start | bytes 24580
  52.2 5.5 %copy-start.21 = (s32[1,256]{1,0:T(1,128)S(1)}, s32[1,256]{1,0:T(1,128)}, u32[]{:S(2)}) copy-start(s32[1,256]{1,0:T(1,128)} %get-tuple-element.35.refs_10_) | copy-start | bytes 3076
  54.8 2.9 %collective-permute-start.2 = (f32[64,128]{1,0:T(8,128)S(1)}, f32[64,128]{1,0:T(8,128)S(1)}, u32[]{:S(2)}, u32[]{:S(2)}) collective-permute-start(f32[64,128]{1,0:T(8,128)S(1)} %get-tuple-element.27), channel_id=1, source_target_pairs={{0,1},{1,0},{2,3},{3,2},{4,5},{5,4},{6,7},{7,6},{8,9},{9,8},{10,11... | collective-permute-start | bytes 98312 | tf_op jit(solution)/shard_map/ppermute | solution.py:484
  89.2 14.7 %all-to-all-start.2 = ((f32[8,64,128]{2,1,0:T(8,128)}), f32[8,64,128]{2,1,0:T(8,128)S(1)}, u32[]{:S(2)}, u32[]{:S(2)}) async-start(f32[8,64,128]{2,1,0:T(8,128)} %bitcast.19), calls=%async_computation.2 | async-start | bytes 524288 | tf_op jit(solution)/shard_map/all_to_all | solution.py:613

commit v6 on v5

--- a/solution.py
+++ b/solution.py
@@ -11,7 +11,9 @@
 MT_DEV = 8
 CAP = 2
 CAPT = 4
-CLASSES = 16
+CLASSES = 32
+CLASS_SHIFT = 5
+RINGS = 4
 CODE_ZERO = 4096.0
 VMEM_LIMIT = 6 * 1024 * 1024
 
@@ -237,61 +239,38 @@
     lax.fori_loop(0, count, body, buoy[0] * mid[0], unroll=4)
 
 
-PACK_CHUNK = 512
-
-
-def pack_traces_kernel(groups_in, receivers_in, traces_in, out, groups, receivers, traces, made, sems):
+def pack_traces_kernel(groups_in, receivers_in, traces_in, out, groups, receivers, traces, sems):
+    copies = [
+        pltpu.make_async_copy(src, dst, sems.at[i])
+        for i, (src, dst) in enumerate(
+            ((groups_in, groups), (receivers_in, receivers), (traces_in, traces))
+        )
+    ]
+    for copy in copies:
+        copy.start()
     shots, cap, wide = out.shape
     slots = shots * cap
     count, samples = traces.shape
-    starts = range(0, samples, PACK_CHUNK)
-    small = [
-        pltpu.make_async_copy(groups_in, groups, sems.at[0]),
-        pltpu.make_async_copy(receivers_in, receivers, sems.at[1]),
-    ]
-    loads = []
-    for i, start in enumerate(starts):
-        part = pl.ds(start, PACK_CHUNK)
-        loads.append(
-            pltpu.make_async_copy(traces_in.at[:, part], traces.at[:, part], sems.at[2 + i])
-        )
-    for copy in small + loads:
-        copy.start()
-    small[0].wait()
+    copies[0].wait()
     keys = groups[...]
     place = keys.astype(F32) * CAP + rank_row(keys)
     chosen = (iota((slots, count), 0).astype(F32) == place).astype(F32).astype(BF16)
-    small[1].wait()
+    copies[1].wait()
     ids = as_column(receivers[...].astype(F32))
     ids = jnp.where(iota((count, 128), 1) == 0, ids, 0.0).astype(BF16)
     named = jnp.dot(chosen, ids, preferred_element_type=F32).astype(BF16)
-    made[:, :, samples:] = named.reshape(shots, cap, wide - samples)
-    stores = []
-
-    def send(start, width):
-        part = pl.ds(start, width)
-        copy = pltpu.make_async_copy(
-            made.at[:, :, part], out.at[:, :, part], sems.at[2 + len(loads) + len(stores)]
-        )
-        copy.start()
-        stores.append(copy)
-
-    send(samples, wide - samples)
-    for load, start in zip(loads, starts):
-        load.wait()
-        moved = jnp.dot(
-            chosen, traces[:, start : start + PACK_CHUNK], preferred_element_type=F32
-        ).astype(BF16)
-        made[:, :, start : start + PACK_CHUNK] = moved.reshape(shots, cap, PACK_CHUNK)
-        send(start, PACK_CHUNK)
-    for copy in stores:
-        copy.wait()
+    out[:, :, samples:] = named.reshape(shots, cap, wide - samples)
+    copies[2].wait()
+    moved = jnp.dot(chosen, traces[...], preferred_element_type=F32).astype(BF16)
+    out[:, :, :samples] = moved.reshape(shots, cap, samples)
 
 
 def places_kernel(
     at, cells, mid, end, bulk, owners, slots, about_out, hot_second_out, place_out, cls_out,
-    spot_out, ids_out, rows_mid, rows_end, rows_bulk,
+    spot_out, ids_out, end_out, rows_mid, rows_end, rows_bulk, sem,
 ):
+    keep_end = pltpu.make_async_copy(end, end_out, sem)
+    keep_end.start()
     low = which_half()
     lanes = 128
     count = cells.shape[1]
@@ -325,8 +304,8 @@
     tiles = owner.shape[1]
     rank = rank_row(owner).astype(I32)
     cls = owner & (CLASSES - 1)
-    spot = lax.shift_right_logical(owner, 4) * CAPT + rank
-    per_class = 8 * CAPT
+    spot = lax.shift_right_logical(owner, CLASS_SHIFT) * CAPT + rank
+    per_class = RINGS * CAPT
     place_out[...] = cls * (per_class + 1) + spot
     cls_hot = (iota((CLASSES, tiles), 0) == cls).astype(F32).astype(BF16)
     cls_out[...] = cls_hot
@@ -336,6 +315,7 @@
     ids_out[...] = jnp.dot(
         cls_hot, (spot_hot * slot_col).astype(BF16), preferred_element_type=F32
     )
+    keep_end.wait()
 
 
 def residual_kernel(rows_in, filters, about, hot_second, sum_mid, sum_end, face_out):
@@ -381,7 +361,7 @@
 
 def image_kernel(
     arrived, faces, mid_face, adj_face, mid, add, nxt, bulk, buoy, lap_mid, lap_now, place, cls_hot, spot_hot, ids,
-    last_out, send_out, codes, scaled_face,
+    last_out, send_out, codes, scaled_face, last_held, sem,
 ):
     low = which_half()
     count, rows, lanes = mid.shape
@@ -406,14 +386,16 @@
             flux,
             side_sums,
         )
-        last_out[x] = 2.0 * here - nxt[x] + (0.5 * STEP) * lap + add[x]
+        last_held[x] = 2.0 * here - nxt[x] + (0.5 * STEP) * lap + add[x]
         return flux
 
     lax.fori_loop(0, count, body, buoy[0] * (bulk[0] * mid[0]), unroll=4)
+    keep_last = pltpu.make_async_copy(last_held, last_out, sem)
+    keep_last.start()
     arrived()
 
     def pack(x, carry):
-        image = mid[x] * lap_mid[x] + last_out[x] * lap_now[x]
+        image = mid[x] * lap_mid[x] + last_held[x] * lap_now[x]
         image = (STEP * image).reshape(tiles, 8, lanes)
         peak = jnp.max(jnp.max(jnp.abs(image), axis=1), axis=1, keepdims=True)
         code = jnp.ceil(16.0 * jnp.log2(jnp.maximum(peak, 1e-30))) + 1.0
@@ -442,12 +424,12 @@
             jnp.where(place_row == 1, sent[c : c + 1, :], 0.0),
         )
         send_out[c * per_class + per_class - 1] = tile.astype(I32).astype(jnp.int16)
-
-
-def combine_kernel(got, out, gains_v, slots_v, gains, slots, sems, *partial):
+    keep_last.wait()
+
+
+def combine_kernel(got, keep_out, send_out, gains_v, slots_v, gains, slots, sems, total, *partial):
     per_class = got.shape[0] // CLASSES
     used = per_class - 1
-    lanes = got.shape[2]
     for c in range(CLASSES):
         meta = got[c * per_class + used].astype(I32)
         slots_v[c : c + 1, :] = meta[0:1, :]
@@ -467,17 +449,30 @@
 
     def body(src, carry):
         for s in range(used):
-            part = partial[s % CAPT]
-            at = (s // CAPT) * MT_DEV + slots[src, s]
+            ring, rank = s // CAPT, s % CAPT
+            part = partial[(ring % 2) * CAPT + rank]
+            at = (ring // 2) * MT_DEV + slots[src, s]
             value = got[src * per_class + s].astype(I32).astype(F32) * gains[src, s]
             part[at] = part[at] + value
         return carry
 
-    lax.fori_loop(0, CLASSES, body, 0)
-    total = partial[0][...]
-    for part in partial[1:]:
-        total = total + part[...]
-    out[...] = total
+    lax.fori_loop(0, CLASSES, body, 0, unroll=2)
+    for ring in range(RINGS):
+        own = slice((ring // 2) * MT_DEV, (ring // 2 + 1) * MT_DEV)
+        parts = [partial[(ring % 2) * CAPT + rank][own] for rank in range(CAPT)]
+        total[ring * MT_DEV : (ring + 1) * MT_DEV] = (parts[0] + parts[1]) + (parts[2] + parts[3])
+    low_bit = lax.shift_right_logical(lax.axis_index("shot"), CLASS_SHIFT) & 1
+    for high in range(RINGS // 2):
+        here = slice(high * MT_DEV, (high + 1) * MT_DEV)
+        keep_out[here] = total[pl.ds((2 * high + low_bit) * MT_DEV, MT_DEV)]
+        send_out[here] = total[pl.ds((2 * high + 1 - low_bit) * MT_DEV, MT_DEV)]
+
+
+def fold_kernel(kept, came, keep_out, send_out):
+    bit = lax.shift_right_logical(lax.axis_index("shot"), CLASS_SHIFT + 1)
+    own, other = pl.ds(bit * MT_DEV, MT_DEV), pl.ds((1 - bit) * MT_DEV, MT_DEV)
+    keep_out[...] = kept[own] + came[own]
+    send_out[...] = kept[other] + came[other]
 
 
 def swap(face):
@@ -500,7 +495,8 @@
     tile_slot,
 ):
     shots = lax.axis_size("shot")
-    rings = shots // CLASSES
+    rings = RINGS
+    assert shots == RINGS * CLASSES
     prev, now, late, nxt = wave_prev[0], wave_now[0], adjoint_late[0], adjoint_next[0]
     bulk, buoy = bulk[0], buoyancy[0]
     count, rows, lanes = now.shape
@@ -518,11 +514,10 @@
             pltpu.VMEM((1, own_rows), I32),
             pltpu.VMEM((1, own_rows), I32),
             pltpu.VMEM((own_rows, samples), BF16),
-            pltpu.VMEM((shots, CAP, samples + 128), BF16),
-            pltpu.SemaphoreType.DMA((3 + 2 * (samples // PACK_CHUNK),)),
+            pltpu.SemaphoreType.DMA((3,)),
         ],
         hbm=(0, 1, 2),
-        raw_out=(0,),
+        hbm_out=(0,),
     )(
         trace_group.reshape(1, -1), trace_receiver.reshape(1, -1), traces
     )
@@ -541,7 +536,7 @@
     receivers = receiver_cell.shape[1]
     tiles = tile_owner.shape[0]
     per_receiver = pltpu.VMEM((receivers, lanes), F32)
-    about, hot_second, place, cls_hot, spot_hot, ids = call(
+    about, hot_second, place, cls_hot, spot_hot, ids, wave_end = call(
         places_kernel,
         "places",
         (
@@ -551,10 +546,12 @@
             sds((CLASSES, tiles), BF16),
             sds((tiles, lanes)),
             sds((CLASSES, lanes)),
+            flat,
         ),
-        [per_receiver] * 3,
+        [per_receiver] * 3 + [pltpu.SemaphoreType.DMA],
         smem=(0,),
         hbm_out=(1, 2, 3, 4, 5),
+        raw_out=(6,),
     )(
         receiver_cell,
         receiver_cell,
@@ -572,13 +569,19 @@
     adj_mid, adj_add = call(inject_kernel, "inject", (flat, flat), smem=(0,))(
         receiver_cell, sum_mid, sum_end, adj_base.reshape(flat.shape)
     )
-    per_class = (shots // CLASSES) * CAPT + 1
+    per_class = rings * CAPT + 1
     adj_end, send = call(
         image_kernel,
         "image",
         (field, sds((CLASSES * per_class, 8, lanes), jnp.int16)),
-        [pltpu.VMEM((tiles, lanes), F32), pltpu.VMEM((rows, lanes), F32)],
+        [
+            pltpu.VMEM((tiles, lanes), F32),
+            pltpu.VMEM((rows, lanes), F32),
+            pltpu.VMEM(now.shape, F32),
+            pltpu.SemaphoreType.DMA,
+        ],
         smem=(10,),
+        raw_out=(0,),
         stage=(8, 9),
         late=True,
     )(
@@ -586,7 +589,6 @@
         bulk, buoy, lap_mid, lap_now, place, cls_hot, spot_hot, ids,
     )
     near = [[r * CLASSES + c for c in range(CLASSES)] for r in range(rings)]
-    far = [[r * CLASSES + c for r in range(rings)] for c in range(CLASSES)]
     got = lax.all_to_all(
         send.reshape(CLASSES, per_class * 8, lanes),
         "shot",
@@ -595,31 +597,28 @@
         axis_index_groups=near,
         tiled=True,
     )
-    owned = rings * MT_DEV
     table = (CLASSES, lanes)
-    dense = call(
+    half = sds((rings // 2 * MT_DEV, 8, lanes))
+    kept, sent = call(
         combine_kernel,
         "combine",
-        sds((owned, 8, lanes)),
+        (half, half),
         [
             pltpu.VMEM(table, F32),
             pltpu.VMEM(table, I32),
             pltpu.SMEM(table, F32),
             pltpu.SMEM(table, I32),
             pltpu.SemaphoreType.DMA((2,)),
+            pltpu.VMEM((rings * MT_DEV, 8, lanes), F32),
         ]
-        + [pltpu.VMEM((owned, 8, lanes), F32)] * CAPT,
+        + [pltpu.VMEM(half.shape, F32)] * (2 * CAPT),
     )(got.reshape(CLASSES * per_class, 8, lanes))
-    shared = lax.all_to_all(
-        dense.reshape(rings, MT_DEV * 8, lanes),
-        "shot",
-        split_axis=0,
-        concat_axis=0,
-        axis_index_groups=far,
-        tiled=True,
-    )
-    model_grad = jnp.sum(shared, axis=0).reshape(MT_DEV, 8, lanes)
-    return (model_grad, wave_end[None], adj_end[None])
+    came = lax.ppermute(sent, "shot", [(i, i ^ CLASSES) for i in range(shots)])
+    quarter = sds((MT_DEV, 8, lanes))
+    kept, sent = call(fold_kernel, "fold", (quarter, quarter))(kept, came)
+    came = lax.ppermute(sent, "shot", [(i, i ^ (2 * CLASSES)) for i in range(shots)])
+    model_grad = kept + came
+    return (model_grad, wave_end.reshape(1, *now.shape), adj_end[None])
 
 
 def solution(mesh):

time: 105 us -> 104 us (level)
  local copies, waits for them, and re-layouts: 3.26 us -> 1.3 us
  blocking collectives: 23.8 us -> 25.2 us
    ppermute x0 -> x2, waiting for transfers between devices: none -> 9.68 us  [the longest x1 5.36 us: local(): came = lax.ppermute(sent, 'shot', [(i, i ^ CLASSES) for i in range(shots)])]
    all_to_all x1 -> x0, waiting for transfers between devices: 9.04 us -> none  [local(): lax.all_to_all(dense.reshape(rings, MT_DEV * 8, lanes), 'shot', split_axi...]
    all_to_all x1 -> x0, starting transfers between devices: 3.75 us -> none  [local(): lax.all_to_all(dense.reshape(rings, MT_DEV * 8, lanes), 'shot', split_axi...]
    ppermute x0 -> x2, starting transfers between devices: none -> 3.37 us  [the longest x1 2.44 us: local(): lax.ppermute(sent, 'shot', [(i, i ^ 2 * CLASSES) for i in range(shots)])]
    unnamed x46 -> x38, local copies, waits for them, and re-layouts: 3.26 us -> 1.3 us
    all_to_all x1, blocking collectives: 23.8 us -> 25.2 us  [local(): lax.all_to_all(send.reshape(CLASSES, per_class * 8, lanes), 'shot', split...]
    pallas_call x9 -> x10, Pallas kernels: 31.2 us -> 30.3 us  [run(): pl.pallas_call(body, out_shape=jax.tree.unflatten(tree, shapes), in_specs...]
  transfers between devices with their start and end apart: 5 -> 6, of which waited for: 5 -> 6; matrix products, arithmetic and copies ran while one was open for 2% -> 0% of each run, Pallas kernels for 17% -> 17%
where the time goes in v6:
time: 104 us; the launch traced here: 103 us
  Pallas kernels  30.3 us (29%)
  blocking collectives  25.2 us (24%)
  waiting for transfers between devices  23.5 us (23%)
  starting transfers between devices  21.6 us (21%)
  local copies, waits for them, and re-layouts  1.3 us (1%)
    pallas_call x10, Pallas kernels, run(): pl.pallas_call(body, out_shape=jax.tree.unflatten(tree, shapes), in_specs...  30.3 us
    all_to_all x1, blocking collectives, local(): lax.all_to_all(send.reshape(CLASSES, per_class * 8, lanes), 'shot', split...  25.2 us
    all_to_all x1, starting transfers between devices, local(): lax.all_to_all(packed, 'shot', split_axis=0, concat_axis=0, tiled=True)  16.9 us
    all_to_all x1, waiting for transfers between devices, local(): lax.all_to_all(packed, 'shot', split_axis=0, concat_axis=0, tiled=True)  7.39 us
    ppermute x3, waiting for transfers between devices, swap(): return lax.ppermute(face, 'ap', [(0, 1), (1, 0)])  6.41 us
    ppermute x1, waiting for transfers between devices, local(): came = lax.ppermute(sent, 'shot', [(i, i ^ CLASSES) for i in range(shots)])  5.36 us
    ppermute x1, waiting for transfers between devices, local(): lax.ppermute(sent, 'shot', [(i, i ^ 2 * CLASSES) for i in range(shots)])  4.32 us
    ppermute x1, starting transfers between devices, local(): lax.ppermute(sent, 'shot', [(i, i ^ 2 * CLASSES) for i in range(shots)])  2.44 us
  transfers between devices with their start and end apart: 6, of which 6 were waited for; matrix products, arithmetic and copies ran while one was open for 0% of the time, Pallas kernels for 17%

profile of v6, /device:TPU:1, one launch (start us, length us, event | category | flops | bytes accessed | tf_op | source)
XLA Modules:
  0.0 103.4 jit_solution(11885952107243518143)
XLA Ops:
  0.6 0.0 copy-start.2
  0.6 2.6 %pack_traces.1 = bf16[128,2,2176]{2,1,0:T(2,128)(2,1)} custom-call(s32[1,128]{1,0:T(1,128)} %bitcast.48, s32[1,128]{1,0:T(1,128)} %bitcast.49, bf16[128,2048]{1,0:T(8,128)(2,1)} %traces_in.1), custom_call_target="tpu_custom_call" | custom-call | tf_op jit(solution)/shard_map/pack_traces/pallas_call | solution.py:75
  3.3 0.0 copy-start
  3.3 0.0 copy-start.1
  3.3 16.9 %all-to-all-start = ((bf16[128,2,2176]{2,1,0:T(2,128)(2,1)}), bf16[128,2,2176]{2,1,0:T(2,128)(2,1)}, u32[]{:S(2)}, u32[]{:S(2)}) async-start(bf16[128,2,2176]{2,1,0:T(2,128)(2,1)} %pack_traces.1), calls=%async_computation | async-start | bytes 2228224 | tf_op jit(solution)/shard_map/all_to_all | solution.py:524
  20.3 0.0 copy-start.3
  20.3 1.2 %copy-done.3 = f32[1,32,64,128]{3,2,1,0:T(8,128)S(1)} copy-done((f32[1,32,64,128]{3,2,1,0:T(8,128)S(1)}, f32[1,32,64,128]{3,2,1,0:T(8,128)}, u32[]{:S(2)}) %copy-start.3) | copy-done | bytes 1048600
  21.5 1.9 %faces.1 = f32[64,128]{1,0:T(8,128)S(1)} custom-call(f32[32,64,128]{2,1,0:T(8,128)S(1)} %bitcast.30, f32[32,64,128]{2,1,0:T(8,128)S(1)} %bitcast.26, f32[32,64,128]{2,1,0:T(8,128)S(1)} %bitcast.21, f32[32,64,128]{2,1,0:T(8,128)S(1)} %bitcast.33), custom_call_target="tpu_custom_call" | custom-call | tf_op jit(solution)/shard_map/faces/pallas_call | solution.py:75
  23.4 0.5 collective-permute-start
  23.9 3.0 %collective-permute-done.faces.refs_0_ = f32[64,128]{1,0:T(8,128)S(1)} collective-permute-done((f32[64,128]{1,0:T(8,128)S(1)}, f32[64,128]{1,0:T(8,128)S(1)}, u32[]{:S(2)}, u32[]{:S(2)}) %collective-permute-start) | collective-permute-done | bytes 32800 | tf_op jit(solution)/shard_map/ppermute | solution.py:479
  26.9 8.0 %first_step.1 = (f32[32,64,128]{2,1,0:T(8,128)}, f32[32,64,128]{2,1,0:T(8,128)S(1)}, f32[32,64,128]{2,1,0:T(8,128)}, f32[64,128]{1,0:T(8,128)S(1)}) custom-call(f32[64,128]{1,0:T(8,128)S(1)} %collective-permute-done.faces.refs_0_, f32[32,64,128]{2,1,0:T(8,128)S(1)} %bitcast.31, f32[32,64,128]{2,1,0:T(8,128)S(1)} %bitcast.41, f32[32,64,128]{2,1,0:T(8,128)S(1)} %bitcast.22, ...), custom_call_target="tpu_custom_call" | custom-call | tf_op jit(solution)/shard_map/first_step/pallas_call | solution.py:75
  34.8 0.3 collective-permute-start.1
  35.2 2.9 %collective-permute-done.1.mid_face.refs_1_ = f32[64,128]{1,0:T(8,128)S(1)} collective-permute-done((f32[64,128]{1,0:T(8,128)S(1)}, f32[64,128]{1,0:T(8,128)S(1)}, u32[]{:S(2)}, u32[]{:S(2)}) %collective-permute-start.1) | collective-permute-done | bytes 32800 | tf_op jit(solution)/shard_map/ppermute | solution.py:479
  38.1 0.0 copy-start.17
  38.2 3.8 %second_step.1 = (f32[32,64,128]{2,1,0:T(8,128)}, f32[32,64,128]{2,1,0:T(8,128)S(1)}) custom-call(f32[64,128]{1,0:T(8,128)S(1)} %collective-permute-done.faces.refs_0_, f32[64,128]{1,0:T(8,128)S(1)} %collective-permute-done.1.mid_face.refs_1_, f32[32,64,128]{2,1,0:T(8,128)S(1)} %get-tuple-element.28.mid, f32[32,64,128]{2,1,0:T(8,128)S(1)} %bitcast.32, ...), custom_call_target="tpu_custom_call" | custom-call | tf_op jit(solution)/shard_map/second_step/pallas_call | solution.py:75
  42.0 2.5 %places.1 = (f32[256,384]{1,0:T(8,128)S(1)}, bf16[64,256]{1,0:T(8,128)(2,1)}, s32[1,256]{1,0:T(1,128)}, bf16[32,256]{1,0:T(8,128)(2,1)}, f32[256,128]{1,0:T(8,12...) custom-call(s32[1,256]{1,0:T(1,128)S(1)} %copy-done.15, s32[1,256]{1,0:T(1,128)S(1)} %copy-done.15, f32[2048,128]{1,0:T(8,128)S(1)} %bitcast.37, ...), custom_call_target="tpu_custom_call" | custom-call | tf_op jit(solution)/shard_map/places/pallas_call | solution.py:75
  44.5 0.0 copy-start.5
  44.5 7.4 %all-to-all-done.refs_0_ = bf16[128,2,2176]{2,1,0:T(2,128)(2,1)} async-done(((bf16[128,2,2176]{2,1,0:T(2,128)(2,1)}), bf16[128,2,2176]{2,1,0:T(2,128)(2,1)}, u32[]{:S(2)}, u32[]{:S(2)}) %all-to-all-start) | async-done | bytes 1114144 | tf_op jit(solution)/shard_map/all_to_all | solution.py:524
  51.9 0.0 copy-start.13
  52.0 0.0 copy-start.14
  52.0 2.5 %residual.1 = (f32[256,128]{1,0:T(8,128)S(1)}, f32[256,128]{1,0:T(8,128)S(1)}, f32[64,128]{1,0:T(8,128)S(1)}) custom-call(bf16[128,2,2176]{2,1,0:T(2,128)(2,1)} %all-to-all-done.refs_0_, bf16[2,2048]{1,0:T(2,128)(2,1)} %bitcast.47, f32[256,384]{1,0:T(8,128)S(1)} %get-tuple-element.30.refs_2_, bf16[64,256]{1,0:T(8,128)(2,1)} %get-tuple-element.31.refs_3_), custom_call_target="tpu_custom_call" | custom-call | tf_op jit(solution)/shard_map/residual/pallas_call | solution.py:75
  54.5 0.5 collective-permute-start.2
  54.9 1.9 %inject.1 = (f32[2048,128]{1,0:T(8,128)S(1)}, f32[2048,128]{1,0:T(8,128)S(1)}) custom-call(s32[1,256]{1,0:T(1,128)S(1)} %copy-done.15, f32[256,128]{1,0:T(8,128)S(1)} %get-tuple-element.33.sum_mid, f32[256,128]{1,0:T(8,128)S(1)} %get-tuple-element.34.sum_end, f32[2048,128]{1,0:T(8,128)S(1)} %bitcast.39), custom_call_target="tpu_custom_call" | custom-call | tf_op jit(solution)/shard_map/inject/pallas_call | solution.py:75
  56.8 0.5 collective-permute-done.2.refs_2_
  57.4 5.2 %image.1 = (f32[32,64,128]{2,1,0:T(8,128)}, s16[544,8,128]{2,1,0:T(8,128)(2,1)S(1)}) custom-call(f32[64,128]{1,0:T(8,128)S(1)} %copy-done.9, f32[64,128]{1,0:T(8,128)S(1)} %copy-done.12, f32[64,128]{1,0:T(8,128)S(1)} %collective-permute-done.2.refs_2_, f32[32,64,128]{2,1,0:T(8,128)S(1)} %bitcast.43, f32[32,64,128]{2,1,0:T(8,128)S(1)} %bitcast.44, ...), custom_call_target="tpu_custom_call" | custom-call | tf_op jit(solution)/shard_map/image/pallas_call | solution.py:75
  62.6 25.2 %all_to_all.10 = s16[32,136,128]{2,1,0:T(8,128)(2,1)S(1)} all-to-all(s16[32,136,128]{2,1,0:T(8,128)(2,1)S(1)} %bitcast.38), channel_id=1, replica_groups={{0,2,4,6,8,10,12,14,16,18,20,22,24,26,28,30,32,34,36,38,40,42,44,46,48,..., dimensions={0} | all-to-all | bytes 2228224 | tf_op jit(solution)/shard_map/all_to_all | solution.py:592
  87.8 1.9 %combine.1 = (f32[16,8,128]{2,1,0:T(8,128)S(1)}, f32[16,8,128]{2,1,0:T(8,128)S(1)}) custom-call(s16[544,8,128]{2,1,0:T(8,128)(2,1)S(1)} %bitcast.36), custom_call_target="tpu_custom_call" | custom-call | tf_op jit(solution)/shard_map/combine/pallas_call | solution.py:75
  89.8 0.9 collective-permute-start.3
  90.7 5.4 %collective-permute-done.3.came = f32[16,8,128]{2,1,0:T(8,128)S(1)} collective-permute-done((f32[16,8,128]{2,1,0:T(8,128)S(1)}, f32[16,8,128]{2,1,0:T(8,128)S(1)}, u32[]{:S(2)}, u32[]{:S(2)}) %collective-permute-start.3) | collective-permute-done | bytes 65568 | tf_op jit(solution)/shard_map/ppermute | solution.py:616
  96.1 2.4 %collective-permute-start.4 = (f32[8,8,128]{2,1,0:T(8,128)S(1)}, f32[8,8,128]{2,1,0:T(8,128)S(1)}, u32[]{:S(2)}, u32[]{:S(2)}) collective-permute-start(f32[8,8,128]{2,1,0:T(8,128)S(1)} %get-tuple-element.48), channel_id=1, source_target_pairs={{0,128},{2,130},{4,132},{6,134},{8,136},{10,138},{12,140},{14,142}... | collective-permute-start | bytes 98312 | tf_op jit(solution)/shard_map/ppermute | solution.py:619
  98.5 4.3 %collective-permute-done.4 = f32[8,8,128]{2,1,0:T(8,128)S(1)} collective-permute-done((f32[8,8,128]{2,1,0:T(8,128)S(1)}, f32[8,8,128]{2,1,0:T(8,128)S(1)}, u32[]{:S(2)}, u32[]{:S(2)}) %collective-permute-start.4) | collective-permute-done | bytes 32800 | tf_op jit(solution)/shard_map/ppermute | solution.py:619
  102.8 0.6 add.3
  (30 shorter events, 0.1 us)
Async XLA Ops:
  0.6 19.6 %copy-start.2 = (f32[1,32,64,128]{3,2,1,0:T(8,128)S(1)}, f32[1,32,64,128]{3,2,1,0:T(8,128)}, u32[]{:S(2)}) copy-start(f32[1,32,64,128]{3,2,1,0:T(8,128)} %param.14) | copy-start | bytes 3145732
  3.3 17.0 %copy-start = (f32[1,32,64,128]{3,2,1,0:T(8,128)S(1)}, f32[1,32,64,128]{3,2,1,0:T(8,128)}, u32[]{:S(2)}) copy-start(f32[1,32,64,128]{3,2,1,0:T(8,128)} %param.17) | copy-start | bytes 3145732
  3.3 17.0 %copy-start.1 = (f32[1,32,64,128]{3,2,1,0:T(8,128)S(1)}, f32[1,32,64,128]{3,2,1,0:T(8,128)}, u32[]{:S(2)}) copy-start(f32[1,32,64,128]{3,2,1,0:T(8,128)} %param.18) | copy-start | bytes 3145732
  3.3 48.7 %all-to-all-start = ((bf16[128,2,2176]{2,1,0:T(2,128)(2,1)}), bf16[128,2,2176]{2,1,0:T(2,128)(2,1)}, u32[]{:S(2)}, u32[]{:S(2)}) async-start(bf16[128,2,2176]{2,1,0:T(2,128)(2,1)} %pack_traces.1), calls=%async_computation | async-start | bytes 2228224 | tf_op jit(solution)/shard_map/all_to_all | solution.py:524
  20.3 1.2 %copy-start.3 = (f32[1,32,64,128]{3,2,1,0:T(8,128)S(1)}, f32[1,32,64,128]{3,2,1,0:T(8,128)}, u32[]{:S(2)}) copy-start(f32[1,32,64,128]{3,2,1,0:T(8,128)} %param.16) | copy-start | bytes 3145732
  21.5 5.4 %copy-start.6 = (f32[1,32,64,128]{3,2,1,0:T(8,128)S(1)}, f32[1,32,64,128]{3,2,1,0:T(8,128)}, u32[]{:S(2)}) copy-start(f32[1,32,64,128]{3,2,1,0:T(8,128)} %param.13) | copy-start | bytes 3145732
  21.5 5.4 %copy-start.7 = (f32[1,32,64,128]{3,2,1,0:T(8,128)S(1)}, f32[1,32,64,128]{3,2,1,0:T(8,128)}, u32[]{:S(2)}) copy-start(f32[1,32,64,128]{3,2,1,0:T(8,128)} %param.15) | copy-start | bytes 3145732
  23.4 3.5 %collective-permute-start = (f32[64,128]{1,0:T(8,128)S(1)}, f32[64,128]{1,0:T(8,128)S(1)}, u32[]{:S(2)}, u32[]{:S(2)}) collective-permute-start(f32[64,128]{1,0:T(8,128)S(1)} %faces.1), channel_id=1, source_target_pairs={{0,1},{1,0},{2,3},{3,2},{4,5},{5,4},{6,7},{7,6},{8,9},{9,8},{10,11... | collective-permute-start | bytes 98312 | tf_op jit(solution)/shard_map/ppermute | solution.py:479
  26.9 11.3 %copy-start.8 = (f32[64,128]{1,0:T(8,128)}, f32[64,128]{1,0:T(8,128)S(1)}, u32[]{:S(2)}) copy-start(f32[64,128]{1,0:T(8,128)S(1)} %collective-permute-done.faces.refs_0_) | copy-start | bytes 98308
  34.8 3.3 %collective-permute-start.1 = (f32[64,128]{1,0:T(8,128)S(1)}, f32[64,128]{1,0:T(8,128)S(1)}, u32[]{:S(2)}, u32[]{:S(2)}) collective-permute-start(f32[64,128]{1,0:T(8,128)S(1)} %get-tuple-element.27), channel_id=1, source_target_pairs={{0,1},{1,0},{2,3},{3,2},{4,5},{5,4},{6,7},{7,6},{8,9},{9,8},{10,11... | collective-permute-start | bytes 98312 | tf_op jit(solution)/shard_map/ppermute | solution.py:479
  38.1 3.9 %copy-start.11 = (f32[64,128]{1,0:T(8,128)}, f32[64,128]{1,0:T(8,128)S(1)}, u32[]{:S(2)}) copy-start(f32[64,128]{1,0:T(8,128)S(1)} %collective-permute-done.1.mid_face.refs_1_) | copy-start | bytes 98308
  38.1 3.9 %copy-start.15 = (s32[1,256]{1,0:T(1,128)S(1)}, s32[1,256]{1,0:T(1,128)}, u32[]{:S(2)}) copy-start(s32[1,256]{1,0:T(1,128)} %at.3) | copy-start | bytes 3076
  38.1 3.9 %copy-start.16 = (s32[256,1]{0,1:T(1,128)S(1)}, s32[256,1]{0,1:T(1,128)}, u32[]{:S(2)}) copy-start(s32[256,1]{0,1:T(1,128)} %param.24) | copy-start | bytes 3076
  38.1 3.9 %copy-start.17 = (s32[256]{0:T(256)S(1)}, s32[256]{0:T(256)}, u32[]{:S(2)}) copy-start(s32[256]{0:T(256)} %param.25) | copy-start | bytes 3076
  44.5 10.4 %copy-start.5 = (f32[32,64,128]{2,1,0:T(8,128)S(1)}, f32[32,64,128]{2,1,0:T(8,128)}, u32[]{:S(2)}) copy-start(f32[32,64,128]{2,1,0:T(8,128)} %get-tuple-element.35) | copy-start | bytes 3145732
  51.9 5.4 %copy-start.4 = (f32[1,32,64,128]{3,2,1,0:T(8,128)S(1)}, f32[1,32,64,128]{3,2,1,0:T(8,128)}, u32[]{:S(2)}) copy-start(f32[1,32,64,128]{3,2,1,0:T(8,128)} %param.16) | copy-start | bytes 3145732
  51.9 5.4 %copy-start.9 = (f32[64,128]{1,0:T(8,128)S(1)}, f32[64,128]{1,0:T(8,128)}, u32[]{:S(2)}) copy-start(f32[64,128]{1,0:T(8,128)} %copy-done.8) | copy-start | bytes 98308
  51.9 5.4 %copy-start.10 = (f32[256,128]{1,0:T(8,128)S(1)}, f32[256,128]{1,0:T(8,128)}, u32[]{:S(2)}) copy-start(f32[256,128]{1,0:T(8,128)} %get-tuple-element.42.refs_12_) | copy-start | bytes 393220
  51.9 5.4 %copy-start.12 = (f32[64,128]{1,0:T(8,128)S(1)}, f32[64,128]{1,0:T(8,128)}, u32[]{:S(2)}) copy-start(f32[64,128]{1,0:T(8,128)} %copy-done.11) | copy-start | bytes 98308
  51.9 5.4 %copy-start.13 = (bf16[32,256]{1,0:T(8,128)(2,1)S(1)}, bf16[32,256]{1,0:T(8,128)(2,1)}, u32[]{:S(2)}) copy-start(bf16[32,256]{1,0:T(8,128)(2,1)} %get-tuple-element.41.refs_11_) | copy-start | bytes 49156
  52.0 5.4 %copy-start.14 = (f32[32,128]{1,0:T(8,128)S(1)}, f32[32,128]{1,0:T(8,128)}, u32[]{:S(2)}) copy-start(f32[32,128]{1,0:T(8,128)} %get-tuple-element.43.refs_13_) | copy-start | bytes 49156
  52.0 5.4 %copy-start.18 = (s32[1,256]{1,0:T(1,128)S(1)}, s32[1,256]{1,0:T(1,128)}, u32[]{:S(2)}) copy-start(s32[1,256]{1,0:T(1,128)} %get-tuple-element.40.refs_10_) | copy-start | bytes 3076
  54.5 2.9 %collective-permute-start.2 = (f32[64,128]{1,0:T(8,128)S(1)}, f32[64,128]{1,0:T(8,128)S(1)}, u32[]{:S(2)}, u32[]{:S(2)}) collective-permute-start(f32[64,128]{1,0:T(8,128)S(1)} %get-tuple-element.32), channel_id=1, source_target_pairs={{0,1},{1,0},{2,3},{3,2},{4,5},{5,4},{6,7},{7,6},{8,9},{9,8},{10,11... | collective-permute-start | bytes 98312 | tf_op jit(solution)/shard_map/ppermute | solution.py:479
  89.8 6.3 %collective-permute-start.3 = (f32[16,8,128]{2,1,0:T(8,128)S(1)}, f32[16,8,128]{2,1,0:T(8,128)S(1)}, u32[]{:S(2)}, u32[]{:S(2)}) collective-permute-start(f32[16,8,128]{2,1,0:T(8,128)S(1)} %get-tuple-element.46), channel_id=1, source_target_pairs={{0,64},{2,66},{4,68},{6,70},{8,72},{10,74},{12,76},{14,78},{16,80}... | collective-permute-start | bytes 196616 | tf_op jit(solution)/shard_map/ppermute | solution.py:616
  96.1 6.8 %collective-permute-start.4 = (f32[8,8,128]{2,1,0:T(8,128)S(1)}, f32[8,8,128]{2,1,0:T(8,128)S(1)}, u32[]{:S(2)}, u32[]{:S(2)}) collective-permute-start(f32[8,8,128]{2,1,0:T(8,128)S(1)} %get-tuple-element.48), channel_id=1, source_target_pairs={{0,128},{2,130},{4,132},{6,134},{8,136},{10,138},{12,140},{14,142}... | collective-permute-start | bytes 98312 | tf_op jit(solution)/shard_map/ppermute | solution.py:619

commit v7 on v6

--- a/solution.py
+++ b/solution.py
@@ -239,7 +239,9 @@
     lax.fori_loop(0, count, body, buoy[0] * mid[0], unroll=4)
 
 
-def pack_traces_kernel(groups_in, receivers_in, traces_in, out, groups, receivers, traces, sems):
+def pack_traces_kernel(
+    groups_in, receivers_in, traces_in, out, groups, receivers, traces, made, sems
+):
     copies = [
         pltpu.make_async_copy(src, dst, sems.at[i])
         for i, (src, dst) in enumerate(
@@ -259,10 +261,18 @@
     ids = as_column(receivers[...].astype(F32))
     ids = jnp.where(iota((count, 128), 1) == 0, ids, 0.0).astype(BF16)
     named = jnp.dot(chosen, ids, preferred_element_type=F32).astype(BF16)
-    out[:, :, samples:] = named.reshape(shots, cap, wide - samples)
+    made[:, :, samples:] = named.reshape(shots, cap, wide - samples)
     copies[2].wait()
-    moved = jnp.dot(chosen, traces[...], preferred_element_type=F32).astype(BF16)
-    out[:, :, :samples] = moved.reshape(shots, cap, samples)
+    stores = []
+    for n in range(2):
+        part = slice(n * slots // 2, (n + 1) * slots // 2)
+        dest = pl.ds(n * shots // 2, shots // 2)
+        moved = jnp.dot(chosen[part], traces[...], preferred_element_type=F32).astype(BF16)
+        made[dest, :, :samples] = moved.reshape(shots // 2, cap, samples)
+        stores.append(pltpu.make_async_copy(made.at[dest], out.at[dest], sems.at[3 + n]))
+        stores[-1].start()
+    for copy in stores:
+        copy.wait()
 
 
 def places_kernel(
@@ -318,26 +328,42 @@
     keep_end.wait()
 
 
-def residual_kernel(rows_in, filters, about, hot_second, sum_mid, sum_end, face_out):
+def residual_kernel(
+    arrived, rows_in, filters, about, hot_second, sum_mid, sum_end, face_out, held, sems
+):
+    shots, cap, wide = rows_in.shape
+    parts = sems.shape[0]
+    each = shots // parts
+    copies = []
+    for n in range(parts):
+        part = pl.ds(n * each, each)
+        copies.append(pltpu.make_async_copy(rows_in.at[part], held.at[part], sems.at[n]))
+        copies[-1].start()
     samples = filters.shape[1]
     count, lanes = sum_mid.shape
-    slots = rows_in.shape[0] * rows_in.shape[1]
+    slots = each * cap
     last_dims = (((1,), (1,)), ((), ()))
-    values = lax.dot_general(
-        rows_in[:, :, :samples].reshape(slots, samples),
-        filters[...],
-        last_dims,
-        preferred_element_type=F32,
-    )
     pick = ((iota((8, 128), 0) == 0) & (iota((8, 128), 1) == 0)).astype(F32).astype(BF16)
-    ids = lax.dot_general(
-        pick,
-        rows_in[:, :, samples:].reshape(slots, rows_in.shape[2] - samples),
-        last_dims,
-        preferred_element_type=F32,
-    )
-    hot = (iota((count, slots), 0).astype(F32) == ids[0:1, :]).astype(F32).astype(BF16)
-    observed = exact_dot(hot, values)
+    receiver = iota((count, slots), 0).astype(F32)
+    observed = jnp.zeros((count, filters.shape[0]), F32)
+    arrived()
+    for n in range(parts):
+        copies[n].wait()
+        here = slice(n * each, (n + 1) * each)
+        values = lax.dot_general(
+            held[here, :, :samples].reshape(slots, samples),
+            filters[...],
+            last_dims,
+            preferred_element_type=F32,
+        )
+        ids = lax.dot_general(
+            pick,
+            held[here, :, samples:].reshape(slots, wide - samples),
+            last_dims,
+            preferred_element_type=F32,
+        )
+        hot = (receiver == ids[0:1, :]).astype(F32).astype(BF16)
+        observed = observed + exact_dot(hot, values)
     resid_mid = about[:, 0:1] - observed[:, 0:1]
     resid_end = about[:, 1:2] - observed[:, 1:2]
     hot_depth = about[:, lanes : 2 * lanes]
@@ -368,12 +394,6 @@
     tiles = rows // 8
     per_class = send_out.shape[0] // CLASSES
     scaled_face[...] = mid_face[...] + adj_face[...]
-
-    def clear(c, carry):
-        send_out[pl.ds(c * per_class, per_class)] = jnp.zeros((per_class, 8, lanes), jnp.int16)
-        return carry
-
-    lax.fori_loop(0, CLASSES, clear, 0)
 
     def body(x, flux):
         after, keep = following(x, count)
@@ -389,7 +409,7 @@
         last_held[x] = 2.0 * here - nxt[x] + (0.5 * STEP) * lap + add[x]
         return flux
 
-    lax.fori_loop(0, count, body, buoy[0] * (bulk[0] * mid[0]), unroll=4)
+    lax.fori_loop(0, count, body, buoy[0] * (bulk[0] * mid[0]), unroll=8)
     keep_last = pltpu.make_async_copy(last_held, last_out, sem)
     keep_last.start()
     arrived()
@@ -408,7 +428,7 @@
             send_out[place[0, x * tiles + t]] = whole[t]
         return carry
 
-    lax.fori_loop(0, count, pack, 0, unroll=4)
+    lax.fori_loop(0, count, pack, 0, unroll=8)
     code = codes[...]
     upper = jnp.floor(code * (1.0 / 64.0))
     lower = code - 64.0 * upper
@@ -461,18 +481,24 @@
         own = slice((ring // 2) * MT_DEV, (ring // 2 + 1) * MT_DEV)
         parts = [partial[(ring % 2) * CAPT + rank][own] for rank in range(CAPT)]
         total[ring * MT_DEV : (ring + 1) * MT_DEV] = (parts[0] + parts[1]) + (parts[2] + parts[3])
-    low_bit = lax.shift_right_logical(lax.axis_index("shot"), CLASS_SHIFT) & 1
-    for high in range(RINGS // 2):
-        here = slice(high * MT_DEV, (high + 1) * MT_DEV)
-        keep_out[here] = total[pl.ds((2 * high + low_bit) * MT_DEV, MT_DEV)]
-        send_out[here] = total[pl.ds((2 * high + 1 - low_bit) * MT_DEV, MT_DEV)]
+    ring = lax.shift_right_logical(lax.axis_index("shot"), CLASS_SHIFT)
+
+    def owned(other):
+        return total[pl.ds((ring ^ other) * MT_DEV, MT_DEV)]
+
+    keep_out[:MT_DEV] = owned(0)
+    keep_out[MT_DEV:] = owned(3)
+    send_out[:MT_DEV] = owned(1)
+    send_out[MT_DEV:] = owned(2)
 
 
 def fold_kernel(kept, came, keep_out, send_out):
-    bit = lax.shift_right_logical(lax.axis_index("shot"), CLASS_SHIFT + 1)
-    own, other = pl.ds(bit * MT_DEV, MT_DEV), pl.ds((1 - bit) * MT_DEV, MT_DEV)
-    keep_out[...] = kept[own] + came[own]
-    send_out[...] = kept[other] + came[other]
+    keep_out[...] = kept[:MT_DEV] + came[:MT_DEV]
+    send_out[...] = kept[MT_DEV:] + came[MT_DEV:]
+
+
+def last_kernel(kept, came, out):
+    out[...] = kept[...] + came[...]
 
 
 def swap(face):
@@ -514,10 +540,11 @@
             pltpu.VMEM((1, own_rows), I32),
             pltpu.VMEM((1, own_rows), I32),
             pltpu.VMEM((own_rows, samples), BF16),
-            pltpu.SemaphoreType.DMA((3,)),
+            pltpu.VMEM((shots, CAP, samples + 128), BF16),
+            pltpu.SemaphoreType.DMA((5,)),
         ],
         hbm=(0, 1, 2),
-        hbm_out=(0,),
+        raw_out=(0,),
     )(
         trace_group.reshape(1, -1), trace_receiver.reshape(1, -1), traces
     )
@@ -563,7 +590,13 @@
     )
     spread = sds((receivers, lanes))
     sum_mid, sum_end, adj_face = call(
-        residual_kernel, "residual", (spread, spread, face), stage=(0, 1, 3)
+        residual_kernel,
+        "residual",
+        (spread, spread, face),
+        [pltpu.VMEM(got_rows.shape, BF16), pltpu.SemaphoreType.DMA((2,))],
+        hbm=(0,),
+        stage=(1, 3),
+        late=True,
     )(got_rows, group_filter[0], about, hot_second)
     adj_face = swap(adj_face)
     adj_mid, adj_add = call(inject_kernel, "inject", (flat, flat), smem=(0,))(
@@ -616,8 +649,8 @@
     came = lax.ppermute(sent, "shot", [(i, i ^ CLASSES) for i in range(shots)])
     quarter = sds((MT_DEV, 8, lanes))
     kept, sent = call(fold_kernel, "fold", (quarter, quarter))(kept, came)
-    came = lax.ppermute(sent, "shot", [(i, i ^ (2 * CLASSES)) for i in range(shots)])
-    model_grad = kept + came
+    came = lax.ppermute(sent, "shot", [(i, i ^ (3 * CLASSES)) for i in range(shots)])
+    model_grad = call(last_kernel, "last_sum", quarter, hbm_out=(0,))(kept, came)
     return (model_grad, wave_end.reshape(1, *now.shape), adj_end[None])
 
 

time: 104 us -> 102 us (0.981)
  starting transfers between devices: 21.6 us -> 19.3 us
    ppermute x1, starting transfers between devices: 2.44 us -> 0.09 us  [local(): lax.ppermute(sent, 'shot', [(i, i ^ 3 * CLASSES) for i in range(shots)])]
    pallas_call x10 -> x11, Pallas kernels: 30.3 us -> 30.6 us  [run(): pl.pallas_call(body, out_shape=jax.tree.unflatten(tree, shapes), in_specs...]
  transfers between devices with their start and end apart: 6 -> 6, of which waited for: 6 -> 6; matrix products, arithmetic and copies ran while one was open for 0% -> 0% of each run, Pallas kernels for 17% -> 18%
where the time goes in v7:
time: 102 us; the launch traced here: 101 us
  Pallas kernels  30.6 us (30%)
  blocking collectives  25.2 us (25%)
  waiting for transfers between devices  24 us (24%)
  starting transfers between devices  19.3 us (19%)
  local copies, waits for them, and re-layouts  1.3 us (1%)
    pallas_call x11, Pallas kernels, run(): pl.pallas_call(body, out_shape=jax.tree.unflatten(tree, shapes), in_specs...  30.6 us
    all_to_all x1, blocking collectives, local(): lax.all_to_all(send.reshape(CLASSES, per_class * 8, lanes), 'shot', split...  25.2 us
    all_to_all x1, starting transfers between devices, local(): lax.all_to_all(packed, 'shot', split_axis=0, concat_axis=0, tiled=True)  17 us
    all_to_all x1, waiting for transfers between devices, local(): lax.all_to_all(packed, 'shot', split_axis=0, concat_axis=0, tiled=True)  7.39 us
    ppermute x3, waiting for transfers between devices, swap(): return lax.ppermute(face, 'ap', [(0, 1), (1, 0)])  6.41 us
    ppermute x1, waiting for transfers between devices, local(): came = lax.ppermute(sent, 'shot', [(i, i ^ CLASSES) for i in range(shots)])  5.37 us
    ppermute x1, waiting for transfers between devices, local(): lax.ppermute(sent, 'shot', [(i, i ^ 3 * CLASSES) for i in range(shots)])  4.86 us
  transfers between devices with their start and end apart: 6, of which 6 were waited for; matrix products, arithmetic and copies ran while one was open for 0% of the time, Pallas kernels for 18%

profile of v7, /device:TPU:1, one launch (start us, length us, event | category | flops | bytes accessed | tf_op | source)
XLA Modules:
  0.0 101.3 jit_solution(12579452136149785194)
XLA Ops:
  0.6 2.5 %pack_traces.1 = bf16[128,2,2176]{2,1,0:T(2,128)(2,1)} custom-call(s32[1,128]{1,0:T(1,128)} %bitcast.48, s32[1,128]{1,0:T(1,128)} %bitcast.49, bf16[128,2048]{1,0:T(8,128)(2,1)} %traces_in.1), custom_call_target="tpu_custom_call" | custom-call | tf_op jit(solution)/shard_map/pack_traces/pallas_call | solution.py:75
  3.1 0.0 copy-start
  3.2 0.0 copy-start.1
  3.2 17.0 %all-to-all-start = ((bf16[128,2,2176]{2,1,0:T(2,128)(2,1)}), bf16[128,2,2176]{2,1,0:T(2,128)(2,1)}, u32[]{:S(2)}, u32[]{:S(2)}) async-start(bf16[128,2,2176]{2,1,0:T(2,128)(2,1)} %pack_traces.1), calls=%async_computation | async-start | bytes 2228224 | tf_op jit(solution)/shard_map/all_to_all | solution.py:551
  20.2 0.0 copy-start.3
  20.2 1.2 %copy-done.3 = f32[1,32,64,128]{3,2,1,0:T(8,128)S(1)} copy-done((f32[1,32,64,128]{3,2,1,0:T(8,128)S(1)}, f32[1,32,64,128]{3,2,1,0:T(8,128)}, u32[]{:S(2)}) %copy-start.3) | copy-done | bytes 1048600
  21.4 1.9 %faces.1 = f32[64,128]{1,0:T(8,128)S(1)} custom-call(f32[32,64,128]{2,1,0:T(8,128)S(1)} %bitcast.30, f32[32,64,128]{2,1,0:T(8,128)S(1)} %bitcast.26, f32[32,64,128]{2,1,0:T(8,128)S(1)} %bitcast.21, f32[32,64,128]{2,1,0:T(8,128)S(1)} %bitcast.33), custom_call_target="tpu_custom_call" | custom-call | tf_op jit(solution)/shard_map/faces/pallas_call | solution.py:75
  23.3 0.5 collective-permute-start
  23.8 3.0 %collective-permute-done.faces.refs_0_ = f32[64,128]{1,0:T(8,128)S(1)} collective-permute-done((f32[64,128]{1,0:T(8,128)S(1)}, f32[64,128]{1,0:T(8,128)S(1)}, u32[]{:S(2)}, u32[]{:S(2)}) %collective-permute-start) | collective-permute-done | bytes 32800 | tf_op jit(solution)/shard_map/ppermute | solution.py:505
  26.8 0.0 copy-done.7
  26.8 8.0 %first_step.1 = (f32[32,64,128]{2,1,0:T(8,128)}, f32[32,64,128]{2,1,0:T(8,128)S(1)}, f32[32,64,128]{2,1,0:T(8,128)}, f32[64,128]{1,0:T(8,128)S(1)}) custom-call(f32[64,128]{1,0:T(8,128)S(1)} %collective-permute-done.faces.refs_0_, f32[32,64,128]{2,1,0:T(8,128)S(1)} %bitcast.31, f32[32,64,128]{2,1,0:T(8,128)S(1)} %bitcast.41, f32[32,64,128]{2,1,0:T(8,128)S(1)} %bitcast.22, ...), custom_call_target="tpu_custom_call" | custom-call | tf_op jit(solution)/shard_map/first_step/pallas_call | solution.py:75
  34.7 0.3 collective-permute-start.1
  35.1 2.9 %collective-permute-done.1.mid_face.refs_1_ = f32[64,128]{1,0:T(8,128)S(1)} collective-permute-done((f32[64,128]{1,0:T(8,128)S(1)}, f32[64,128]{1,0:T(8,128)S(1)}, u32[]{:S(2)}, u32[]{:S(2)}) %collective-permute-start.1) | collective-permute-done | bytes 32800 | tf_op jit(solution)/shard_map/ppermute | solution.py:505
  38.0 0.0 copy-start.17
  38.1 3.8 %second_step.1 = (f32[32,64,128]{2,1,0:T(8,128)}, f32[32,64,128]{2,1,0:T(8,128)S(1)}) custom-call(f32[64,128]{1,0:T(8,128)S(1)} %collective-permute-done.faces.refs_0_, f32[64,128]{1,0:T(8,128)S(1)} %collective-permute-done.1.mid_face.refs_1_, f32[32,64,128]{2,1,0:T(8,128)S(1)} %get-tuple-element.28.mid, f32[32,64,128]{2,1,0:T(8,128)S(1)} %bitcast.32, ...), custom_call_target="tpu_custom_call" | custom-call | tf_op jit(solution)/shard_map/second_step/pallas_call | solution.py:75
  41.9 0.0 copy-done.15
  41.9 2.5 %places.1 = (f32[256,384]{1,0:T(8,128)S(1)}, bf16[64,256]{1,0:T(8,128)(2,1)}, s32[1,256]{1,0:T(1,128)}, bf16[32,256]{1,0:T(8,128)(2,1)}, f32[256,128]{1,0:T(8,12...) custom-call(s32[1,256]{1,0:T(1,128)S(1)} %copy-done.15, s32[1,256]{1,0:T(1,128)S(1)} %copy-done.15, f32[2048,128]{1,0:T(8,128)S(1)} %bitcast.37, ...), custom_call_target="tpu_custom_call" | custom-call | tf_op jit(solution)/shard_map/places/pallas_call | solution.py:75
  44.4 0.0 copy-start.5
  44.4 7.4 %all-to-all-done.refs_0_ = bf16[128,2,2176]{2,1,0:T(2,128)(2,1)} async-done(((bf16[128,2,2176]{2,1,0:T(2,128)(2,1)}), bf16[128,2,2176]{2,1,0:T(2,128)(2,1)}, u32[]{:S(2)}, u32[]{:S(2)}) %all-to-all-start) | async-done | bytes 1114144 | tf_op jit(solution)/shard_map/all_to_all | solution.py:551
  51.9 2.7 %residual.1 = (f32[256,128]{1,0:T(8,128)S(1)}, f32[256,128]{1,0:T(8,128)S(1)}, f32[64,128]{1,0:T(8,128)S(1)}) custom-call(bf16[128,2,2176]{2,1,0:T(2,128)(2,1)} %all-to-all-done.refs_0_, bf16[2,2048]{1,0:T(2,128)(2,1)} %bitcast.47, f32[256,384]{1,0:T(8,128)S(1)} %get-tuple-element.30.refs_2_, bf16[64,256]{1,0:T(8,128)(2,1)} %get-tuple-element.31.refs_3_), custom_call_target="tpu_custom_call" | custom-call | tf_op jit(solution)/shard_map/residual/pallas_call | solution.py:75
  54.5 0.5 collective-permute-start.2
  55.0 0.0 copy-done.5
  55.0 1.9 %inject.1 = (f32[2048,128]{1,0:T(8,128)S(1)}, f32[2048,128]{1,0:T(8,128)S(1)}) custom-call(s32[1,256]{1,0:T(1,128)S(1)} %copy-done.15, f32[256,128]{1,0:T(8,128)S(1)} %get-tuple-element.33.sum_mid, f32[256,128]{1,0:T(8,128)S(1)} %get-tuple-element.34.sum_end, f32[2048,128]{1,0:T(8,128)S(1)} %bitcast.39), custom_call_target="tpu_custom_call" | custom-call | tf_op jit(solution)/shard_map/inject/pallas_call | solution.py:75
  56.9 0.5 collective-permute-done.2.refs_2_
  57.4 4.7 %image.1 = (f32[32,64,128]{2,1,0:T(8,128)}, s16[544,8,128]{2,1,0:T(8,128)(2,1)S(1)}) custom-call(f32[64,128]{1,0:T(8,128)S(1)} %copy-done.9, f32[64,128]{1,0:T(8,128)S(1)} %copy-done.12, f32[64,128]{1,0:T(8,128)S(1)} %collective-permute-done.2.refs_2_, f32[32,64,128]{2,1,0:T(8,128)S(1)} %bitcast.43, f32[32,64,128]{2,1,0:T(8,128)S(1)} %bitcast.44, ...), custom_call_target="tpu_custom_call" | custom-call | tf_op jit(solution)/shard_map/image/pallas_call | solution.py:75
  62.2 25.2 %all_to_all.10 = s16[32,136,128]{2,1,0:T(8,128)(2,1)S(1)} all-to-all(s16[32,136,128]{2,1,0:T(8,128)(2,1)S(1)} %bitcast.38), channel_id=1, replica_groups={{0,2,4,6,8,10,12,14,16,18,20,22,24,26,28,30,32,34,36,38,40,42,44,46,48,..., dimensions={0} | all-to-all | bytes 2228224 | tf_op jit(solution)/shard_map/all_to_all | solution.py:625
  87.4 1.9 %combine.1 = (f32[16,8,128]{2,1,0:T(8,128)S(1)}, f32[16,8,128]{2,1,0:T(8,128)S(1)}) custom-call(s16[544,8,128]{2,1,0:T(8,128)(2,1)S(1)} %bitcast.36), custom_call_target="tpu_custom_call" | custom-call | tf_op jit(solution)/shard_map/combine/pallas_call | solution.py:75
  89.4 0.9 collective-permute-start.3
  90.3 5.4 %collective-permute-done.3.came = f32[16,8,128]{2,1,0:T(8,128)S(1)} collective-permute-done((f32[16,8,128]{2,1,0:T(8,128)S(1)}, f32[16,8,128]{2,1,0:T(8,128)S(1)}, u32[]{:S(2)}, u32[]{:S(2)}) %collective-permute-start.3) | collective-permute-done | bytes 65568 | tf_op jit(solution)/shard_map/ppermute | solution.py:649
  95.7 0.1 collective-permute-start.4
  95.8 4.9 %collective-permute-done.4.came = f32[8,8,128]{2,1,0:T(8,128)S(1)} collective-permute-done((f32[8,8,128]{2,1,0:T(8,128)S(1)}, f32[8,8,128]{2,1,0:T(8,128)S(1)}, u32[]{:S(2)}, u32[]{:S(2)}) %collective-permute-start.4) | collective-permute-done | bytes 32800 | tf_op jit(solution)/shard_map/ppermute | solution.py:652
  100.7 0.6 last_sum.1
  (30 shorter events, 0.1 us)
Async XLA Ops:
  0.6 19.5 %copy-start.2 = (f32[1,32,64,128]{3,2,1,0:T(8,128)S(1)}, f32[1,32,64,128]{3,2,1,0:T(8,128)}, u32[]{:S(2)}) copy-start(f32[1,32,64,128]{3,2,1,0:T(8,128)} %param.14) | copy-start | bytes 3145732
  3.1 17.0 %copy-start = (f32[1,32,64,128]{3,2,1,0:T(8,128)S(1)}, f32[1,32,64,128]{3,2,1,0:T(8,128)}, u32[]{:S(2)}) copy-start(f32[1,32,64,128]{3,2,1,0:T(8,128)} %param.17) | copy-start | bytes 3145732
  3.2 17.0 %copy-start.1 = (f32[1,32,64,128]{3,2,1,0:T(8,128)S(1)}, f32[1,32,64,128]{3,2,1,0:T(8,128)}, u32[]{:S(2)}) copy-start(f32[1,32,64,128]{3,2,1,0:T(8,128)} %param.18) | copy-start | bytes 3145732
  3.2 48.7 %all-to-all-start = ((bf16[128,2,2176]{2,1,0:T(2,128)(2,1)}), bf16[128,2,2176]{2,1,0:T(2,128)(2,1)}, u32[]{:S(2)}, u32[]{:S(2)}) async-start(bf16[128,2,2176]{2,1,0:T(2,128)(2,1)} %pack_traces.1), calls=%async_computation | async-start | bytes 2228224 | tf_op jit(solution)/shard_map/all_to_all | solution.py:551
  20.2 1.2 %copy-start.3 = (f32[1,32,64,128]{3,2,1,0:T(8,128)S(1)}, f32[1,32,64,128]{3,2,1,0:T(8,128)}, u32[]{:S(2)}) copy-start(f32[1,32,64,128]{3,2,1,0:T(8,128)} %param.16) | copy-start | bytes 3145732
  21.4 5.4 %copy-start.6 = (f32[1,32,64,128]{3,2,1,0:T(8,128)S(1)}, f32[1,32,64,128]{3,2,1,0:T(8,128)}, u32[]{:S(2)}) copy-start(f32[1,32,64,128]{3,2,1,0:T(8,128)} %param.13) | copy-start | bytes 3145732
  21.4 5.4 %copy-start.7 = (f32[1,32,64,128]{3,2,1,0:T(8,128)S(1)}, f32[1,32,64,128]{3,2,1,0:T(8,128)}, u32[]{:S(2)}) copy-start(f32[1,32,64,128]{3,2,1,0:T(8,128)} %param.15) | copy-start | bytes 3145732
  23.3 3.5 %collective-permute-start = (f32[64,128]{1,0:T(8,128)S(1)}, f32[64,128]{1,0:T(8,128)S(1)}, u32[]{:S(2)}, u32[]{:S(2)}) collective-permute-start(f32[64,128]{1,0:T(8,128)S(1)} %faces.1), channel_id=1, source_target_pairs={{0,1},{1,0},{2,3},{3,2},{4,5},{5,4},{6,7},{7,6},{8,9},{9,8},{10,11... | collective-permute-start | bytes 98312 | tf_op jit(solution)/shard_map/ppermute | solution.py:505
  26.8 11.3 %copy-start.8 = (f32[64,128]{1,0:T(8,128)}, f32[64,128]{1,0:T(8,128)S(1)}, u32[]{:S(2)}) copy-start(f32[64,128]{1,0:T(8,128)S(1)} %collective-permute-done.faces.refs_0_) | copy-start | bytes 98308
  34.7 3.3 %collective-permute-start.1 = (f32[64,128]{1,0:T(8,128)S(1)}, f32[64,128]{1,0:T(8,128)S(1)}, u32[]{:S(2)}, u32[]{:S(2)}) collective-permute-start(f32[64,128]{1,0:T(8,128)S(1)} %get-tuple-element.27), channel_id=1, source_target_pairs={{0,1},{1,0},{2,3},{3,2},{4,5},{5,4},{6,7},{7,6},{8,9},{9,8},{10,11... | collective-permute-start | bytes 98312 | tf_op jit(solution)/shard_map/ppermute | solution.py:505
  38.0 3.9 %copy-start.11 = (f32[64,128]{1,0:T(8,128)}, f32[64,128]{1,0:T(8,128)S(1)}, u32[]{:S(2)}) copy-start(f32[64,128]{1,0:T(8,128)S(1)} %collective-permute-done.1.mid_face.refs_1_) | copy-start | bytes 98308
  38.0 3.9 %copy-start.15 = (s32[1,256]{1,0:T(1,128)S(1)}, s32[1,256]{1,0:T(1,128)}, u32[]{:S(2)}) copy-start(s32[1,256]{1,0:T(1,128)} %at.3) | copy-start | bytes 3076
  38.0 3.9 %copy-start.16 = (s32[256,1]{0,1:T(1,128)S(1)}, s32[256,1]{0,1:T(1,128)}, u32[]{:S(2)}) copy-start(s32[256,1]{0,1:T(1,128)} %param.24) | copy-start | bytes 3076
  38.0 3.9 %copy-start.17 = (s32[256]{0:T(256)S(1)}, s32[256]{0:T(256)}, u32[]{:S(2)}) copy-start(s32[256]{0:T(256)} %param.25) | copy-start | bytes 3076
  44.4 10.6 %copy-start.5 = (f32[32,64,128]{2,1,0:T(8,128)S(1)}, f32[32,64,128]{2,1,0:T(8,128)}, u32[]{:S(2)}) copy-start(f32[32,64,128]{2,1,0:T(8,128)} %get-tuple-element.35) | copy-start | bytes 3145732
  51.8 5.6 %copy-start.4 = (f32[1,32,64,128]{3,2,1,0:T(8,128)S(1)}, f32[1,32,64,128]{3,2,1,0:T(8,128)}, u32[]{:S(2)}) copy-start(f32[1,32,64,128]{3,2,1,0:T(8,128)} %param.16) | copy-start | bytes 3145732
  51.8 5.6 %copy-start.9 = (f32[64,128]{1,0:T(8,128)S(1)}, f32[64,128]{1,0:T(8,128)}, u32[]{:S(2)}) copy-start(f32[64,128]{1,0:T(8,128)} %copy-done.8) | copy-start | bytes 98308
  51.8 5.6 %copy-start.10 = (f32[256,128]{1,0:T(8,128)S(1)}, f32[256,128]{1,0:T(8,128)}, u32[]{:S(2)}) copy-start(f32[256,128]{1,0:T(8,128)} %get-tuple-element.42.refs_12_) | copy-start | bytes 393220
  51.8 5.6 %copy-start.12 = (f32[64,128]{1,0:T(8,128)S(1)}, f32[64,128]{1,0:T(8,128)}, u32[]{:S(2)}) copy-start(f32[64,128]{1,0:T(8,128)} %copy-done.11) | copy-start | bytes 98308
  51.8 5.6 %copy-start.13 = (bf16[32,256]{1,0:T(8,128)(2,1)S(1)}, bf16[32,256]{1,0:T(8,128)(2,1)}, u32[]{:S(2)}) copy-start(bf16[32,256]{1,0:T(8,128)(2,1)} %get-tuple-element.41.refs_11_) | copy-start | bytes 49156
  51.9 5.6 %copy-start.14 = (f32[32,128]{1,0:T(8,128)S(1)}, f32[32,128]{1,0:T(8,128)}, u32[]{:S(2)}) copy-start(f32[32,128]{1,0:T(8,128)} %get-tuple-element.43.refs_13_) | copy-start | bytes 49156
  51.9 5.6 %copy-start.18 = (s32[1,256]{1,0:T(1,128)S(1)}, s32[1,256]{1,0:T(1,128)}, u32[]{:S(2)}) copy-start(s32[1,256]{1,0:T(1,128)} %get-tuple-element.40.refs_10_) | copy-start | bytes 3076
  54.5 2.9 %collective-permute-start.2 = (f32[64,128]{1,0:T(8,128)S(1)}, f32[64,128]{1,0:T(8,128)S(1)}, u32[]{:S(2)}, u32[]{:S(2)}) collective-permute-start(f32[64,128]{1,0:T(8,128)S(1)} %get-tuple-element.32), channel_id=1, source_target_pairs={{0,1},{1,0},{2,3},{3,2},{4,5},{5,4},{6,7},{7,6},{8,9},{9,8},{10,11... | collective-permute-start | bytes 98312 | tf_op jit(solution)/shard_map/ppermute | solution.py:505
  89.4 6.3 %collective-permute-start.3 = (f32[16,8,128]{2,1,0:T(8,128)S(1)}, f32[16,8,128]{2,1,0:T(8,128)S(1)}, u32[]{:S(2)}, u32[]{:S(2)}) collective-permute-start(f32[16,8,128]{2,1,0:T(8,128)S(1)} %get-tuple-element.46), channel_id=1, source_target_pairs={{0,64},{2,66},{4,68},{6,70},{8,72},{10,74},{12,76},{14,78},{16,80}... | collective-permute-start | bytes 196616 | tf_op jit(solution)/shard_map/ppermute | solution.py:649
  95.7 5.0 %collective-permute-start.4 = (f32[8,8,128]{2,1,0:T(8,128)S(1)}, f32[8,8,128]{2,1,0:T(8,128)S(1)}, u32[]{:S(2)}, u32[]{:S(2)}) collective-permute-start(f32[8,8,128]{2,1,0:T(8,128)S(1)} %get-tuple-element.48), channel_id=1, source_target_pairs={{0,192},{2,194},{4,196},{6,198},{8,200},{10,202},{12,204},{14,206}... | collective-permute-start | bytes 98312 | tf_op jit(solution)/shard_map/ppermute | solution.py:652

commit v8 on v7

--- a/solution.py
+++ b/solution.py
@@ -175,16 +175,19 @@
     return jnp.minimum(x + 1, count - 1), (x < count - 1).astype(F32)
 
 
-def faces_kernel(now, buoy, bulk, nxt, out):
+def faces_kernel(arrived, now, buoy, bulk, nxt, out):
     low = which_half()
     count = now.shape[0]
 
-    def body(x, held):
-        held = put_face(held, now[x], x, low)
-        held = put_face(held, buoy[x], 32 + x, low)
+    def plain(x, held):
+        return put_face(put_face(held, now[x], x, low), buoy[x], 32 + x, low)
+
+    def scaled(x, held):
         return put_face(held, bulk[x] * nxt[x], 64 + x, low)
 
-    out[...] = lax.fori_loop(0, count, body, jnp.zeros(now.shape[1:], F32), unroll=2)
+    held = lax.fori_loop(0, count, plain, jnp.zeros(now.shape[1:], F32), unroll=4)
+    arrived()
+    out[...] = lax.fori_loop(0, count, scaled, held, unroll=8)
 
 
 def first_kernel(
@@ -220,7 +223,16 @@
     face_out[...] = held
 
 
-def second_kernel(faces, mid_face, mid, now, bulk, buoy, lap_out, end_out):
+def second_kernel(
+    faces, mid_face, mid, now, bulk, buoy, lap_first, base, lap_out, end_out, lap_kept, base_kept,
+    sems,
+):
+    copies = [
+        pltpu.make_async_copy(lap_first, lap_kept, sems.at[0]),
+        pltpu.make_async_copy(base, base_kept, sems.at[1]),
+    ]
+    for copy in copies:
+        copy.start()
     low = which_half()
     count = now.shape[0]
 
@@ -237,6 +249,8 @@
         return flux
 
     lax.fori_loop(0, count, body, buoy[0] * mid[0], unroll=4)
+    for copy in copies:
+        copy.wait()
 
 
 def pack_traces_kernel(
@@ -276,19 +290,15 @@
 
 
 def places_kernel(
-    at, cells, mid, end, bulk, owners, slots, about_out, hot_second_out, place_out, cls_out,
-    spot_out, ids_out, end_out, rows_mid, rows_end, rows_bulk, sem,
+    at, cells, bulk, owners, slots, marks_out, hot_second_out, place_out, cls_out, spot_out,
+    ids_out, rows_bulk,
 ):
-    keep_end = pltpu.make_async_copy(end, end_out, sem)
-    keep_end.start()
     low = which_half()
     lanes = 128
     count = cells.shape[1]
 
     def body(r, carry):
         row = lax.shift_right_logical(at[0, r], 7)
-        rows_mid[pl.ds(r, 1), :] = mid[pl.ds(row, 1), :]
-        rows_end[pl.ds(r, 1), :] = end[pl.ds(row, 1), :]
         rows_bulk[pl.ds(r, 1), :] = bulk[pl.ds(row, 1), :]
         return carry
 
@@ -296,16 +306,12 @@
     cell_row = cells[...]
     cell_col = as_column(cell_row)
     lane = iota((count, lanes), 1)
-    depth_col = cell_col & (lanes - 1)
-    here = lane == depth_col
-    seen_mid = jnp.sum(jnp.where(here, rows_mid[...], 0.0), axis=1, keepdims=True)
-    seen_end = jnp.sum(jnp.where(here, rows_end[...], 0.0), axis=1, keepdims=True)
+    here = lane == (cell_col & (lanes - 1))
     at_edge = here & (lane == edge_lane(low, lanes))
     edge_bulk = jnp.sum(jnp.where(at_edge, rows_bulk[...], 0.0), axis=1, keepdims=True)
-    about_out[:, :lanes] = jnp.where(lane == 0, seen_mid, seen_end)
-    about_out[:, lanes : 2 * lanes] = here.astype(F32)
+    marks_out[:, :lanes] = here.astype(F32)
     first_col = lax.shift_right_logical(cell_col, 13)
-    about_out[:, 2 * lanes :] = jnp.where(lane == first_col + 32, edge_bulk, 0.0)
+    marks_out[:, lanes:] = jnp.where(lane == first_col + 32, edge_bulk, 0.0)
     rows = hot_second_out.shape[0]
     second_row = lax.shift_right_logical(cell_row, 7) & (rows - 1)
     hot_second_out[...] = (iota((rows, count), 0) == second_row).astype(F32).astype(BF16)
@@ -325,51 +331,61 @@
     ids_out[...] = jnp.dot(
         cls_hot, (spot_hot * slot_col).astype(BF16), preferred_element_type=F32
     )
-    keep_end.wait()
-
-
-def residual_kernel(
-    arrived, rows_in, filters, about, hot_second, sum_mid, sum_end, face_out, held, sems
+
+
+def seen_kernel(
+    arrived, at, marks, mid, end, lap_mid, seen_out, end_kept, lap_kept, rows_mid, rows_end, sems
 ):
-    shots, cap, wide = rows_in.shape
-    parts = sems.shape[0]
-    each = shots // parts
-    copies = []
-    for n in range(parts):
-        part = pl.ds(n * each, each)
-        copies.append(pltpu.make_async_copy(rows_in.at[part], held.at[part], sems.at[n]))
-        copies[-1].start()
+    copies = [
+        pltpu.make_async_copy(end, end_kept, sems.at[0]),
+        pltpu.make_async_copy(lap_mid, lap_kept, sems.at[1]),
+    ]
+    for copy in copies:
+        copy.start()
+    count, lanes = seen_out.shape
+
+    def body(r, carry):
+        row = lax.shift_right_logical(at[0, r], 7)
+        rows_mid[pl.ds(r, 1), :] = mid[pl.ds(row, 1), :]
+        rows_end[pl.ds(r, 1), :] = end[pl.ds(row, 1), :]
+        return carry
+
+    lax.fori_loop(0, count, body, 0, unroll=8)
+    arrived()
+    here = marks[:, :lanes] > 0.5
+    seen_mid = jnp.sum(jnp.where(here, rows_mid[...], 0.0), axis=1, keepdims=True)
+    seen_end = jnp.sum(jnp.where(here, rows_end[...], 0.0), axis=1, keepdims=True)
+    seen_out[...] = jnp.where(iota((count, lanes), 1) == 0, seen_mid, seen_end)
+    for copy in copies:
+        copy.wait()
+
+
+def residual_kernel(rows_in, filters, seen, marks, hot_second, sum_mid, sum_end, face_out):
     samples = filters.shape[1]
     count, lanes = sum_mid.shape
-    slots = each * cap
+    slots = rows_in.shape[0] * rows_in.shape[1]
     last_dims = (((1,), (1,)), ((), ()))
+    values = lax.dot_general(
+        rows_in[:, :, :samples].reshape(slots, samples),
+        filters[...],
+        last_dims,
+        preferred_element_type=F32,
+    )
     pick = ((iota((8, 128), 0) == 0) & (iota((8, 128), 1) == 0)).astype(F32).astype(BF16)
-    receiver = iota((count, slots), 0).astype(F32)
-    observed = jnp.zeros((count, filters.shape[0]), F32)
-    arrived()
-    for n in range(parts):
-        copies[n].wait()
-        here = slice(n * each, (n + 1) * each)
-        values = lax.dot_general(
-            held[here, :, :samples].reshape(slots, samples),
-            filters[...],
-            last_dims,
-            preferred_element_type=F32,
-        )
-        ids = lax.dot_general(
-            pick,
-            held[here, :, samples:].reshape(slots, wide - samples),
-            last_dims,
-            preferred_element_type=F32,
-        )
-        hot = (receiver == ids[0:1, :]).astype(F32).astype(BF16)
-        observed = observed + exact_dot(hot, values)
-    resid_mid = about[:, 0:1] - observed[:, 0:1]
-    resid_end = about[:, 1:2] - observed[:, 1:2]
-    hot_depth = about[:, lanes : 2 * lanes]
+    ids = lax.dot_general(
+        pick,
+        rows_in[:, :, samples:].reshape(slots, rows_in.shape[2] - samples),
+        last_dims,
+        preferred_element_type=F32,
+    )
+    hot = (iota((count, slots), 0).astype(F32) == ids[0:1, :]).astype(F32).astype(BF16)
+    observed = exact_dot(hot, values)
+    resid_mid = seen[:, 0:1] - observed[:, 0:1]
+    resid_end = seen[:, 1:2] - observed[:, 1:2]
+    hot_depth = marks[:, :lanes]
     sum_mid[...] = hot_depth * resid_mid
     sum_end[...] = hot_depth * resid_end
-    face_out[...] = exact_dot(hot_second[...], about[:, 2 * lanes :] * resid_end)
+    face_out[...] = exact_dot(hot_second[...], marks[:, lanes:] * resid_end)
 
 
 def inject_kernel(at, sum_mid, sum_end, base, mid_out, add_out):
@@ -552,52 +568,63 @@
         packed, "shot", split_axis=0, concat_axis=0, tiled=True
     )
 
-    faces = swap(call(faces_kernel, "faces", face)(now, buoy, bulk, nxt))
+    faces = swap(call(faces_kernel, "faces", face, stage=(3,), late=True)(now, buoy, bulk, nxt))
     lap_now, wave_mid, adj_base, mid_face = call(
-        first_kernel, "first_step", (field, field, field, face), hbm_out=(0, 2)
+        first_kernel, "first_step", (field, field, field, face)
     )(faces, now, prev, bulk, buoy, nxt, late)
     mid_face = swap(mid_face)
-    lap_mid, wave_end = call(second_kernel, "second_step", (field, field), hbm_out=(0,))(
-        faces, mid_face, wave_mid, now, bulk, buoy
-    )
+    lap_mid, wave_end, lap_now, adj_base = call(
+        second_kernel,
+        "second_step",
+        (field, field, field, field),
+        [pltpu.SemaphoreType.DMA((2,))],
+        raw_out=(2, 3),
+    )(faces, mid_face, wave_mid, now, bulk, buoy, lap_now, adj_base)
     receivers = receiver_cell.shape[1]
     tiles = tile_owner.shape[0]
     per_receiver = pltpu.VMEM((receivers, lanes), F32)
-    about, hot_second, place, cls_hot, spot_hot, ids, wave_end = call(
+    marks, hot_second, place, cls_hot, spot_hot, ids = call(
         places_kernel,
         "places",
         (
-            sds((receivers, 3 * lanes)),
+            sds((receivers, 2 * lanes)),
             sds((rows, receivers), BF16),
             sds((1, tiles), I32),
             sds((CLASSES, tiles), BF16),
             sds((tiles, lanes)),
             sds((CLASSES, lanes)),
-            flat,
         ),
-        [per_receiver] * 3 + [pltpu.SemaphoreType.DMA],
+        [per_receiver],
         smem=(0,),
-        hbm_out=(1, 2, 3, 4, 5),
-        raw_out=(6,),
+        hbm_out=(0, 1, 2, 3, 4, 5),
     )(
         receiver_cell,
         receiver_cell,
-        wave_mid.reshape(flat.shape),
-        wave_end.reshape(flat.shape),
         bulk.reshape(flat.shape),
         tile_owner.reshape(1, -1),
         tile_slot.reshape(1, -1),
     )
     spread = sds((receivers, lanes))
+    seen, wave_end, lap_mid = call(
+        seen_kernel,
+        "seen",
+        (spread, flat, flat),
+        [per_receiver, per_receiver, pltpu.SemaphoreType.DMA((2,))],
+        smem=(0,),
+        raw_out=(1, 2),
+        stage=(1,),
+        late=True,
+    )(
+        receiver_cell,
+        marks,
+        wave_mid.reshape(flat.shape),
+        wave_end.reshape(flat.shape),
+        lap_mid.reshape(flat.shape),
+    )
+    lap_mid = lap_mid.reshape(now.shape)
     sum_mid, sum_end, adj_face = call(
-        residual_kernel,
-        "residual",
-        (spread, spread, face),
-        [pltpu.VMEM(got_rows.shape, BF16), pltpu.SemaphoreType.DMA((2,))],
-        hbm=(0,),
-        stage=(1, 3),
-        late=True,
-    )(got_rows, group_filter[0], about, hot_second)
+        residual_kernel, "residual", (spread, spread, face), stage=(0, 1, 3, 4)
+    )(got_rows, group_filter[0], seen, marks, hot_second)
     adj_face = swap(adj_face)
     adj_mid, adj_add = call(inject_kernel, "inject", (flat, flat), smem=(0,))(
         receiver_cell, sum_mid, sum_end, adj_base.reshape(flat.shape)

time: 102 us -> 101 us (level)
  local copies, waits for them, and re-layouts: 1.3 us -> 0.08 us
    all_to_all x1, waiting for transfers between devices: 7.39 us -> 11 us  [local(): lax.all_to_all(packed, 'shot', split_axis=0, concat_axis=0, tiled=True)]
    ppermute x3, waiting for transfers between devices: 6.41 us -> 3.68 us  [swap(): return lax.ppermute(face, 'ap', [(0, 1), (1, 0)])]
    unnamed x38 -> x30, local copies, waits for them, and re-layouts: 1.3 us -> 0.08 us
    pallas_call x11 -> x12, Pallas kernels: 30.6 us -> 30.1 us  [run(): pl.pallas_call(body, out_shape=jax.tree.unflatten(tree, shapes), in_specs...]
  transfers between devices with their start and end apart: 6 -> 6, of which waited for: 6 -> 6; matrix products, arithmetic and copies ran while one was open for 0% -> 0% of each run, Pallas kernels for 18% -> 17%
where the time goes in v8:
time: 101 us
  Pallas kernels  30.1 us (30%)
  blocking collectives  25.2 us (25%)
  waiting for transfers between devices  24.9 us (25%)
  starting transfers between devices  20 us (20%)
    pallas_call x12, Pallas kernels, run(): pl.pallas_call(body, out_shape=jax.tree.unflatten(tree, shapes), in_specs...  30.1 us
    all_to_all x1, blocking collectives, local(): lax.all_to_all(send.reshape(CLASSES, per_class * 8, lanes), 'shot', split...  25.2 us
    all_to_all x1, starting transfers between devices, local(): lax.all_to_all(packed, 'shot', split_axis=0, concat_axis=0, tiled=True)  17 us
    all_to_all x1, waiting for transfers between devices, local(): lax.all_to_all(packed, 'shot', split_axis=0, concat_axis=0, tiled=True)  11 us
    ppermute x1, waiting for transfers between devices, local(): came = lax.ppermute(sent, 'shot', [(i, i ^ CLASSES) for i in range(shots)])  5.37 us
    ppermute x1, waiting for transfers between devices, local(): lax.ppermute(sent, 'shot', [(i, i ^ 3 * CLASSES) for i in range(shots)])  4.86 us
    ppermute x3, waiting for transfers between devices, swap(): return lax.ppermute(face, 'ap', [(0, 1), (1, 0)])  3.68 us
    ppermute x3, starting transfers between devices, swap(): return lax.ppermute(face, 'ap', [(0, 1), (1, 0)])  2.06 us
  transfers between devices with their start and end apart: 6, of which 6 were waited for; matrix products, arithmetic and copies ran while one was open for 0% of the time, Pallas kernels for 17%

profile of v8, /device:TPU:1, one launch (start us, length us, event | category | flops | bytes accessed | tf_op | source)
XLA Modules:
  0.0 101.2 jit_solution(6494437441521801304)
XLA Ops:
  0.6 2.5 %pack_traces.1 = bf16[128,2,2176]{2,1,0:T(2,128)(2,1)} custom-call(s32[1,128]{1,0:T(1,128)} %bitcast.52, s32[1,128]{1,0:T(1,128)} %bitcast.53, bf16[128,2048]{1,0:T(8,128)(2,1)} %traces_in.1), custom_call_target="tpu_custom_call" | custom-call | tf_op jit(solution)/shard_map/pack_traces/pallas_call | solution.py:75
  3.2 0.0 copy-start
  3.2 0.0 copy-start.1
  3.2 17.0 %all-to-all-start = ((bf16[128,2,2176]{2,1,0:T(2,128)(2,1)}), bf16[128,2,2176]{2,1,0:T(2,128)(2,1)}, u32[]{:S(2)}, u32[]{:S(2)}) async-start(bf16[128,2,2176]{2,1,0:T(2,128)(2,1)} %pack_traces.1), calls=%async_computation | async-start | bytes 2228224 | tf_op jit(solution)/shard_map/all_to_all | solution.py:567
  20.2 0.0 copy-start.3
  20.2 0.0 copy-start.6
  20.2 0.0 copy-start.7
  20.2 1.9 %faces.1 = f32[64,128]{1,0:T(8,128)S(1)} custom-call(f32[32,64,128]{2,1,0:T(8,128)S(1)} %bitcast.32, f32[32,64,128]{2,1,0:T(8,128)S(1)} %bitcast.28, f32[32,64,128]{2,1,0:T(8,128)S(1)} %bitcast.23, f32[32,64,128]{2,1,0:T(8,128)} %bitcast.35), custom_call_target="tpu_custom_call" | custom-call | tf_op jit(solution)/shard_map/faces/pallas_call | solution.py:75
  22.2 0.5 collective-permute-start
  22.6 3.0 %collective-permute-done.faces.refs_0_ = f32[64,128]{1,0:T(8,128)S(1)} collective-permute-done((f32[64,128]{1,0:T(8,128)S(1)}, f32[64,128]{1,0:T(8,128)S(1)}, u32[]{:S(2)}, u32[]{:S(2)}) %collective-permute-start) | collective-permute-done | bytes 32800 | tf_op jit(solution)/shard_map/ppermute | solution.py:521
  25.7 0.0 copy-start.13
  25.7 0.0 copy-start.14
  25.7 6.8 %first_step.1 = (f32[32,64,128]{2,1,0:T(8,128)S(1)}, f32[32,64,128]{2,1,0:T(8,128)S(1)}, f32[32,64,128]{2,1,0:T(8,128)S(1)}, f32[64,128]{1,0:T(8,128)S(1)}) custom-call(f32[64,128]{1,0:T(8,128)S(1)} %collective-permute-done.faces.refs_0_, f32[32,64,128]{2,1,0:T(8,128)S(1)} %bitcast.33, f32[32,64,128]{2,1,0:T(8,128)S(1)} %bitcast.44, ...), custom_call_target="tpu_custom_call" | custom-call | tf_op jit(solution)/shard_map/first_step/pallas_call | solution.py:75
  32.5 1.1 %collective-permute-start.1 = (f32[64,128]{1,0:T(8,128)S(1)}, f32[64,128]{1,0:T(8,128)S(1)}, u32[]{:S(2)}, u32[]{:S(2)}) collective-permute-start(f32[64,128]{1,0:T(8,128)S(1)} %get-tuple-element.31), channel_id=1, source_target_pairs={{0,1},{1,0},{2,3},{3,2},{4,5},{5,4},{6,7},{7,6},{8,9},{9,8},{10,11... | collective-permute-start | bytes 98312 | tf_op jit(solution)/shard_map/ppermute | solution.py:521
  33.6 2.2 %places.1 = (f32[256,256]{1,0:T(8,128)}, bf16[64,256]{1,0:T(8,128)(2,1)}, s32[1,256]{1,0:T(1,128)}, bf16[32,256]{1,0:T(8,128)(2,1)}, f32[256,128]{1,0:T(8,128)}, /*index=5*/f32[32,128]{1,0:T(8,128)}) custom-call(s32[1,256]{1,0:T(1,128)S(1)} %copy-done.11, s32[1,256]{1,0:T(1,128)S(1)} %copy-done.11, f32[2048,128]{1,0:T(8,128)S(1)} %bitcast.25, ...), custom_call_target="tpu_custom_call" | custom-call | tf_op jit(solution)/shard_map/places/pallas_call | solution.py:75
  35.9 0.1 collective-permute-done.1.mid_face.refs_1_
  36.0 2.9 %second_step.1 = (f32[32,64,128]{2,1,0:T(8,128)S(1)}, f32[32,64,128]{2,1,0:T(8,128)S(1)}, f32[32,64,128]{2,1,0:T(8,128)}, f32[32,64,128]{2,1,0:T(8,128)}) custom-call(f32[64,128]{1,0:T(8,128)S(1)} %collective-permute-done.faces.refs_0_, f32[64,128]{1,0:T(8,128)S(1)} %collective-permute-done.1.mid_face.refs_1_, f32[32,64,128]{2,1,0:T(8,128)S(1)} %get-tuple-element.33.mid, ...), custom_call_target="tpu_custom_call" | custom-call | tf_op jit(solution)/shard_map/second_step/pallas_call | solution.py:75
  38.9 1.9 %seen.1 = (f32[256,128]{1,0:T(8,128)S(1)}, f32[2048,128]{1,0:T(8,128)}, f32[2048,128]{1,0:T(8,128)}) custom-call(s32[1,256]{1,0:T(1,128)S(1)} %copy-done.11, f32[256,256]{1,0:T(8,128)} %get-tuple-element.32.refs_1_.refs_3_, f32[2048,128]{1,0:T(8,128)S(1)} %bitcast.39, f32[2048,128]{1,0:T(8,128)S(1)} %bitcast.43, f32[2048,128]{1,0:T(8,128)S(1)} %bitcast.42), custom_call_target="tpu_custom_call" | custom-call | tf_op jit(solution)/shard_map/seen/pallas_call | solution.py:75
  40.8 0.0 copy-start.5
  40.8 11.0 %all-to-all-done.refs_0_ = bf16[128,2,2176]{2,1,0:T(2,128)(2,1)} async-done(((bf16[128,2,2176]{2,1,0:T(2,128)(2,1)}), bf16[128,2,2176]{2,1,0:T(2,128)(2,1)}, u32[]{:S(2)}, u32[]{:S(2)}) %all-to-all-start) | async-done | bytes 1114144 | tf_op jit(solution)/shard_map/all_to_all | solution.py:567
  51.9 2.5 %residual.1 = (f32[256,128]{1,0:T(8,128)S(1)}, f32[256,128]{1,0:T(8,128)S(1)}, f32[64,128]{1,0:T(8,128)S(1)}) custom-call(bf16[128,2,2176]{2,1,0:T(2,128)(2,1)} %all-to-all-done.refs_0_, bf16[2,2048]{1,0:T(2,128)(2,1)} %bitcast.51, f32[256,128]{1,0:T(8,128)S(1)} %get-tuple-element.38.refs_2_, f32[256,256]{1,0:T(8,128)} %get-tuple-element.32.refs_1_.refs_3_, ...), custom_call_target="tpu_custom_call" | custom-call | tf_op jit(solution)/shard_map/residual/pallas_call | solution.py:75
  54.4 0.5 collective-permute-start.2
  54.9 1.9 %inject.1 = (f32[2048,128]{1,0:T(8,128)S(1)}, f32[2048,128]{1,0:T(8,128)S(1)}) custom-call(s32[1,256]{1,0:T(1,128)S(1)} %copy-done.11, f32[256,128]{1,0:T(8,128)S(1)} %get-tuple-element.41.sum_mid, f32[256,128]{1,0:T(8,128)S(1)} %get-tuple-element.42.sum_end, f32[2048,128]{1,0:T(8,128)S(1)} %bitcast.41), custom_call_target="tpu_custom_call" | custom-call | tf_op jit(solution)/shard_map/inject/pallas_call | solution.py:75
  56.8 0.5 collective-permute-done.2.refs_2_
  57.3 4.8 %image.1 = (f32[32,64,128]{2,1,0:T(8,128)}, s16[544,8,128]{2,1,0:T(8,128)(2,1)S(1)}) custom-call(f32[64,128]{1,0:T(8,128)S(1)} %collective-permute-done.faces.refs_0_, f32[64,128]{1,0:T(8,128)S(1)} %collective-permute-done.1.mid_face.refs_1_, f32[64,128]{1,0:T(8,128)S(1)} %collective-permute-done.2.refs_2_, f32[32,64,128]{2,1,0:T(8,128)S(1)} %bitcast.46, ...), custom_call_target="tpu_custom_call" | custom-call | tf_op jit(solution)/shard_map/image/pallas_call | solution.py:75
  62.1 25.2 %all_to_all.10 = s16[32,136,128]{2,1,0:T(8,128)(2,1)S(1)} all-to-all(s16[32,136,128]{2,1,0:T(8,128)(2,1)S(1)} %bitcast.40), channel_id=1, replica_groups={{0,2,4,6,8,10,12,14,16,18,20,22,24,26,28,30,32,34,36,38,40,42,44,46,48,..., dimensions={0} | all-to-all | bytes 2228224 | tf_op jit(solution)/shard_map/all_to_all | solution.py:652
  87.4 1.9 %combine.1 = (f32[16,8,128]{2,1,0:T(8,128)S(1)}, f32[16,8,128]{2,1,0:T(8,128)S(1)}) custom-call(s16[544,8,128]{2,1,0:T(8,128)(2,1)S(1)} %bitcast.38), custom_call_target="tpu_custom_call" | custom-call | tf_op jit(solution)/shard_map/combine/pallas_call | solution.py:75
  89.3 0.9 collective-permute-start.3
  90.2 5.4 %collective-permute-done.3.came = f32[16,8,128]{2,1,0:T(8,128)S(1)} collective-permute-done((f32[16,8,128]{2,1,0:T(8,128)S(1)}, f32[16,8,128]{2,1,0:T(8,128)S(1)}, u32[]{:S(2)}, u32[]{:S(2)}) %collective-permute-start.3) | collective-permute-done | bytes 65568 | tf_op jit(solution)/shard_map/ppermute | solution.py:676
  95.6 0.1 collective-permute-start.4
  95.7 4.9 %collective-permute-done.4.came = f32[8,8,128]{2,1,0:T(8,128)S(1)} collective-permute-done((f32[8,8,128]{2,1,0:T(8,128)S(1)}, f32[8,8,128]{2,1,0:T(8,128)S(1)}, u32[]{:S(2)}, u32[]{:S(2)}) %collective-permute-start.4) | collective-permute-done | bytes 32800 | tf_op jit(solution)/shard_map/ppermute | solution.py:679
  100.6 0.6 last_sum.1
  (23 shorter events, 0.1 us)
Async XLA Ops:
  0.6 19.5 %copy-start.2 = (f32[1,32,64,128]{3,2,1,0:T(8,128)S(1)}, f32[1,32,64,128]{3,2,1,0:T(8,128)}, u32[]{:S(2)}) copy-start(f32[1,32,64,128]{3,2,1,0:T(8,128)} %param.14) | copy-start | bytes 3145732
  3.2 17.0 %copy-start = (f32[1,32,64,128]{3,2,1,0:T(8,128)S(1)}, f32[1,32,64,128]{3,2,1,0:T(8,128)}, u32[]{:S(2)}) copy-start(f32[1,32,64,128]{3,2,1,0:T(8,128)} %param.17) | copy-start | bytes 3145732
  3.2 17.0 %copy-start.1 = (f32[1,32,64,128]{3,2,1,0:T(8,128)S(1)}, f32[1,32,64,128]{3,2,1,0:T(8,128)}, u32[]{:S(2)}) copy-start(f32[1,32,64,128]{3,2,1,0:T(8,128)} %param.18) | copy-start | bytes 3145732
  3.2 48.7 %all-to-all-start = ((bf16[128,2,2176]{2,1,0:T(2,128)(2,1)}), bf16[128,2,2176]{2,1,0:T(2,128)(2,1)}, u32[]{:S(2)}, u32[]{:S(2)}) async-start(bf16[128,2,2176]{2,1,0:T(2,128)(2,1)} %pack_traces.1), calls=%async_computation | async-start | bytes 2228224 | tf_op jit(solution)/shard_map/all_to_all | solution.py:567
  20.2 5.5 %copy-start.3 = (f32[1,32,64,128]{3,2,1,0:T(8,128)S(1)}, f32[1,32,64,128]{3,2,1,0:T(8,128)}, u32[]{:S(2)}) copy-start(f32[1,32,64,128]{3,2,1,0:T(8,128)} %param.16) | copy-start | bytes 3145732
  20.2 5.5 %copy-start.6 = (f32[1,32,64,128]{3,2,1,0:T(8,128)S(1)}, f32[1,32,64,128]{3,2,1,0:T(8,128)}, u32[]{:S(2)}) copy-start(f32[1,32,64,128]{3,2,1,0:T(8,128)} %param.13) | copy-start | bytes 3145732
  20.2 5.5 %copy-start.7 = (f32[1,32,64,128]{3,2,1,0:T(8,128)S(1)}, f32[1,32,64,128]{3,2,1,0:T(8,128)}, u32[]{:S(2)}) copy-start(f32[1,32,64,128]{3,2,1,0:T(8,128)} %param.15) | copy-start | bytes 3145732
  22.2 3.5 %collective-permute-start = (f32[64,128]{1,0:T(8,128)S(1)}, f32[64,128]{1,0:T(8,128)S(1)}, u32[]{:S(2)}, u32[]{:S(2)}) collective-permute-start(f32[64,128]{1,0:T(8,128)S(1)} %faces.1), channel_id=1, source_target_pairs={{0,1},{1,0},{2,3},{3,2},{4,5},{5,4},{6,7},{7,6},{8,9},{9,8},{10,11... | collective-permute-start | bytes 98312 | tf_op jit(solution)/shard_map/ppermute | solution.py:521
  25.7 8.0 %copy-start.11 = (s32[1,256]{1,0:T(1,128)S(1)}, s32[1,256]{1,0:T(1,128)}, u32[]{:S(2)}) copy-start(s32[1,256]{1,0:T(1,128)} %at.3) | copy-start | bytes 3076
  25.7 7.9 %copy-start.13 = (s32[256,1]{0,1:T(1,128)S(1)}, s32[256,1]{0,1:T(1,128)}, u32[]{:S(2)}) copy-start(s32[256,1]{0,1:T(1,128)} %param.24) | copy-start | bytes 3076
  25.7 7.9 %copy-start.14 = (s32[256]{0:T(256)S(1)}, s32[256]{0:T(256)}, u32[]{:S(2)}) copy-start(s32[256]{0:T(256)} %param.25) | copy-start | bytes 3076
  32.5 3.5 %collective-permute-start.1 = (f32[64,128]{1,0:T(8,128)S(1)}, f32[64,128]{1,0:T(8,128)S(1)}, u32[]{:S(2)}, u32[]{:S(2)}) collective-permute-start(f32[64,128]{1,0:T(8,128)S(1)} %get-tuple-element.31), channel_id=1, source_target_pairs={{0,1},{1,0},{2,3},{3,2},{4,5},{5,4},{6,7},{7,6},{8,9},{9,8},{10,11... | collective-permute-start | bytes 98312 | tf_op jit(solution)/shard_map/ppermute | solution.py:521
  40.8 14.1 %copy-start.5 = (f32[32,64,128]{2,1,0:T(8,128)S(1)}, f32[32,64,128]{2,1,0:T(8,128)}, u32[]{:S(2)}) copy-start(f32[32,64,128]{2,1,0:T(8,128)} %get-tuple-element.43) | copy-start | bytes 3145732
  51.9 5.4 %copy-start.4 = (f32[1,32,64,128]{3,2,1,0:T(8,128)S(1)}, f32[1,32,64,128]{3,2,1,0:T(8,128)}, u32[]{:S(2)}) copy-start(f32[1,32,64,128]{3,2,1,0:T(8,128)} %param.16) | copy-start | bytes 3145732
  51.9 5.4 %copy-start.8 = (f32[256,128]{1,0:T(8,128)S(1)}, f32[256,128]{1,0:T(8,128)}, u32[]{:S(2)}) copy-start(f32[256,128]{1,0:T(8,128)} %get-tuple-element.50.refs_12_) | copy-start | bytes 393220
  51.9 5.4 %copy-start.9 = (bf16[32,256]{1,0:T(8,128)(2,1)S(1)}, bf16[32,256]{1,0:T(8,128)(2,1)}, u32[]{:S(2)}) copy-start(bf16[32,256]{1,0:T(8,128)(2,1)} %get-tuple-element.49.refs_11_) | copy-start | bytes 49156
  51.9 5.4 %copy-start.10 = (f32[32,128]{1,0:T(8,128)S(1)}, f32[32,128]{1,0:T(8,128)}, u32[]{:S(2)}) copy-start(f32[32,128]{1,0:T(8,128)} %get-tuple-element.51.refs_13_) | copy-start | bytes 49156
  51.9 5.4 %copy-start.12 = (s32[1,256]{1,0:T(1,128)S(1)}, s32[1,256]{1,0:T(1,128)}, u32[]{:S(2)}) copy-start(s32[1,256]{1,0:T(1,128)} %get-tuple-element.48.refs_10_) | copy-start | bytes 3076
  54.4 2.9 %collective-permute-start.2 = (f32[64,128]{1,0:T(8,128)S(1)}, f32[64,128]{1,0:T(8,128)S(1)}, u32[]{:S(2)}, u32[]{:S(2)}) collective-permute-start(f32[64,128]{1,0:T(8,128)S(1)} %get-tuple-element.40), channel_id=1, source_target_pairs={{0,1},{1,0},{2,3},{3,2},{4,5},{5,4},{6,7},{7,6},{8,9},{9,8},{10,11... | collective-permute-start | bytes 98312 | tf_op jit(solution)/shard_map/ppermute | solution.py:521
  89.3 6.3 %collective-permute-start.3 = (f32[16,8,128]{2,1,0:T(8,128)S(1)}, f32[16,8,128]{2,1,0:T(8,128)S(1)}, u32[]{:S(2)}, u32[]{:S(2)}) collective-permute-start(f32[16,8,128]{2,1,0:T(8,128)S(1)} %get-tuple-element.54), channel_id=1, source_target_pairs={{0,64},{2,66},{4,68},{6,70},{8,72},{10,74},{12,76},{14,78},{16,80}... | collective-permute-start | bytes 196616 | tf_op jit(solution)/shard_map/ppermute | solution.py:676
  95.6 5.0 %collective-permute-start.4 = (f32[8,8,128]{2,1,0:T(8,128)S(1)}, f32[8,8,128]{2,1,0:T(8,128)S(1)}, u32[]{:S(2)}, u32[]{:S(2)}) collective-permute-start(f32[8,8,128]{2,1,0:T(8,128)S(1)} %get-tuple-element.56), channel_id=1, source_target_pairs={{0,192},{2,194},{4,196},{6,198},{8,200},{10,202},{12,204},{14,206}... | collective-permute-start | bytes 98312 | tf_op jit(solution)/shard_map/ppermute | solution.py:679

commit v9 on v8

--- a/solution.py
+++ b/solution.py
@@ -463,7 +463,9 @@
     keep_last.wait()
 
 
-def combine_kernel(got, keep_out, send_out, gains_v, slots_v, gains, slots, sems, total, *partial):
+def combine_kernel(
+    got, keep_out, one_out, two_out, three_out, gains_v, slots_v, gains, slots, sems, total, *partial
+):
     per_class = got.shape[0] // CLASSES
     used = per_class - 1
     for c in range(CLASSES):
@@ -498,23 +500,12 @@
         parts = [partial[(ring % 2) * CAPT + rank][own] for rank in range(CAPT)]
         total[ring * MT_DEV : (ring + 1) * MT_DEV] = (parts[0] + parts[1]) + (parts[2] + parts[3])
     ring = lax.shift_right_logical(lax.axis_index("shot"), CLASS_SHIFT)
-
-    def owned(other):
-        return total[pl.ds((ring ^ other) * MT_DEV, MT_DEV)]
-
-    keep_out[:MT_DEV] = owned(0)
-    keep_out[MT_DEV:] = owned(3)
-    send_out[:MT_DEV] = owned(1)
-    send_out[MT_DEV:] = owned(2)
-
-
-def fold_kernel(kept, came, keep_out, send_out):
-    keep_out[...] = kept[:MT_DEV] + came[:MT_DEV]
-    send_out[...] = kept[MT_DEV:] + came[MT_DEV:]
-
-
-def last_kernel(kept, came, out):
-    out[...] = kept[...] + came[...]
+    for other, out in enumerate((keep_out, one_out, two_out, three_out)):
+        out[...] = total[pl.ds((ring ^ other) * MT_DEV, MT_DEV)]
+
+
+def last_kernel(kept, one, two, three, out):
+    out[...] = (kept[...] + one[...]) + (two[...] + three[...])
 
 
 def swap(face):
@@ -658,11 +649,11 @@
         tiled=True,
     )
     table = (CLASSES, lanes)
-    half = sds((rings // 2 * MT_DEV, 8, lanes))
-    kept, sent = call(
+    quarter = sds((MT_DEV, 8, lanes))
+    kept, *sent = call(
         combine_kernel,
         "combine",
-        (half, half),
+        (quarter,) * RINGS,
         [
             pltpu.VMEM(table, F32),
             pltpu.VMEM(table, I32),
@@ -671,13 +662,13 @@
             pltpu.SemaphoreType.DMA((2,)),
             pltpu.VMEM((rings * MT_DEV, 8, lanes), F32),
         ]
-        + [pltpu.VMEM(half.shape, F32)] * (2 * CAPT),
+        + [pltpu.VMEM((rings // 2 * MT_DEV, 8, lanes), F32)] * (2 * CAPT),
     )(got.reshape(CLASSES * per_class, 8, lanes))
-    came = lax.ppermute(sent, "shot", [(i, i ^ CLASSES) for i in range(shots)])
-    quarter = sds((MT_DEV, 8, lanes))
-    kept, sent = call(fold_kernel, "fold", (quarter, quarter))(kept, came)
-    came = lax.ppermute(sent, "shot", [(i, i ^ (3 * CLASSES)) for i in range(shots)])
-    model_grad = call(last_kernel, "last_sum", quarter, hbm_out=(0,))(kept, came)
+    came = [
+        lax.ppermute(part, "shot", [(i, i ^ (k * CLASSES)) for i in range(shots)])
+        for k, part in enumerate(sent, 1)
+    ]
+    model_grad = call(last_kernel, "last_sum", quarter, hbm_out=(0,))(kept, *came)
     return (model_grad, wave_end.reshape(1, *now.shape), adj_end[None])
 
 

time: 101 us -> 99.4 us (0.984)
  waiting for transfers between devices: 24.9 us -> 18.1 us
  starting transfers between devices: 20 us -> 24.8 us
    ppermute x2 -> x3, waiting for transfers between devices: 10.2 us -> 3.44 us  [local(): lax.ppermute(part, 'shot', [(i, i ^ k * CLASSES) for i in range(shots)])]
    ppermute x2 -> x3, starting transfers between devices: 1.02 us -> 5.74 us  [local(): lax.ppermute(part, 'shot', [(i, i ^ k * CLASSES) for i in range(shots)])]
    pallas_call x12 -> x11, Pallas kernels: 30.1 us -> 30.1 us  [run(): pl.pallas_call(body, out_shape=jax.tree.unflatten(tree, shapes), in_specs...]
  transfers between devices with their start and end apart: 6 -> 7, of which waited for: 6 -> 6; matrix products, arithmetic and copies ran while one was open for 0% -> 0% of each run, Pallas kernels for 17% -> 18%
where the time goes in v9:
time: 99.4 us; the launch traced here: 99.1 us
  Pallas kernels  30.1 us (30%)
  blocking collectives  25.2 us (25%)
  starting transfers between devices  24.8 us (25%)
  waiting for transfers between devices  18.1 us (18%)
    pallas_call x11, Pallas kernels, run(): pl.pallas_call(body, out_shape=jax.tree.unflatten(tree, shapes), in_specs...  30.1 us
    all_to_all x1, blocking collectives, local(): lax.all_to_all(send.reshape(CLASSES, per_class * 8, lanes), 'shot', split...  25.2 us
    all_to_all x1, starting transfers between devices, local(): lax.all_to_all(packed, 'shot', split_axis=0, concat_axis=0, tiled=True)  17 us
    all_to_all x1, waiting for transfers between devices, local(): lax.all_to_all(packed, 'shot', split_axis=0, concat_axis=0, tiled=True)  11 us
    ppermute x3, starting transfers between devices, local(): lax.ppermute(part, 'shot', [(i, i ^ k * CLASSES) for i in range(shots)])  5.74 us
    ppermute x3, waiting for transfers between devices, swap(): return lax.ppermute(face, 'ap', [(0, 1), (1, 0)])  3.68 us
    ppermute x3, waiting for transfers between devices, local(): lax.ppermute(part, 'shot', [(i, i ^ k * CLASSES) for i in range(shots)])  3.44 us
    ppermute x3, starting transfers between devices, swap(): return lax.ppermute(face, 'ap', [(0, 1), (1, 0)])  2.06 us
  transfers between devices with their start and end apart: 7, of which 6 were waited for; matrix products, arithmetic and copies ran while one was open for 0% of the time, Pallas kernels for 18%

profile of v9, /device:TPU:1, one launch (start us, length us, event | category | flops | bytes accessed | tf_op | source)
XLA Modules:
  0.0 99.1 jit_solution(3918511789242877787)
XLA Ops:
  0.6 2.5 %pack_traces.1 = bf16[128,2,2176]{2,1,0:T(2,128)(2,1)} custom-call(s32[1,128]{1,0:T(1,128)} %bitcast.52, s32[1,128]{1,0:T(1,128)} %bitcast.53, bf16[128,2048]{1,0:T(8,128)(2,1)} %traces_in.1), custom_call_target="tpu_custom_call" | custom-call | tf_op jit(solution)/shard_map/pack_traces/pallas_call | solution.py:75
  3.2 0.0 copy-start
  3.2 0.0 copy-start.1
  3.2 17.0 %all-to-all-start = ((bf16[128,2,2176]{2,1,0:T(2,128)(2,1)}), bf16[128,2,2176]{2,1,0:T(2,128)(2,1)}, u32[]{:S(2)}, u32[]{:S(2)}) async-start(bf16[128,2,2176]{2,1,0:T(2,128)(2,1)} %pack_traces.1), calls=%async_computation | async-start | bytes 2228224 | tf_op jit(solution)/shard_map/all_to_all | solution.py:558
  20.2 0.0 copy-start.3
  20.2 0.0 copy-start.6
  20.2 0.0 copy-start.7
  20.2 1.9 %faces.1 = f32[64,128]{1,0:T(8,128)S(1)} custom-call(f32[32,64,128]{2,1,0:T(8,128)S(1)} %bitcast.32, f32[32,64,128]{2,1,0:T(8,128)S(1)} %bitcast.28, f32[32,64,128]{2,1,0:T(8,128)S(1)} %bitcast.23, f32[32,64,128]{2,1,0:T(8,128)} %bitcast.35), custom_call_target="tpu_custom_call" | custom-call | tf_op jit(solution)/shard_map/faces/pallas_call | solution.py:75
  22.2 0.5 collective-permute-start
  22.6 3.0 %collective-permute-done.faces.refs_0_ = f32[64,128]{1,0:T(8,128)S(1)} collective-permute-done((f32[64,128]{1,0:T(8,128)S(1)}, f32[64,128]{1,0:T(8,128)S(1)}, u32[]{:S(2)}, u32[]{:S(2)}) %collective-permute-start) | collective-permute-done | bytes 32800 | tf_op jit(solution)/shard_map/ppermute | solution.py:512
  25.7 0.0 copy-start.14
  25.7 6.8 %first_step.1 = (f32[32,64,128]{2,1,0:T(8,128)S(1)}, f32[32,64,128]{2,1,0:T(8,128)S(1)}, f32[32,64,128]{2,1,0:T(8,128)S(1)}, f32[64,128]{1,0:T(8,128)S(1)}) custom-call(f32[64,128]{1,0:T(8,128)S(1)} %collective-permute-done.faces.refs_0_, f32[32,64,128]{2,1,0:T(8,128)S(1)} %bitcast.33, f32[32,64,128]{2,1,0:T(8,128)S(1)} %bitcast.44, ...), custom_call_target="tpu_custom_call" | custom-call | tf_op jit(solution)/shard_map/first_step/pallas_call | solution.py:75
  32.5 1.1 %collective-permute-start.1 = (f32[64,128]{1,0:T(8,128)S(1)}, f32[64,128]{1,0:T(8,128)S(1)}, u32[]{:S(2)}, u32[]{:S(2)}) collective-permute-start(f32[64,128]{1,0:T(8,128)S(1)} %get-tuple-element.31), channel_id=1, source_target_pairs={{0,1},{1,0},{2,3},{3,2},{4,5},{5,4},{6,7},{7,6},{8,9},{9,8},{10,11... | collective-permute-start | bytes 98312 | tf_op jit(solution)/shard_map/ppermute | solution.py:512
  33.6 2.2 %places.1 = (f32[256,256]{1,0:T(8,128)}, bf16[64,256]{1,0:T(8,128)(2,1)}, s32[1,256]{1,0:T(1,128)}, bf16[32,256]{1,0:T(8,128)(2,1)}, f32[256,128]{1,0:T(8,128)}, /*index=5*/f32[32,128]{1,0:T(8,128)}) custom-call(s32[1,256]{1,0:T(1,128)S(1)} %copy-done.11, s32[1,256]{1,0:T(1,128)S(1)} %copy-done.11, f32[2048,128]{1,0:T(8,128)S(1)} %bitcast.25, ...), custom_call_target="tpu_custom_call" | custom-call | tf_op jit(solution)/shard_map/places/pallas_call | solution.py:75
  35.9 0.1 collective-permute-done.1.mid_face.refs_1_
  36.0 2.9 %second_step.1 = (f32[32,64,128]{2,1,0:T(8,128)S(1)}, f32[32,64,128]{2,1,0:T(8,128)S(1)}, f32[32,64,128]{2,1,0:T(8,128)}, f32[32,64,128]{2,1,0:T(8,128)}) custom-call(f32[64,128]{1,0:T(8,128)S(1)} %collective-permute-done.faces.refs_0_, f32[64,128]{1,0:T(8,128)S(1)} %collective-permute-done.1.mid_face.refs_1_, f32[32,64,128]{2,1,0:T(8,128)S(1)} %get-tuple-element.33.mid, ...), custom_call_target="tpu_custom_call" | custom-call | tf_op jit(solution)/shard_map/second_step/pallas_call | solution.py:75
  38.9 1.9 %seen.1 = (f32[256,128]{1,0:T(8,128)S(1)}, f32[2048,128]{1,0:T(8,128)}, f32[2048,128]{1,0:T(8,128)}) custom-call(s32[1,256]{1,0:T(1,128)S(1)} %copy-done.11, f32[256,256]{1,0:T(8,128)} %get-tuple-element.32.refs_1_.refs_3_, f32[2048,128]{1,0:T(8,128)S(1)} %bitcast.39, f32[2048,128]{1,0:T(8,128)S(1)} %bitcast.43, f32[2048,128]{1,0:T(8,128)S(1)} %bitcast.42), custom_call_target="tpu_custom_call" | custom-call | tf_op jit(solution)/shard_map/seen/pallas_call | solution.py:75
  40.8 0.0 copy-start.5
  40.8 11.0 %all-to-all-done.refs_0_ = bf16[128,2,2176]{2,1,0:T(2,128)(2,1)} async-done(((bf16[128,2,2176]{2,1,0:T(2,128)(2,1)}), bf16[128,2,2176]{2,1,0:T(2,128)(2,1)}, u32[]{:S(2)}, u32[]{:S(2)}) %all-to-all-start) | async-done | bytes 1114144 | tf_op jit(solution)/shard_map/all_to_all | solution.py:558
  51.9 2.5 %residual.1 = (f32[256,128]{1,0:T(8,128)S(1)}, f32[256,128]{1,0:T(8,128)S(1)}, f32[64,128]{1,0:T(8,128)S(1)}) custom-call(bf16[128,2,2176]{2,1,0:T(2,128)(2,1)} %all-to-all-done.refs_0_, bf16[2,2048]{1,0:T(2,128)(2,1)} %bitcast.51, f32[256,128]{1,0:T(8,128)S(1)} %get-tuple-element.38.refs_2_, f32[256,256]{1,0:T(8,128)} %get-tuple-element.32.refs_1_.refs_3_, ...), custom_call_target="tpu_custom_call" | custom-call | tf_op jit(solution)/shard_map/residual/pallas_call | solution.py:75
  54.4 0.5 collective-permute-start.2
  54.9 1.9 %inject.1 = (f32[2048,128]{1,0:T(8,128)S(1)}, f32[2048,128]{1,0:T(8,128)S(1)}) custom-call(s32[1,256]{1,0:T(1,128)S(1)} %copy-done.11, f32[256,128]{1,0:T(8,128)S(1)} %get-tuple-element.41.sum_mid, f32[256,128]{1,0:T(8,128)S(1)} %get-tuple-element.42.sum_end, f32[2048,128]{1,0:T(8,128)S(1)} %bitcast.41), custom_call_target="tpu_custom_call" | custom-call | tf_op jit(solution)/shard_map/inject/pallas_call | solution.py:75
  56.8 0.5 collective-permute-done.2.refs_2_
  57.3 4.8 %image.1 = (f32[32,64,128]{2,1,0:T(8,128)}, s16[544,8,128]{2,1,0:T(8,128)(2,1)S(1)}) custom-call(f32[64,128]{1,0:T(8,128)S(1)} %collective-permute-done.faces.refs_0_, f32[64,128]{1,0:T(8,128)S(1)} %collective-permute-done.1.mid_face.refs_1_, f32[64,128]{1,0:T(8,128)S(1)} %collective-permute-done.2.refs_2_, f32[32,64,128]{2,1,0:T(8,128)S(1)} %bitcast.46, ...), custom_call_target="tpu_custom_call" | custom-call | tf_op jit(solution)/shard_map/image/pallas_call | solution.py:75
  62.1 25.2 %all_to_all.10 = s16[32,136,128]{2,1,0:T(8,128)(2,1)S(1)} all-to-all(s16[32,136,128]{2,1,0:T(8,128)(2,1)S(1)} %bitcast.40), channel_id=1, replica_groups={{0,2,4,6,8,10,12,14,16,18,20,22,24,26,28,30,32,34,36,38,40,42,44,46,48,..., dimensions={0} | all-to-all | bytes 2228224 | tf_op jit(solution)/shard_map/all_to_all | solution.py:643
  87.4 1.9 %combine.1 = (f32[8,8,128]{2,1,0:T(8,128)S(1)}, f32[8,8,128]{2,1,0:T(8,128)S(1)}, f32[8,8,128]{2,1,0:T(8,128)S(1)}, f32[8,8,128]{2,1,0:T(8,128)S(1)}) custom-call(s16[544,8,128]{2,1,0:T(8,128)(2,1)S(1)} %bitcast.38), custom_call_target="tpu_custom_call" | custom-call | tf_op jit(solution)/shard_map/combine/pallas_call | solution.py:75
  89.3 0.9 collective-permute-start.3
  90.2 3.0 %collective-permute-start.4 = (f32[8,8,128]{2,1,0:T(8,128)S(1)}, f32[8,8,128]{2,1,0:T(8,128)S(1)}, u32[]{:S(2)}, u32[]{:S(2)}) collective-permute-start(f32[8,8,128]{2,1,0:T(8,128)S(1)} %get-tuple-element.55), channel_id=1, source_target_pairs={{0,128},{2,130},{4,132},{6,134},{8,136},{10,138},{12,140},{14,142}... | collective-permute-start | bytes 98312 | tf_op jit(solution)/shard_map/ppermute | solution.py:668
  93.3 1.8 %collective-permute-start.5 = (f32[8,8,128]{2,1,0:T(8,128)S(1)}, f32[8,8,128]{2,1,0:T(8,128)S(1)}, u32[]{:S(2)}, u32[]{:S(2)}) collective-permute-start(f32[8,8,128]{2,1,0:T(8,128)S(1)} %get-tuple-element.56), channel_id=1, source_target_pairs={{0,192},{2,194},{4,196},{6,198},{8,200},{10,202},{12,204},{14,206}... | collective-permute-start | bytes 98312 | tf_op jit(solution)/shard_map/ppermute | solution.py:668
  95.1 1.9 %collective-permute-done.4.two = f32[8,8,128]{2,1,0:T(8,128)S(1)} collective-permute-done((f32[8,8,128]{2,1,0:T(8,128)S(1)}, f32[8,8,128]{2,1,0:T(8,128)S(1)}, u32[]{:S(2)}, u32[]{:S(2)}) %collective-permute-start.4) | collective-permute-done | bytes 32800 | tf_op jit(solution)/shard_map/ppermute | solution.py:668
  96.9 1.6 %collective-permute-done.5.three = f32[8,8,128]{2,1,0:T(8,128)S(1)} collective-permute-done((f32[8,8,128]{2,1,0:T(8,128)S(1)}, f32[8,8,128]{2,1,0:T(8,128)S(1)}, u32[]{:S(2)}, u32[]{:S(2)}) %collective-permute-start.5) | collective-permute-done | bytes 32800 | tf_op jit(solution)/shard_map/ppermute | solution.py:668
  98.5 0.6 last_sum.1
  (24 shorter events, 0.1 us)
Async XLA Ops:
  0.6 19.5 %copy-start.2 = (f32[1,32,64,128]{3,2,1,0:T(8,128)S(1)}, f32[1,32,64,128]{3,2,1,0:T(8,128)}, u32[]{:S(2)}) copy-start(f32[1,32,64,128]{3,2,1,0:T(8,128)} %param.14) | copy-start | bytes 3145732
  3.2 17.0 %copy-start = (f32[1,32,64,128]{3,2,1,0:T(8,128)S(1)}, f32[1,32,64,128]{3,2,1,0:T(8,128)}, u32[]{:S(2)}) copy-start(f32[1,32,64,128]{3,2,1,0:T(8,128)} %param.17) | copy-start | bytes 3145732
  3.2 17.0 %copy-start.1 = (f32[1,32,64,128]{3,2,1,0:T(8,128)S(1)}, f32[1,32,64,128]{3,2,1,0:T(8,128)}, u32[]{:S(2)}) copy-start(f32[1,32,64,128]{3,2,1,0:T(8,128)} %param.18) | copy-start | bytes 3145732
  3.2 48.7 %all-to-all-start = ((bf16[128,2,2176]{2,1,0:T(2,128)(2,1)}), bf16[128,2,2176]{2,1,0:T(2,128)(2,1)}, u32[]{:S(2)}, u32[]{:S(2)}) async-start(bf16[128,2,2176]{2,1,0:T(2,128)(2,1)} %pack_traces.1), calls=%async_computation | async-start | bytes 2228224 | tf_op jit(solution)/shard_map/all_to_all | solution.py:558
  20.2 5.5 %copy-start.3 = (f32[1,32,64,128]{3,2,1,0:T(8,128)S(1)}, f32[1,32,64,128]{3,2,1,0:T(8,128)}, u32[]{:S(2)}) copy-start(f32[1,32,64,128]{3,2,1,0:T(8,128)} %param.16) | copy-start | bytes 3145732
  20.2 5.5 %copy-start.6 = (f32[1,32,64,128]{3,2,1,0:T(8,128)S(1)}, f32[1,32,64,128]{3,2,1,0:T(8,128)}, u32[]{:S(2)}) copy-start(f32[1,32,64,128]{3,2,1,0:T(8,128)} %param.13) | copy-start | bytes 3145732
  20.2 5.5 %copy-start.7 = (f32[1,32,64,128]{3,2,1,0:T(8,128)S(1)}, f32[1,32,64,128]{3,2,1,0:T(8,128)}, u32[]{:S(2)}) copy-start(f32[1,32,64,128]{3,2,1,0:T(8,128)} %param.15) | copy-start | bytes 3145732
  22.2 3.5 %collective-permute-start = (f32[64,128]{1,0:T(8,128)S(1)}, f32[64,128]{1,0:T(8,128)S(1)}, u32[]{:S(2)}, u32[]{:S(2)}) collective-permute-start(f32[64,128]{1,0:T(8,128)S(1)} %faces.1), channel_id=1, source_target_pairs={{0,1},{1,0},{2,3},{3,2},{4,5},{5,4},{6,7},{7,6},{8,9},{9,8},{10,11... | collective-permute-start | bytes 98312 | tf_op jit(solution)/shard_map/ppermute | solution.py:512
  25.7 8.0 %copy-start.11 = (s32[1,256]{1,0:T(1,128)S(1)}, s32[1,256]{1,0:T(1,128)}, u32[]{:S(2)}) copy-start(s32[1,256]{1,0:T(1,128)} %at.3) | copy-start | bytes 3076
  25.7 7.9 %copy-start.13 = (s32[256,1]{0,1:T(1,128)S(1)}, s32[256,1]{0,1:T(1,128)}, u32[]{:S(2)}) copy-start(s32[256,1]{0,1:T(1,128)} %param.24) | copy-start | bytes 3076
  25.7 7.9 %copy-start.14 = (s32[256]{0:T(256)S(1)}, s32[256]{0:T(256)}, u32[]{:S(2)}) copy-start(s32[256]{0:T(256)} %param.25) | copy-start | bytes 3076
  32.5 3.5 %collective-permute-start.1 = (f32[64,128]{1,0:T(8,128)S(1)}, f32[64,128]{1,0:T(8,128)S(1)}, u32[]{:S(2)}, u32[]{:S(2)}) collective-permute-start(f32[64,128]{1,0:T(8,128)S(1)} %get-tuple-element.31), channel_id=1, source_target_pairs={{0,1},{1,0},{2,3},{3,2},{4,5},{5,4},{6,7},{7,6},{8,9},{9,8},{10,11... | collective-permute-start | bytes 98312 | tf_op jit(solution)/shard_map/ppermute | solution.py:512
  40.8 14.1 %copy-start.5 = (f32[32,64,128]{2,1,0:T(8,128)S(1)}, f32[32,64,128]{2,1,0:T(8,128)}, u32[]{:S(2)}) copy-start(f32[32,64,128]{2,1,0:T(8,128)} %get-tuple-element.43) | copy-start | bytes 3145732
  51.9 5.4 %copy-start.4 = (f32[1,32,64,128]{3,2,1,0:T(8,128)S(1)}, f32[1,32,64,128]{3,2,1,0:T(8,128)}, u32[]{:S(2)}) copy-start(f32[1,32,64,128]{3,2,1,0:T(8,128)} %param.16) | copy-start | bytes 3145732
  51.9 5.4 %copy-start.8 = (f32[256,128]{1,0:T(8,128)S(1)}, f32[256,128]{1,0:T(8,128)}, u32[]{:S(2)}) copy-start(f32[256,128]{1,0:T(8,128)} %get-tuple-element.50.refs_12_) | copy-start | bytes 393220
  51.9 5.4 %copy-start.9 = (bf16[32,256]{1,0:T(8,128)(2,1)S(1)}, bf16[32,256]{1,0:T(8,128)(2,1)}, u32[]{:S(2)}) copy-start(bf16[32,256]{1,0:T(8,128)(2,1)} %get-tuple-element.49.refs_11_) | copy-start | bytes 49156
  51.9 5.4 %copy-start.10 = (f32[32,128]{1,0:T(8,128)S(1)}, f32[32,128]{1,0:T(8,128)}, u32[]{:S(2)}) copy-start(f32[32,128]{1,0:T(8,128)} %get-tuple-element.51.refs_13_) | copy-start | bytes 49156
  51.9 5.4 %copy-start.12 = (s32[1,256]{1,0:T(1,128)S(1)}, s32[1,256]{1,0:T(1,128)}, u32[]{:S(2)}) copy-start(s32[1,256]{1,0:T(1,128)} %get-tuple-element.48.refs_10_) | copy-start | bytes 3076
  54.4 2.9 %collective-permute-start.2 = (f32[64,128]{1,0:T(8,128)S(1)}, f32[64,128]{1,0:T(8,128)S(1)}, u32[]{:S(2)}, u32[]{:S(2)}) collective-permute-start(f32[64,128]{1,0:T(8,128)S(1)} %get-tuple-element.40), channel_id=1, source_target_pairs={{0,1},{1,0},{2,3},{3,2},{4,5},{5,4},{6,7},{7,6},{8,9},{9,8},{10,11... | collective-permute-start | bytes 98312 | tf_op jit(solution)/shard_map/ppermute | solution.py:512
  89.3 5.7 %collective-permute-start.3 = (f32[8,8,128]{2,1,0:T(8,128)S(1)}, f32[8,8,128]{2,1,0:T(8,128)S(1)}, u32[]{:S(2)}, u32[]{:S(2)}) collective-permute-start(f32[8,8,128]{2,1,0:T(8,128)S(1)} %get-tuple-element.54), channel_id=1, source_target_pairs={{0,64},{2,66},{4,68},{6,70},{8,72},{10,74},{12,76},{14,78},{16,80}... | collective-permute-start | bytes 98312 | tf_op jit(solution)/shard_map/ppermute | solution.py:668
  90.2 6.7 %collective-permute-start.4 = (f32[8,8,128]{2,1,0:T(8,128)S(1)}, f32[8,8,128]{2,1,0:T(8,128)S(1)}, u32[]{:S(2)}, u32[]{:S(2)}) collective-permute-start(f32[8,8,128]{2,1,0:T(8,128)S(1)} %get-tuple-element.55), channel_id=1, source_target_pairs={{0,128},{2,130},{4,132},{6,134},{8,136},{10,138},{12,140},{14,142}... | collective-permute-start | bytes 98312 | tf_op jit(solution)/shard_map/ppermute | solution.py:668
  93.3 5.2 %collective-permute-start.5 = (f32[8,8,128]{2,1,0:T(8,128)S(1)}, f32[8,8,128]{2,1,0:T(8,128)S(1)}, u32[]{:S(2)}, u32[]{:S(2)}) collective-permute-start(f32[8,8,128]{2,1,0:T(8,128)S(1)} %get-tuple-element.56), channel_id=1, source_target_pairs={{0,192},{2,194},{4,196},{6,198},{8,200},{10,202},{12,204},{14,206}... | collective-permute-start | bytes 98312 | tf_op jit(solution)/shard_map/ppermute | solution.py:668

commit v10 on v9

--- a/solution.py
+++ b/solution.py
@@ -444,7 +444,7 @@
             send_out[place[0, x * tiles + t]] = whole[t]
         return carry
 
-    lax.fori_loop(0, count, pack, 0, unroll=8)
+    lax.fori_loop(0, count, pack, 0, unroll=16)
     code = codes[...]
     upper = jnp.floor(code * (1.0 / 64.0))
     lower = code - 64.0 * upper
@@ -665,8 +665,8 @@
         + [pltpu.VMEM((rings // 2 * MT_DEV, 8, lanes), F32)] * (2 * CAPT),
     )(got.reshape(CLASSES * per_class, 8, lanes))
     came = [
-        lax.ppermute(part, "shot", [(i, i ^ (k * CLASSES)) for i in range(shots)])
-        for k, part in enumerate(sent, 1)
+        lax.ppermute(sent[k - 1], "shot", [(i, i ^ (k * CLASSES)) for i in range(shots)])
+        for k in (2, 3, 1)
     ]
     model_grad = call(last_kernel, "last_sum", quarter, hbm_out=(0,))(kept, *came)
     return (model_grad, wave_end.reshape(1, *now.shape), adj_end[None])

time: 99.4 us -> 98.7 us (level)
  transfers between devices with their start and end apart: 7 -> 7, of which waited for: 6 -> 7; matrix products, arithmetic and copies ran while one was open for 0% -> 0% of each run, Pallas kernels for 18% -> 18%
where the time goes in v10:
time: 98.7 us; the launch traced here: 98.4 us
  Pallas kernels  30 us (30%)
  blocking collectives  25.2 us (26%)
  starting transfers between devices  24.8 us (25%)
  waiting for transfers between devices  17.6 us (18%)
    pallas_call x11, Pallas kernels, run(): pl.pallas_call(body, out_shape=jax.tree.unflatten(tree, shapes), in_specs...  30 us
    all_to_all x1, blocking collectives, local(): lax.all_to_all(send.reshape(CLASSES, per_class * 8, lanes), 'shot', split...  25.2 us
    all_to_all x1, starting transfers between devices, local(): lax.all_to_all(packed, 'shot', split_axis=0, concat_axis=0, tiled=True)  17 us
    all_to_all x1, waiting for transfers between devices, local(): lax.all_to_all(packed, 'shot', split_axis=0, concat_axis=0, tiled=True)  11 us
    ppermute x3, starting transfers between devices, local(): lax.ppermute(sent[k - 1], 'shot', [(i, i ^ k * CLASSES) for i in range(sh...  5.74 us
    ppermute x3, waiting for transfers between devices, swap(): return lax.ppermute(face, 'ap', [(0, 1), (1, 0)])  3.68 us
    ppermute x3, waiting for transfers between devices, local(): lax.ppermute(sent[k - 1], 'shot', [(i, i ^ k * CLASSES) for i in range(sh...  2.86 us
    ppermute x3, starting transfers between devices, swap(): return lax.ppermute(face, 'ap', [(0, 1), (1, 0)])  2.06 us
  transfers between devices with their start and end apart: 7, of which 7 were waited for; matrix products, arithmetic and copies ran while one was open for 0% of the time, Pallas kernels for 18%

profile of v10, /device:TPU:1, one launch (start us, length us, event | category | flops | bytes accessed | tf_op | source)
XLA Modules:
  0.0 98.4 jit_solution(13190357157720111358)
XLA Ops:
  0.6 2.5 %pack_traces.1 = bf16[128,2,2176]{2,1,0:T(2,128)(2,1)} custom-call(s32[1,128]{1,0:T(1,128)} %bitcast.52, s32[1,128]{1,0:T(1,128)} %bitcast.53, bf16[128,2048]{1,0:T(8,128)(2,1)} %traces_in.1), custom_call_target="tpu_custom_call" | custom-call | tf_op jit(solution)/shard_map/pack_traces/pallas_call | solution.py:75
  3.2 0.0 copy-start
  3.2 0.0 copy-start.1
  3.2 17.0 %all-to-all-start = ((bf16[128,2,2176]{2,1,0:T(2,128)(2,1)}), bf16[128,2,2176]{2,1,0:T(2,128)(2,1)}, u32[]{:S(2)}, u32[]{:S(2)}) async-start(bf16[128,2,2176]{2,1,0:T(2,128)(2,1)} %pack_traces.1), calls=%async_computation | async-start | bytes 2228224 | tf_op jit(solution)/shard_map/all_to_all | solution.py:558
  20.2 0.0 copy-start.3
  20.2 0.0 copy-start.6
  20.2 0.0 copy-start.7
  20.2 1.9 %faces.1 = f32[64,128]{1,0:T(8,128)S(1)} custom-call(f32[32,64,128]{2,1,0:T(8,128)S(1)} %bitcast.32, f32[32,64,128]{2,1,0:T(8,128)S(1)} %bitcast.28, f32[32,64,128]{2,1,0:T(8,128)S(1)} %bitcast.23, f32[32,64,128]{2,1,0:T(8,128)} %bitcast.35), custom_call_target="tpu_custom_call" | custom-call | tf_op jit(solution)/shard_map/faces/pallas_call | solution.py:75
  22.2 0.5 collective-permute-start
  22.6 3.0 %collective-permute-done.faces.refs_0_ = f32[64,128]{1,0:T(8,128)S(1)} collective-permute-done((f32[64,128]{1,0:T(8,128)S(1)}, f32[64,128]{1,0:T(8,128)S(1)}, u32[]{:S(2)}, u32[]{:S(2)}) %collective-permute-start) | collective-permute-done | bytes 32800 | tf_op jit(solution)/shard_map/ppermute | solution.py:512
  25.7 0.0 copy-start.11
  25.7 6.8 %first_step.1 = (f32[32,64,128]{2,1,0:T(8,128)S(1)}, f32[32,64,128]{2,1,0:T(8,128)S(1)}, f32[32,64,128]{2,1,0:T(8,128)S(1)}, f32[64,128]{1,0:T(8,128)S(1)}) custom-call(f32[64,128]{1,0:T(8,128)S(1)} %collective-permute-done.faces.refs_0_, f32[32,64,128]{2,1,0:T(8,128)S(1)} %bitcast.33, f32[32,64,128]{2,1,0:T(8,128)S(1)} %bitcast.44, ...), custom_call_target="tpu_custom_call" | custom-call | tf_op jit(solution)/shard_map/first_step/pallas_call | solution.py:75
  32.5 1.1 %collective-permute-start.1 = (f32[64,128]{1,0:T(8,128)S(1)}, f32[64,128]{1,0:T(8,128)S(1)}, u32[]{:S(2)}, u32[]{:S(2)}) collective-permute-start(f32[64,128]{1,0:T(8,128)S(1)} %get-tuple-element.31), channel_id=1, source_target_pairs={{0,1},{1,0},{2,3},{3,2},{4,5},{5,4},{6,7},{7,6},{8,9},{9,8},{10,11... | collective-permute-start | bytes 98312 | tf_op jit(solution)/shard_map/ppermute | solution.py:512
  33.6 2.2 %places.1 = (f32[256,256]{1,0:T(8,128)}, bf16[64,256]{1,0:T(8,128)(2,1)}, s32[1,256]{1,0:T(1,128)}, bf16[32,256]{1,0:T(8,128)(2,1)}, f32[256,128]{1,0:T(8,128)}, /*index=5*/f32[32,128]{1,0:T(8,128)}) custom-call(s32[1,256]{1,0:T(1,128)S(1)} %copy-done.11, s32[1,256]{1,0:T(1,128)S(1)} %copy-done.11, f32[2048,128]{1,0:T(8,128)S(1)} %bitcast.25, ...), custom_call_target="tpu_custom_call" | custom-call | tf_op jit(solution)/shard_map/places/pallas_call | solution.py:75
  35.9 0.1 collective-permute-done.1.mid_face.refs_1_
  36.0 2.9 %second_step.1 = (f32[32,64,128]{2,1,0:T(8,128)S(1)}, f32[32,64,128]{2,1,0:T(8,128)S(1)}, f32[32,64,128]{2,1,0:T(8,128)}, f32[32,64,128]{2,1,0:T(8,128)}) custom-call(f32[64,128]{1,0:T(8,128)S(1)} %collective-permute-done.faces.refs_0_, f32[64,128]{1,0:T(8,128)S(1)} %collective-permute-done.1.mid_face.refs_1_, f32[32,64,128]{2,1,0:T(8,128)S(1)} %get-tuple-element.33.mid, ...), custom_call_target="tpu_custom_call" | custom-call | tf_op jit(solution)/shard_map/second_step/pallas_call | solution.py:75
  38.9 1.9 %seen.1 = (f32[256,128]{1,0:T(8,128)S(1)}, f32[2048,128]{1,0:T(8,128)}, f32[2048,128]{1,0:T(8,128)}) custom-call(s32[1,256]{1,0:T(1,128)S(1)} %copy-done.11, f32[256,256]{1,0:T(8,128)} %get-tuple-element.32.refs_1_.refs_3_, f32[2048,128]{1,0:T(8,128)S(1)} %bitcast.39, f32[2048,128]{1,0:T(8,128)S(1)} %bitcast.43, f32[2048,128]{1,0:T(8,128)S(1)} %bitcast.42), custom_call_target="tpu_custom_call" | custom-call | tf_op jit(solution)/shard_map/seen/pallas_call | solution.py:75
  40.8 11.0 %all-to-all-done.refs_0_ = bf16[128,2,2176]{2,1,0:T(2,128)(2,1)} async-done(((bf16[128,2,2176]{2,1,0:T(2,128)(2,1)}), bf16[128,2,2176]{2,1,0:T(2,128)(2,1)}, u32[]{:S(2)}, u32[]{:S(2)}) %all-to-all-start) | async-done | bytes 1114144 | tf_op jit(solution)/shard_map/all_to_all | solution.py:558
  51.9 2.5 %residual.1 = (f32[256,128]{1,0:T(8,128)S(1)}, f32[256,128]{1,0:T(8,128)S(1)}, f32[64,128]{1,0:T(8,128)S(1)}) custom-call(bf16[128,2,2176]{2,1,0:T(2,128)(2,1)} %all-to-all-done.refs_0_, bf16[2,2048]{1,0:T(2,128)(2,1)} %bitcast.51, f32[256,128]{1,0:T(8,128)S(1)} %get-tuple-element.38.refs_2_, f32[256,256]{1,0:T(8,128)} %get-tuple-element.32.refs_1_.refs_3_, ...), custom_call_target="tpu_custom_call" | custom-call | tf_op jit(solution)/shard_map/residual/pallas_call | solution.py:75
  54.4 0.5 collective-permute-start.2
  54.9 1.9 %inject.1 = (f32[2048,128]{1,0:T(8,128)S(1)}, f32[2048,128]{1,0:T(8,128)S(1)}) custom-call(s32[1,256]{1,0:T(1,128)S(1)} %copy-done.11, f32[256,128]{1,0:T(8,128)S(1)} %get-tuple-element.41.sum_mid, f32[256,128]{1,0:T(8,128)S(1)} %get-tuple-element.42.sum_end, f32[2048,128]{1,0:T(8,128)S(1)} %bitcast.41), custom_call_target="tpu_custom_call" | custom-call | tf_op jit(solution)/shard_map/inject/pallas_call | solution.py:75
  56.8 0.5 collective-permute-done.2.refs_2_
  57.3 4.7 %image.1 = (f32[32,64,128]{2,1,0:T(8,128)}, s16[544,8,128]{2,1,0:T(8,128)(2,1)S(1)}) custom-call(f32[64,128]{1,0:T(8,128)S(1)} %collective-permute-done.faces.refs_0_, f32[64,128]{1,0:T(8,128)S(1)} %collective-permute-done.1.mid_face.refs_1_, f32[64,128]{1,0:T(8,128)S(1)} %collective-permute-done.2.refs_2_, f32[32,64,128]{2,1,0:T(8,128)S(1)} %bitcast.46, ...), custom_call_target="tpu_custom_call" | custom-call | tf_op jit(solution)/shard_map/image/pallas_call | solution.py:75
  62.0 25.2 %all_to_all.10 = s16[32,136,128]{2,1,0:T(8,128)(2,1)S(1)} all-to-all(s16[32,136,128]{2,1,0:T(8,128)(2,1)S(1)} %bitcast.40), channel_id=1, replica_groups={{0,2,4,6,8,10,12,14,16,18,20,22,24,26,28,30,32,34,36,38,40,42,44,46,48,..., dimensions={0} | all-to-all | bytes 2228224 | tf_op jit(solution)/shard_map/all_to_all | solution.py:643
  87.3 1.9 %combine.1 = (f32[8,8,128]{2,1,0:T(8,128)S(1)}, f32[8,8,128]{2,1,0:T(8,128)S(1)}, f32[8,8,128]{2,1,0:T(8,128)S(1)}, f32[8,8,128]{2,1,0:T(8,128)S(1)}) custom-call(s16[544,8,128]{2,1,0:T(8,128)(2,1)S(1)} %bitcast.38), custom_call_target="tpu_custom_call" | custom-call | tf_op jit(solution)/shard_map/combine/pallas_call | solution.py:75
  89.2 1.8 %collective-permute-start.3 = (f32[8,8,128]{2,1,0:T(8,128)S(1)}, f32[8,8,128]{2,1,0:T(8,128)S(1)}, u32[]{:S(2)}, u32[]{:S(2)}) collective-permute-start(f32[8,8,128]{2,1,0:T(8,128)S(1)} %get-tuple-element.54), channel_id=1, source_target_pairs={{0,128},{2,130},{4,132},{6,134},{8,136},{10,138},{12,140},{14,142}... | collective-permute-start | bytes 98312 | tf_op jit(solution)/shard_map/ppermute | solution.py:668
  91.1 2.4 %collective-permute-start.4 = (f32[8,8,128]{2,1,0:T(8,128)S(1)}, f32[8,8,128]{2,1,0:T(8,128)S(1)}, u32[]{:S(2)}, u32[]{:S(2)}) collective-permute-start(f32[8,8,128]{2,1,0:T(8,128)S(1)} %get-tuple-element.55), channel_id=1, source_target_pairs={{0,192},{2,194},{4,196},{6,198},{8,200},{10,202},{12,204},{14,206}... | collective-permute-start | bytes 98312 | tf_op jit(solution)/shard_map/ppermute | solution.py:668
  93.4 1.5 %collective-permute-start.5 = (f32[8,8,128]{2,1,0:T(8,128)S(1)}, f32[8,8,128]{2,1,0:T(8,128)S(1)}, u32[]{:S(2)}, u32[]{:S(2)}) collective-permute-start(f32[8,8,128]{2,1,0:T(8,128)S(1)} %get-tuple-element.56), channel_id=1, source_target_pairs={{0,64},{2,66},{4,68},{6,70},{8,72},{10,74},{12,76},{14,78},{16,80}... | collective-permute-start | bytes 98312 | tf_op jit(solution)/shard_map/ppermute | solution.py:668
  95.0 1.1 %collective-permute-done.3.one = f32[8,8,128]{2,1,0:T(8,128)S(1)} collective-permute-done((f32[8,8,128]{2,1,0:T(8,128)S(1)}, f32[8,8,128]{2,1,0:T(8,128)S(1)}, u32[]{:S(2)}, u32[]{:S(2)}) %collective-permute-start.3) | collective-permute-done | bytes 32800 | tf_op jit(solution)/shard_map/ppermute | solution.py:668
  96.1 0.5 collective-permute-done.4.two
  96.6 1.2 %collective-permute-done.5.three = f32[8,8,128]{2,1,0:T(8,128)S(1)} collective-permute-done((f32[8,8,128]{2,1,0:T(8,128)S(1)}, f32[8,8,128]{2,1,0:T(8,128)S(1)}, u32[]{:S(2)}, u32[]{:S(2)}) %collective-permute-start.5) | collective-permute-done | bytes 32800 | tf_op jit(solution)/shard_map/ppermute | solution.py:668
  97.8 0.6 last_sum.1
  (24 shorter events, 0.1 us)
Async XLA Ops:
  0.6 19.5 %copy-start.2 = (f32[1,32,64,128]{3,2,1,0:T(8,128)S(1)}, f32[1,32,64,128]{3,2,1,0:T(8,128)}, u32[]{:S(2)}) copy-start(f32[1,32,64,128]{3,2,1,0:T(8,128)} %param.14) | copy-start | bytes 3145732
  3.2 17.0 %copy-start = (f32[1,32,64,128]{3,2,1,0:T(8,128)S(1)}, f32[1,32,64,128]{3,2,1,0:T(8,128)}, u32[]{:S(2)}) copy-start(f32[1,32,64,128]{3,2,1,0:T(8,128)} %param.17) | copy-start | bytes 3145732
  3.2 17.0 %copy-start.1 = (f32[1,32,64,128]{3,2,1,0:T(8,128)S(1)}, f32[1,32,64,128]{3,2,1,0:T(8,128)}, u32[]{:S(2)}) copy-start(f32[1,32,64,128]{3,2,1,0:T(8,128)} %param.18) | copy-start | bytes 3145732
  3.2 48.7 %all-to-all-start = ((bf16[128,2,2176]{2,1,0:T(2,128)(2,1)}), bf16[128,2,2176]{2,1,0:T(2,128)(2,1)}, u32[]{:S(2)}, u32[]{:S(2)}) async-start(bf16[128,2,2176]{2,1,0:T(2,128)(2,1)} %pack_traces.1), calls=%async_computation | async-start | bytes 2228224 | tf_op jit(solution)/shard_map/all_to_all | solution.py:558
  20.2 5.5 %copy-start.3 = (f32[1,32,64,128]{3,2,1,0:T(8,128)S(1)}, f32[1,32,64,128]{3,2,1,0:T(8,128)}, u32[]{:S(2)}) copy-start(f32[1,32,64,128]{3,2,1,0:T(8,128)} %param.16) | copy-start | bytes 3145732
  20.2 5.5 %copy-start.6 = (f32[1,32,64,128]{3,2,1,0:T(8,128)S(1)}, f32[1,32,64,128]{3,2,1,0:T(8,128)}, u32[]{:S(2)}) copy-start(f32[1,32,64,128]{3,2,1,0:T(8,128)} %param.13) | copy-start | bytes 3145732
  20.2 5.5 %copy-start.7 = (f32[1,32,64,128]{3,2,1,0:T(8,128)S(1)}, f32[1,32,64,128]{3,2,1,0:T(8,128)}, u32[]{:S(2)}) copy-start(f32[1,32,64,128]{3,2,1,0:T(8,128)} %param.15) | copy-start | bytes 3145732
  22.2 3.5 %collective-permute-start = (f32[64,128]{1,0:T(8,128)S(1)}, f32[64,128]{1,0:T(8,128)S(1)}, u32[]{:S(2)}, u32[]{:S(2)}) collective-permute-start(f32[64,128]{1,0:T(8,128)S(1)} %faces.1), channel_id=1, source_target_pairs={{0,1},{1,0},{2,3},{3,2},{4,5},{5,4},{6,7},{7,6},{8,9},{9,8},{10,11... | collective-permute-start | bytes 98312 | tf_op jit(solution)/shard_map/ppermute | solution.py:512
  25.7 8.0 %copy-start.11 = (s32[1,256]{1,0:T(1,128)S(1)}, s32[1,256]{1,0:T(1,128)}, u32[]{:S(2)}) copy-start(s32[1,256]{1,0:T(1,128)} %at.3) | copy-start | bytes 3076
  25.7 7.9 %copy-start.13 = (s32[256,1]{0,1:T(1,128)S(1)}, s32[256,1]{0,1:T(1,128)}, u32[]{:S(2)}) copy-start(s32[256,1]{0,1:T(1,128)} %param.24) | copy-start | bytes 3076
  25.7 7.9 %copy-start.14 = (s32[256]{0:T(256)S(1)}, s32[256]{0:T(256)}, u32[]{:S(2)}) copy-start(s32[256]{0:T(256)} %param.25) | copy-start | bytes 3076
  32.5 3.5 %collective-permute-start.1 = (f32[64,128]{1,0:T(8,128)S(1)}, f32[64,128]{1,0:T(8,128)S(1)}, u32[]{:S(2)}, u32[]{:S(2)}) collective-permute-start(f32[64,128]{1,0:T(8,128)S(1)} %get-tuple-element.31), channel_id=1, source_target_pairs={{0,1},{1,0},{2,3},{3,2},{4,5},{5,4},{6,7},{7,6},{8,9},{9,8},{10,11... | collective-permute-start | bytes 98312 | tf_op jit(solution)/shard_map/ppermute | solution.py:512
  40.8 14.1 %copy-start.5 = (f32[32,64,128]{2,1,0:T(8,128)S(1)}, f32[32,64,128]{2,1,0:T(8,128)}, u32[]{:S(2)}) copy-start(f32[32,64,128]{2,1,0:T(8,128)} %get-tuple-element.43) | copy-start | bytes 3145732
  51.9 5.4 %copy-start.4 = (f32[1,32,64,128]{3,2,1,0:T(8,128)S(1)}, f32[1,32,64,128]{3,2,1,0:T(8,128)}, u32[]{:S(2)}) copy-start(f32[1,32,64,128]{3,2,1,0:T(8,128)} %param.16) | copy-start | bytes 3145732
  51.9 5.4 %copy-start.8 = (f32[256,128]{1,0:T(8,128)S(1)}, f32[256,128]{1,0:T(8,128)}, u32[]{:S(2)}) copy-start(f32[256,128]{1,0:T(8,128)} %get-tuple-element.50.refs_12_) | copy-start | bytes 393220
  51.9 5.4 %copy-start.9 = (bf16[32,256]{1,0:T(8,128)(2,1)S(1)}, bf16[32,256]{1,0:T(8,128)(2,1)}, u32[]{:S(2)}) copy-start(bf16[32,256]{1,0:T(8,128)(2,1)} %get-tuple-element.49.refs_11_) | copy-start | bytes 49156
  51.9 5.4 %copy-start.10 = (f32[32,128]{1,0:T(8,128)S(1)}, f32[32,128]{1,0:T(8,128)}, u32[]{:S(2)}) copy-start(f32[32,128]{1,0:T(8,128)} %get-tuple-element.51.refs_13_) | copy-start | bytes 49156
  51.9 5.4 %copy-start.12 = (s32[1,256]{1,0:T(1,128)S(1)}, s32[1,256]{1,0:T(1,128)}, u32[]{:S(2)}) copy-start(s32[1,256]{1,0:T(1,128)} %get-tuple-element.48.refs_10_) | copy-start | bytes 3076
  54.4 2.9 %collective-permute-start.2 = (f32[64,128]{1,0:T(8,128)S(1)}, f32[64,128]{1,0:T(8,128)S(1)}, u32[]{:S(2)}, u32[]{:S(2)}) collective-permute-start(f32[64,128]{1,0:T(8,128)S(1)} %get-tuple-element.40), channel_id=1, source_target_pairs={{0,1},{1,0},{2,3},{3,2},{4,5},{5,4},{6,7},{7,6},{8,9},{9,8},{10,11... | collective-permute-start | bytes 98312 | tf_op jit(solution)/shard_map/ppermute | solution.py:512
  89.2 6.9 %collective-permute-start.3 = (f32[8,8,128]{2,1,0:T(8,128)S(1)}, f32[8,8,128]{2,1,0:T(8,128)S(1)}, u32[]{:S(2)}, u32[]{:S(2)}) collective-permute-start(f32[8,8,128]{2,1,0:T(8,128)S(1)} %get-tuple-element.54), channel_id=1, source_target_pairs={{0,128},{2,130},{4,132},{6,134},{8,136},{10,138},{12,140},{14,142}... | collective-permute-start | bytes 98312 | tf_op jit(solution)/shard_map/ppermute | solution.py:668
  91.1 5.5 %collective-permute-start.4 = (f32[8,8,128]{2,1,0:T(8,128)S(1)}, f32[8,8,128]{2,1,0:T(8,128)S(1)}, u32[]{:S(2)}, u32[]{:S(2)}) collective-permute-start(f32[8,8,128]{2,1,0:T(8,128)S(1)} %get-tuple-element.55), channel_id=1, source_target_pairs={{0,192},{2,194},{4,196},{6,198},{8,200},{10,202},{12,204},{14,206}... | collective-permute-start | bytes 98312 | tf_op jit(solution)/shard_map/ppermute | solution.py:668
  93.4 4.4 %collective-permute-start.5 = (f32[8,8,128]{2,1,0:T(8,128)S(1)}, f32[8,8,128]{2,1,0:T(8,128)S(1)}, u32[]{:S(2)}, u32[]{:S(2)}) collective-permute-start(f32[8,8,128]{2,1,0:T(8,128)S(1)} %get-tuple-element.56), channel_id=1, source_target_pairs={{0,64},{2,66},{4,68},{6,70},{8,72},{10,74},{12,76},{14,78},{16,80}... | collective-permute-start | bytes 98312 | tf_op jit(solution)/shard_map/ppermute | solution.py:668

commit v11 on v10

--- a/solution.py
+++ b/solution.py
@@ -425,7 +425,7 @@
         last_held[x] = 2.0 * here - nxt[x] + (0.5 * STEP) * lap + add[x]
         return flux
 
-    lax.fori_loop(0, count, body, buoy[0] * (bulk[0] * mid[0]), unroll=8)
+    lax.fori_loop(0, count, body, buoy[0] * (bulk[0] * mid[0]), unroll=16)
     keep_last = pltpu.make_async_copy(last_held, last_out, sem)
     keep_last.start()
     arrived()
@@ -494,7 +494,7 @@
             part[at] = part[at] + value
         return carry
 
-    lax.fori_loop(0, CLASSES, body, 0, unroll=2)
+    lax.fori_loop(0, CLASSES, body, 0, unroll=4)
     for ring in range(RINGS):
         own = slice((ring // 2) * MT_DEV, (ring // 2 + 1) * MT_DEV)
         parts = [partial[(ring % 2) * CAPT + rank][own] for rank in range(CAPT)]

time: 98.7 us -> 98.8 us (level)
  no operation moved by 1% of the time
where the time goes in v11:
time: 98.8 us; the launch traced here: 98.5 us
  Pallas kernels  30 us (30%)
  blocking collectives  25.2 us (26%)
  starting transfers between devices  24.8 us (25%)
  waiting for transfers between devices  17.6 us (18%)
    pallas_call x11, Pallas kernels, run(): pl.pallas_call(body, out_shape=jax.tree.unflatten(tree, shapes), in_specs...  30 us
    all_to_all x1, blocking collectives, local(): lax.all_to_all(send.reshape(CLASSES, per_class * 8, lanes), 'shot', split...  25.2 us
    all_to_all x1, starting transfers between devices, local(): lax.all_to_all(packed, 'shot', split_axis=0, concat_axis=0, tiled=True)  17 us
    all_to_all x1, waiting for transfers between devices, local(): lax.all_to_all(packed, 'shot', split_axis=0, concat_axis=0, tiled=True)  11 us
    ppermute x3, starting transfers between devices, local(): lax.ppermute(sent[k - 1], 'shot', [(i, i ^ k * CLASSES) for i in range(sh...  5.74 us
    ppermute x3, waiting for transfers between devices, swap(): return lax.ppermute(face, 'ap', [(0, 1), (1, 0)])  3.68 us
    ppermute x3, waiting for transfers between devices, local(): lax.ppermute(sent[k - 1], 'shot', [(i, i ^ k * CLASSES) for i in range(sh...  2.87 us
    ppermute x3, starting transfers between devices, swap(): return lax.ppermute(face, 'ap', [(0, 1), (1, 0)])  2.06 us
  transfers between devices with their start and end apart: 7, of which 7 were waited for; matrix products, arithmetic and copies ran while one was open for 0% of the time, Pallas kernels for 18%

profile of v11, /device:TPU:1, one launch (start us, length us, event | category | flops | bytes accessed | tf_op | source)
XLA Modules:
  0.0 98.5 jit_solution(16807147341091727123)
XLA Ops:
  0.6 2.5 %pack_traces.1 = bf16[128,2,2176]{2,1,0:T(2,128)(2,1)} custom-call(s32[1,128]{1,0:T(1,128)} %bitcast.52, s32[1,128]{1,0:T(1,128)} %bitcast.53, bf16[128,2048]{1,0:T(8,128)(2,1)} %traces_in.1), custom_call_target="tpu_custom_call" | custom-call | tf_op jit(solution)/shard_map/pack_traces/pallas_call | solution.py:75
  3.2 0.0 copy-start
  3.2 0.0 copy-start.1
  3.2 17.0 %all-to-all-start = ((bf16[128,2,2176]{2,1,0:T(2,128)(2,1)}), bf16[128,2,2176]{2,1,0:T(2,128)(2,1)}, u32[]{:S(2)}, u32[]{:S(2)}) async-start(bf16[128,2,2176]{2,1,0:T(2,128)(2,1)} %pack_traces.1), calls=%async_computation | async-start | bytes 2228224 | tf_op jit(solution)/shard_map/all_to_all | solution.py:558
  20.2 0.0 copy-start.3
  20.2 0.0 copy-start.6
  20.2 1.9 %faces.1 = f32[64,128]{1,0:T(8,128)S(1)} custom-call(f32[32,64,128]{2,1,0:T(8,128)S(1)} %bitcast.32, f32[32,64,128]{2,1,0:T(8,128)S(1)} %bitcast.28, f32[32,64,128]{2,1,0:T(8,128)S(1)} %bitcast.23, f32[32,64,128]{2,1,0:T(8,128)} %bitcast.35), custom_call_target="tpu_custom_call" | custom-call | tf_op jit(solution)/shard_map/faces/pallas_call | solution.py:75
  22.2 0.5 collective-permute-start
  22.6 3.0 %collective-permute-done.faces.refs_0_ = f32[64,128]{1,0:T(8,128)S(1)} collective-permute-done((f32[64,128]{1,0:T(8,128)S(1)}, f32[64,128]{1,0:T(8,128)S(1)}, u32[]{:S(2)}, u32[]{:S(2)}) %collective-permute-start) | collective-permute-done | bytes 32800 | tf_op jit(solution)/shard_map/ppermute | solution.py:512
  25.7 0.0 copy-start.11
  25.7 6.8 %first_step.1 = (f32[32,64,128]{2,1,0:T(8,128)S(1)}, f32[32,64,128]{2,1,0:T(8,128)S(1)}, f32[32,64,128]{2,1,0:T(8,128)S(1)}, f32[64,128]{1,0:T(8,128)S(1)}) custom-call(f32[64,128]{1,0:T(8,128)S(1)} %collective-permute-done.faces.refs_0_, f32[32,64,128]{2,1,0:T(8,128)S(1)} %bitcast.33, f32[32,64,128]{2,1,0:T(8,128)S(1)} %bitcast.44, ...), custom_call_target="tpu_custom_call" | custom-call | tf_op jit(solution)/shard_map/first_step/pallas_call | solution.py:75
  32.5 1.1 %collective-permute-start.1 = (f32[64,128]{1,0:T(8,128)S(1)}, f32[64,128]{1,0:T(8,128)S(1)}, u32[]{:S(2)}, u32[]{:S(2)}) collective-permute-start(f32[64,128]{1,0:T(8,128)S(1)} %get-tuple-element.31), channel_id=1, source_target_pairs={{0,1},{1,0},{2,3},{3,2},{4,5},{5,4},{6,7},{7,6},{8,9},{9,8},{10,11... | collective-permute-start | bytes 98312 | tf_op jit(solution)/shard_map/ppermute | solution.py:512
  33.6 2.2 %places.1 = (f32[256,256]{1,0:T(8,128)}, bf16[64,256]{1,0:T(8,128)(2,1)}, s32[1,256]{1,0:T(1,128)}, bf16[32,256]{1,0:T(8,128)(2,1)}, f32[256,128]{1,0:T(8,128)}, /*index=5*/f32[32,128]{1,0:T(8,128)}) custom-call(s32[1,256]{1,0:T(1,128)S(1)} %copy-done.11, s32[1,256]{1,0:T(1,128)S(1)} %copy-done.11, f32[2048,128]{1,0:T(8,128)S(1)} %bitcast.25, ...), custom_call_target="tpu_custom_call" | custom-call | tf_op jit(solution)/shard_map/places/pallas_call | solution.py:75
  35.9 0.1 collective-permute-done.1.mid_face.refs_1_
  36.0 2.9 %second_step.1 = (f32[32,64,128]{2,1,0:T(8,128)S(1)}, f32[32,64,128]{2,1,0:T(8,128)S(1)}, f32[32,64,128]{2,1,0:T(8,128)}, f32[32,64,128]{2,1,0:T(8,128)}) custom-call(f32[64,128]{1,0:T(8,128)S(1)} %collective-permute-done.faces.refs_0_, f32[64,128]{1,0:T(8,128)S(1)} %collective-permute-done.1.mid_face.refs_1_, f32[32,64,128]{2,1,0:T(8,128)S(1)} %get-tuple-element.33.mid, ...), custom_call_target="tpu_custom_call" | custom-call | tf_op jit(solution)/shard_map/second_step/pallas_call | solution.py:75
  38.9 1.9 %seen.1 = (f32[256,128]{1,0:T(8,128)S(1)}, f32[2048,128]{1,0:T(8,128)}, f32[2048,128]{1,0:T(8,128)}) custom-call(s32[1,256]{1,0:T(1,128)S(1)} %copy-done.11, f32[256,256]{1,0:T(8,128)} %get-tuple-element.32.refs_1_.refs_3_, f32[2048,128]{1,0:T(8,128)S(1)} %bitcast.39, f32[2048,128]{1,0:T(8,128)S(1)} %bitcast.43, f32[2048,128]{1,0:T(8,128)S(1)} %bitcast.42), custom_call_target="tpu_custom_call" | custom-call | tf_op jit(solution)/shard_map/seen/pallas_call | solution.py:75
  40.8 0.0 copy-start.5
  40.8 11.0 %all-to-all-done.refs_0_ = bf16[128,2,2176]{2,1,0:T(2,128)(2,1)} async-done(((bf16[128,2,2176]{2,1,0:T(2,128)(2,1)}), bf16[128,2,2176]{2,1,0:T(2,128)(2,1)}, u32[]{:S(2)}, u32[]{:S(2)}) %all-to-all-start) | async-done | bytes 1114144 | tf_op jit(solution)/shard_map/all_to_all | solution.py:558
  51.9 2.5 %residual.1 = (f32[256,128]{1,0:T(8,128)S(1)}, f32[256,128]{1,0:T(8,128)S(1)}, f32[64,128]{1,0:T(8,128)S(1)}) custom-call(bf16[128,2,2176]{2,1,0:T(2,128)(2,1)} %all-to-all-done.refs_0_, bf16[2,2048]{1,0:T(2,128)(2,1)} %bitcast.51, f32[256,128]{1,0:T(8,128)S(1)} %get-tuple-element.38.refs_2_, f32[256,256]{1,0:T(8,128)} %get-tuple-element.32.refs_1_.refs_3_, ...), custom_call_target="tpu_custom_call" | custom-call | tf_op jit(solution)/shard_map/residual/pallas_call | solution.py:75
  54.4 0.5 collective-permute-start.2
  54.9 1.9 %inject.1 = (f32[2048,128]{1,0:T(8,128)S(1)}, f32[2048,128]{1,0:T(8,128)S(1)}) custom-call(s32[1,256]{1,0:T(1,128)S(1)} %copy-done.11, f32[256,128]{1,0:T(8,128)S(1)} %get-tuple-element.41.sum_mid, f32[256,128]{1,0:T(8,128)S(1)} %get-tuple-element.42.sum_end, f32[2048,128]{1,0:T(8,128)S(1)} %bitcast.41), custom_call_target="tpu_custom_call" | custom-call | tf_op jit(solution)/shard_map/inject/pallas_call | solution.py:75
  56.8 0.5 collective-permute-done.2.refs_2_
  57.3 4.8 %image.1 = (f32[32,64,128]{2,1,0:T(8,128)}, s16[544,8,128]{2,1,0:T(8,128)(2,1)S(1)}) custom-call(f32[64,128]{1,0:T(8,128)S(1)} %collective-permute-done.faces.refs_0_, f32[64,128]{1,0:T(8,128)S(1)} %collective-permute-done.1.mid_face.refs_1_, f32[64,128]{1,0:T(8,128)S(1)} %collective-permute-done.2.refs_2_, f32[32,64,128]{2,1,0:T(8,128)S(1)} %bitcast.46, ...), custom_call_target="tpu_custom_call" | custom-call | tf_op jit(solution)/shard_map/image/pallas_call | solution.py:75
  62.1 25.2 %all_to_all.10 = s16[32,136,128]{2,1,0:T(8,128)(2,1)S(1)} all-to-all(s16[32,136,128]{2,1,0:T(8,128)(2,1)S(1)} %bitcast.40), channel_id=1, replica_groups={{0,2,4,6,8,10,12,14,16,18,20,22,24,26,28,30,32,34,36,38,40,42,44,46,48,..., dimensions={0} | all-to-all | bytes 2228224 | tf_op jit(solution)/shard_map/all_to_all | solution.py:643
  87.4 1.9 %combine.1 = (f32[8,8,128]{2,1,0:T(8,128)S(1)}, f32[8,8,128]{2,1,0:T(8,128)S(1)}, f32[8,8,128]{2,1,0:T(8,128)S(1)}, f32[8,8,128]{2,1,0:T(8,128)S(1)}) custom-call(s16[544,8,128]{2,1,0:T(8,128)(2,1)S(1)} %bitcast.38), custom_call_target="tpu_custom_call" | custom-call | tf_op jit(solution)/shard_map/combine/pallas_call | solution.py:75
  89.3 1.8 %collective-permute-start.3 = (f32[8,8,128]{2,1,0:T(8,128)S(1)}, f32[8,8,128]{2,1,0:T(8,128)S(1)}, u32[]{:S(2)}, u32[]{:S(2)}) collective-permute-start(f32[8,8,128]{2,1,0:T(8,128)S(1)} %get-tuple-element.54), channel_id=1, source_target_pairs={{0,128},{2,130},{4,132},{6,134},{8,136},{10,138},{12,140},{14,142}... | collective-permute-start | bytes 98312 | tf_op jit(solution)/shard_map/ppermute | solution.py:668
  91.1 2.4 %collective-permute-start.4 = (f32[8,8,128]{2,1,0:T(8,128)S(1)}, f32[8,8,128]{2,1,0:T(8,128)S(1)}, u32[]{:S(2)}, u32[]{:S(2)}) collective-permute-start(f32[8,8,128]{2,1,0:T(8,128)S(1)} %get-tuple-element.55), channel_id=1, source_target_pairs={{0,192},{2,194},{4,196},{6,198},{8,200},{10,202},{12,204},{14,206}... | collective-permute-start | bytes 98312 | tf_op jit(solution)/shard_map/ppermute | solution.py:668
  93.5 1.5 %collective-permute-start.5 = (f32[8,8,128]{2,1,0:T(8,128)S(1)}, f32[8,8,128]{2,1,0:T(8,128)S(1)}, u32[]{:S(2)}, u32[]{:S(2)}) collective-permute-start(f32[8,8,128]{2,1,0:T(8,128)S(1)} %get-tuple-element.56), channel_id=1, source_target_pairs={{0,64},{2,66},{4,68},{6,70},{8,72},{10,74},{12,76},{14,78},{16,80}... | collective-permute-start | bytes 98312 | tf_op jit(solution)/shard_map/ppermute | solution.py:668
  95.0 1.1 %collective-permute-done.3.one = f32[8,8,128]{2,1,0:T(8,128)S(1)} collective-permute-done((f32[8,8,128]{2,1,0:T(8,128)S(1)}, f32[8,8,128]{2,1,0:T(8,128)S(1)}, u32[]{:S(2)}, u32[]{:S(2)}) %collective-permute-start.3) | collective-permute-done | bytes 32800 | tf_op jit(solution)/shard_map/ppermute | solution.py:668
  96.1 0.5 collective-permute-done.4.two
  96.6 1.2 %collective-permute-done.5.three = f32[8,8,128]{2,1,0:T(8,128)S(1)} collective-permute-done((f32[8,8,128]{2,1,0:T(8,128)S(1)}, f32[8,8,128]{2,1,0:T(8,128)S(1)}, u32[]{:S(2)}, u32[]{:S(2)}) %collective-permute-start.5) | collective-permute-done | bytes 32800 | tf_op jit(solution)/shard_map/ppermute | solution.py:668
  97.9 0.6 last_sum.1
  (24 shorter events, 0.1 us)
Async XLA Ops:
  0.6 19.5 %copy-start.2 = (f32[1,32,64,128]{3,2,1,0:T(8,128)S(1)}, f32[1,32,64,128]{3,2,1,0:T(8,128)}, u32[]{:S(2)}) copy-start(f32[1,32,64,128]{3,2,1,0:T(8,128)} %param.14) | copy-start | bytes 3145732
  3.2 17.0 %copy-start = (f32[1,32,64,128]{3,2,1,0:T(8,128)S(1)}, f32[1,32,64,128]{3,2,1,0:T(8,128)}, u32[]{:S(2)}) copy-start(f32[1,32,64,128]{3,2,1,0:T(8,128)} %param.17) | copy-start | bytes 3145732
  3.2 17.0 %copy-start.1 = (f32[1,32,64,128]{3,2,1,0:T(8,128)S(1)}, f32[1,32,64,128]{3,2,1,0:T(8,128)}, u32[]{:S(2)}) copy-start(f32[1,32,64,128]{3,2,1,0:T(8,128)} %param.18) | copy-start | bytes 3145732
  3.2 48.7 %all-to-all-start = ((bf16[128,2,2176]{2,1,0:T(2,128)(2,1)}), bf16[128,2,2176]{2,1,0:T(2,128)(2,1)}, u32[]{:S(2)}, u32[]{:S(2)}) async-start(bf16[128,2,2176]{2,1,0:T(2,128)(2,1)} %pack_traces.1), calls=%async_computation | async-start | bytes 2228224 | tf_op jit(solution)/shard_map/all_to_all | solution.py:558
  20.2 5.5 %copy-start.3 = (f32[1,32,64,128]{3,2,1,0:T(8,128)S(1)}, f32[1,32,64,128]{3,2,1,0:T(8,128)}, u32[]{:S(2)}) copy-start(f32[1,32,64,128]{3,2,1,0:T(8,128)} %param.16) | copy-start | bytes 3145732
  20.2 5.5 %copy-start.6 = (f32[1,32,64,128]{3,2,1,0:T(8,128)S(1)}, f32[1,32,64,128]{3,2,1,0:T(8,128)}, u32[]{:S(2)}) copy-start(f32[1,32,64,128]{3,2,1,0:T(8,128)} %param.13) | copy-start | bytes 3145732
  20.2 5.5 %copy-start.7 = (f32[1,32,64,128]{3,2,1,0:T(8,128)S(1)}, f32[1,32,64,128]{3,2,1,0:T(8,128)}, u32[]{:S(2)}) copy-start(f32[1,32,64,128]{3,2,1,0:T(8,128)} %param.15) | copy-start | bytes 3145732
  22.2 3.5 %collective-permute-start = (f32[64,128]{1,0:T(8,128)S(1)}, f32[64,128]{1,0:T(8,128)S(1)}, u32[]{:S(2)}, u32[]{:S(2)}) collective-permute-start(f32[64,128]{1,0:T(8,128)S(1)} %faces.1), channel_id=1, source_target_pairs={{0,1},{1,0},{2,3},{3,2},{4,5},{5,4},{6,7},{7,6},{8,9},{9,8},{10,11... | collective-permute-start | bytes 98312 | tf_op jit(solution)/shard_map/ppermute | solution.py:512
  25.7 8.0 %copy-start.11 = (s32[1,256]{1,0:T(1,128)S(1)}, s32[1,256]{1,0:T(1,128)}, u32[]{:S(2)}) copy-start(s32[1,256]{1,0:T(1,128)} %at.3) | copy-start | bytes 3076
  25.7 7.9 %copy-start.13 = (s32[256,1]{0,1:T(1,128)S(1)}, s32[256,1]{0,1:T(1,128)}, u32[]{:S(2)}) copy-start(s32[256,1]{0,1:T(1,128)} %param.24) | copy-start | bytes 3076
  25.7 7.9 %copy-start.14 = (s32[256]{0:T(256)S(1)}, s32[256]{0:T(256)}, u32[]{:S(2)}) copy-start(s32[256]{0:T(256)} %param.25) | copy-start | bytes 3076
  32.5 3.5 %collective-permute-start.1 = (f32[64,128]{1,0:T(8,128)S(1)}, f32[64,128]{1,0:T(8,128)S(1)}, u32[]{:S(2)}, u32[]{:S(2)}) collective-permute-start(f32[64,128]{1,0:T(8,128)S(1)} %get-tuple-element.31), channel_id=1, source_target_pairs={{0,1},{1,0},{2,3},{3,2},{4,5},{5,4},{6,7},{7,6},{8,9},{9,8},{10,11... | collective-permute-start | bytes 98312 | tf_op jit(solution)/shard_map/ppermute | solution.py:512
  40.8 14.1 %copy-start.5 = (f32[32,64,128]{2,1,0:T(8,128)S(1)}, f32[32,64,128]{2,1,0:T(8,128)}, u32[]{:S(2)}) copy-start(f32[32,64,128]{2,1,0:T(8,128)} %get-tuple-element.43) | copy-start | bytes 3145732
  51.9 5.4 %copy-start.4 = (f32[1,32,64,128]{3,2,1,0:T(8,128)S(1)}, f32[1,32,64,128]{3,2,1,0:T(8,128)}, u32[]{:S(2)}) copy-start(f32[1,32,64,128]{3,2,1,0:T(8,128)} %param.16) | copy-start | bytes 3145732
  51.9 5.4 %copy-start.8 = (f32[256,128]{1,0:T(8,128)S(1)}, f32[256,128]{1,0:T(8,128)}, u32[]{:S(2)}) copy-start(f32[256,128]{1,0:T(8,128)} %get-tuple-element.50.refs_12_) | copy-start | bytes 393220
  51.9 5.4 %copy-start.9 = (bf16[32,256]{1,0:T(8,128)(2,1)S(1)}, bf16[32,256]{1,0:T(8,128)(2,1)}, u32[]{:S(2)}) copy-start(bf16[32,256]{1,0:T(8,128)(2,1)} %get-tuple-element.49.refs_11_) | copy-start | bytes 49156
  51.9 5.4 %copy-start.10 = (f32[32,128]{1,0:T(8,128)S(1)}, f32[32,128]{1,0:T(8,128)}, u32[]{:S(2)}) copy-start(f32[32,128]{1,0:T(8,128)} %get-tuple-element.51.refs_13_) | copy-start | bytes 49156
  51.9 5.4 %copy-start.12 = (s32[1,256]{1,0:T(1,128)S(1)}, s32[1,256]{1,0:T(1,128)}, u32[]{:S(2)}) copy-start(s32[1,256]{1,0:T(1,128)} %get-tuple-element.48.refs_10_) | copy-start | bytes 3076
  54.4 2.9 %collective-permute-start.2 = (f32[64,128]{1,0:T(8,128)S(1)}, f32[64,128]{1,0:T(8,128)S(1)}, u32[]{:S(2)}, u32[]{:S(2)}) collective-permute-start(f32[64,128]{1,0:T(8,128)S(1)} %get-tuple-element.40), channel_id=1, source_target_pairs={{0,1},{1,0},{2,3},{3,2},{4,5},{5,4},{6,7},{7,6},{8,9},{9,8},{10,11... | collective-permute-start | bytes 98312 | tf_op jit(solution)/shard_map/ppermute | solution.py:512
  89.3 6.9 %collective-permute-start.3 = (f32[8,8,128]{2,1,0:T(8,128)S(1)}, f32[8,8,128]{2,1,0:T(8,128)S(1)}, u32[]{:S(2)}, u32[]{:S(2)}) collective-permute-start(f32[8,8,128]{2,1,0:T(8,128)S(1)} %get-tuple-element.54), channel_id=1, source_target_pairs={{0,128},{2,130},{4,132},{6,134},{8,136},{10,138},{12,140},{14,142}... | collective-permute-start | bytes 98312 | tf_op jit(solution)/shard_map/ppermute | solution.py:668
  91.1 5.5 %collective-permute-start.4 = (f32[8,8,128]{2,1,0:T(8,128)S(1)}, f32[8,8,128]{2,1,0:T(8,128)S(1)}, u32[]{:S(2)}, u32[]{:S(2)}) collective-permute-start(f32[8,8,128]{2,1,0:T(8,128)S(1)} %get-tuple-element.55), channel_id=1, source_target_pairs={{0,192},{2,194},{4,196},{6,198},{8,200},{10,202},{12,204},{14,206}... | collective-permute-start | bytes 98312 | tf_op jit(solution)/shard_map/ppermute | solution.py:668
  93.5 4.4 %collective-permute-start.5 = (f32[8,8,128]{2,1,0:T(8,128)S(1)}, f32[8,8,128]{2,1,0:T(8,128)S(1)}, u32[]{:S(2)}, u32[]{:S(2)}) collective-permute-start(f32[8,8,128]{2,1,0:T(8,128)S(1)} %get-tuple-element.56), channel_id=1, source_target_pairs={{0,64},{2,66},{4,68},{6,70},{8,72},{10,74},{12,76},{14,78},{16,80}... | collective-permute-start | bytes 98312 | tf_op jit(solution)/shard_map/ppermute | solution.py:668
